TPU v7x, 32 devices: a whole 2x2x4 slice. The times are simulated.
32 devices in a mesh: dp: 4 (over y, x), row: 4 (over z), col: 2 (over core).
Axes of the slice: x: 2, y: 2, z: 4, core: 2. Of those that a mesh axis runs over, the one named last changes fastest.
Arguments:
- images: bfloat16 [32, 577, 1024], P(('dp', 'row'), None, 'col'), may hold values from -6 to 6
- cotangent: bfloat16 [32, 577, 1024], P(('dp', 'row'), None, 'col'), may hold values from -6 to 6
- micro_batch: int32 [32], P(('dp', 'row')), may hold values from 0 to 1, as said below
- heads_weight: bfloat16 [1024, 3, 1024], P('row', None, 'col'), may hold values from -0.1875 to 0.1875
- heads_bias: bfloat16 [2, 1024], P(None, 'col'), may hold values from -3 to 3
- merge_weight: bfloat16 [1024, 1024], P('col', 'row'), may hold values from -2 to 2
- merge_bias: bfloat16 [1024], P('col'), may hold values from -3 to 3
- expand_weight: bfloat16 [1024, 4096], P('row', 'col'), may hold values from -0.1875 to 0.1875
- expand_bias: bfloat16 [4096], P('col'), may hold values from -3 to 3
- shrink_weight: bfloat16 [4096, 1024], P('col', 'row'), may hold values from -0.09375 to 0.09375
- shrink_bias: bfloat16 [1024], P('col'), may hold values from -3 to 3
- norm_gains: bfloat16 [2, 1024], P(None, 'col'), may hold values from 0.5 to 1.5
- norm_shifts: bfloat16 [2, 1024], P(None, 'col'), may hold values from -2 to 2
Outputs:
- block_out: bfloat16 [32, 577, 1024], P(('dp', 'row'), None, 'col')
- input_grad: float32 [32, 577, 1024], P(('dp', 'row'), None, 'col')
- heads_weight_grad: float32 [1024, 3, 1024], P('row', None, 'col')
- heads_bias_grad: float32 [2, 1024], P(None, 'col')
- merge_weight_grad: float32 [1024, 1024], P('col', 'row')
- merge_bias_grad: float32 [1024], P('col')
- expand_weight_grad: float32 [1024, 4096], P('row', 'col')
- expand_bias_grad: float32 [4096], P('col')
- shrink_weight_grad: float32 [4096, 1024], P('col', 'row')
- shrink_bias_grad: float32 [1024], P('col')
- norm_gains_grad: float32 [2, 1024], P(None, 'col')
- norm_shifts_grad: float32 [2, 1024], P(None, 'col')
Inputs may be any that keep to these rules, and one draw needn't show every extreme that they name: `micro_batch`: every micro-batch number 0 to 1 belongs to at least one image.
All inputs are finite; a program needn't handle non-finite values.
Results may differ from a plain program's by a relative error of at most 0.018.
Values may be sent and summed in bfloat16 or wider, within the bound.
No kernel may reach another device: no remote copies, remote signals or barrier semaphores. Data moves between devices by JAX's collectives and lax.ppermute only.
A program may use at most 192 MiB of HBM per device.

v0:
```python
import functools

import jax
import jax.numpy as jnp
from jax import lax
from jax.experimental import pallas as pl
from jax.experimental.pallas import tpu as pltpu
from jax.sharding import PartitionSpec as P

HEAD_DIM = 64
MICRO = 2
BF16 = jnp.bfloat16
F32 = jnp.float32
VMEM_LIMIT = 58 << 20
STEP = 304
KEYS = 304


def peer(value, axis, p):
    n = lax.axis_size(axis)
    return lax.ppermute(value, axis, [(i, i ^ p) for i in range(n)])


def xor_order(value, dim, axis):
    n = lax.axis_size(axis)
    index = lax.axis_index(axis)
    size = value.shape[dim]
    bit = 1
    while bit < n:
        run = size * bit // n
        pieces = [lax.slice_in_dim(value, at, at + run, axis=dim) for at in range(0, size, run)]
        swapped = lax.concatenate([pieces[k ^ 1] for k in range(len(pieces))], dim)
        value = jnp.where((index & bit) != 0, swapped, value)
        bit *= 2
    return value


def cut(value, dim, n, k):
    run = value.shape[dim] // n
    return lax.slice_in_dim(value, k * run, (k + 1) * run, axis=dim)


def own_part(own, inner_dim):
    run = own.shape[inner_dim] // lax.axis_size("dp")
    return lax.dynamic_slice_in_dim(own, lax.axis_index("dp") * run, run, inner_dim)


def dp_parts(part):
    return [part] + [peer(part, "dp", p) for p in range(1, lax.axis_size("dp"))]


def sum_parts(parts, axis, start=None):
    n = lax.axis_size(axis)
    if start is not None:
        stacked = jnp.stack(parts)
        parts = [lax.dynamic_index_in_dim(stacked, start ^ p, 0, keepdims=False) for p in range(n)]
    total = parts[0].astype(F32)
    for p in range(1, n):
        total = total + peer(parts[p], axis, p).astype(F32)
    return total.astype(BF16)


def dp_sum(blocks):
    n = lax.axis_size("dp")
    blocks = blocks.reshape((n, blocks.shape[0] // n) + blocks.shape[1:])
    return add(lax.all_to_all(blocks, "dp", 0, 0))


def dp_all(part):
    n = lax.axis_size("dp")
    return lax.all_to_all(jnp.broadcast_to(part[None], (n,) + part.shape), "dp", 0, 0)


def scatter_row(value, model_dim):
    return lax.psum_scatter(value, "row", scatter_dimension=model_dim, tiled=True)


def sum_all(value):
    for axis in ("dp", "row"):
        terms = dp_parts(value) if axis == "dp" else [value] + [peer(value, "row", j) for j in range(1, lax.axis_size("row"))]
        while len(terms) > 1:
            terms = [terms[k] + terms[k + 1] for k in range(0, len(terms), 2)]
        value = terms[0]
    return value


def col_join(own, other):
    first = lax.axis_index("col") == 0
    return lax.concatenate([jnp.where(first, own, other), jnp.where(first, other, own)], own.ndim - 1)


def col_full(own, feature_dim):
    return lax.all_gather(own, "col", axis=feature_dim, tiled=True)


def col_own(full, feature_dim):
    n_col = lax.axis_size("col")
    if n_col == 2:
        return jnp.where(
            lax.axis_index("col") == 0, cut(full, feature_dim, 2, 0), cut(full, feature_dim, 2, 1)
        )
    width = full.shape[feature_dim] // n_col
    return lax.dynamic_slice_in_dim(full, lax.axis_index("col") * width, width, feature_dim)


def col_shares(part):
    if lax.axis_size("col") == 2:
        return part, peer(part, "col", 1)
    return lax.psum(part, "col"), jnp.zeros_like(part)


def nt(a, b):
    return lax.dot_general(a, b, (((1,), (1,)), ((), ())), preferred_element_type=F32)


def nn(a, b):
    return lax.dot_general(a, b, (((1,), (0,)), ((), ())), preferred_element_type=F32)


def cost(us, moved=1 << 20):
    return pl.CostEstimate(flops=int(us * 1.0e7), bytes_accessed=1024, transcendentals=0)


def scalar_call(body, at, grid, in_specs, out_specs, out_shape, name, us, scratch=(), limit=24, aliases=None):
    far = lambda a: pltpu.HBM(a.shape, a.dtype)
    out_shape = [far(a) for a in out_shape] if isinstance(out_shape, list) else far(out_shape)
    return pl.pallas_call(
        body,
        grid_spec=pltpu.PrefetchScalarGridSpec(
            num_scalar_prefetch=1,
            grid=grid,
            in_specs=in_specs,
            out_specs=out_specs,
            scratch_shapes=list(scratch),
        ),
        out_shape=out_shape,
        input_output_aliases=aliases or {},
        compiler_params=pltpu.CompilerParams(vmem_limit_bytes=limit << 20),
        cost_estimate=cost(us),
        name=name,
    )


def row_chunks(rows, body):
    for start in range(0, rows, STEP):
        body(pl.ds(start, min(STEP, rows - start)))


def spread_of(value):
    centered = value - jnp.mean(value, axis=1, keepdims=True)
    inverse = lax.rsqrt(jnp.mean(centered * centered, axis=1, keepdims=True) + 1e-05)
    return centered * inverse, inverse


def norm_kernel(x_ref, a_ref, b_ref, params_ref, middle_ref, normed_ref):
    def body(at):
        value = a_ref[at, :].astype(F32) + b_ref[at, :].astype(F32)
        value = x_ref[at, :].astype(F32) + (value + params_ref[0:1, :])
        middle_ref[at, :] = value
        xhat, _ = spread_of(value)
        normed_ref[at, :] = (xhat * params_ref[1:2, :] + params_ref[2:3, :]).astype(BF16)

    row_chunks(x_ref.shape[0], body)


def norm_of_sum(x, share_a, share_b, params):
    count, rows, model = x.shape
    image = pl.BlockSpec((None, rows, model), lambda i: (i, 0, 0))
    return pl.pallas_call(
        norm_kernel,
        grid=(count,),
        in_specs=[image] * 3 + [pl.BlockSpec(params.shape, lambda i: (0, 0))],
        out_specs=[image] * 2,
        out_shape=[pltpu.HBM(x.shape, F32), pltpu.HBM(x.shape, BF16)],
        compiler_params=pltpu.CompilerParams(vmem_limit_bytes=32 << 20),
        cost_estimate=cost(2),
        name="norm_two",
    )(x, share_a, share_b, params)


def norm_back_kernel(second, at_ref, base_ref, v_ref, a_ref, b_ref, gain_ref, weight_ref, *refs):
    grad_ref, *low_ref, sums_ref, scratch = refs
    rows = v_ref.shape[0]
    totals = None

    def body(at):
        nonlocal totals
        xhat, inverse = spread_of(v_ref[at, :].astype(F32))
        upstream = a_ref[at, :].astype(F32) + b_ref[at, :].astype(F32)
        scaled = upstream * gain_ref[...]
        first = jnp.mean(scaled, axis=1, keepdims=True)
        other = jnp.mean(scaled * xhat, axis=1, keepdims=True)
        base = base_ref[at, :].astype(F32)
        if second:
            base = base * weight_ref[pl.program_id(0)]
        grad = base + inverse * (scaled - first - xhat * other)
        parts = [jnp.sum(upstream * xhat, axis=0, keepdims=True), jnp.sum(upstream, axis=0, keepdims=True)]
        if second:
            grad_ref[at, :] = grad
            low = grad.astype(BF16)
            low_ref[0][at, :] = low
            parts.append(jnp.sum(low.astype(F32), axis=0, keepdims=True))
        else:
            scratch[at, :] = grad
        totals = parts if totals is None else [x + y for x, y in zip(totals, parts)]

    row_chunks(rows, body)
    for k, total in enumerate(totals):
        sums_ref[k : k + 1, :] = total
    if not second:
        length, width = grad_ref.shape
        grad_ref[...] = scratch[:length, pl.ds(pl.multiple_of(at_ref[2] * width, width), width)]


def norm_back(at, base, v, share_a, share_b, gain, weight, own):
    count, rows, model = v.shape
    second = own is None
    shape = jax.ShapeDtypeStruct
    image = pl.BlockSpec((None, rows, model), lambda i, at: (i, 0, 0))
    sums = 3 if second else 2
    outs = [image, image] if second else [pl.BlockSpec((None,) + own, lambda i, at: (i, 0, 0))]
    shapes = [shape(v.shape, F32), shape(v.shape, BF16)] if second else [shape((count,) + own, F32)]
    return scalar_call(
        functools.partial(norm_back_kernel, second),
        at,
        (count,),
        [image] * 4
        + [pl.BlockSpec((1, model), lambda i, at: (0, 0)), pl.BlockSpec(memory_space=pltpu.SMEM)],
        outs + [pl.BlockSpec((None, sums, model), lambda i, at: (i, 0, 0))],
        shapes + [shape((count, sums, model), F32)],
        "norm_back",
        2,
        scratch=[pltpu.VMEM((8, 128) if second else (rows, model), F32)],
        limit=48,
    )(at, base, v, share_a, share_b, gain[None], weight)


def join_kernel(normal, at_ref, own_ref, other_ref, *refs):
    out_ref = refs[2] if normal else refs[0]
    rows, width = own_ref.shape
    to = pl.ds(pl.multiple_of(at_ref[2] * width, width), width)
    away = pl.ds(pl.multiple_of((1 - at_ref[2]) * width, width), width)
    out_ref[:, to] = own_ref[...]
    out_ref[:, away] = other_ref[...]
    if not normal:
        return
    gain_ref, shift_ref, _, normed_ref = refs

    def body(at):
        value = out_ref[at, :].astype(F32)
        centered = value - jnp.mean(value, axis=1, keepdims=True)
        inverse = lax.rsqrt(jnp.mean(centered * centered, axis=1, keepdims=True) + 1e-05)
        normed_ref[at, :] = (centered * inverse * gain_ref[...] + shift_ref[...]).astype(BF16)

    row_chunks(rows, body)


def join(at, own, other, vectors=None):
    count, rows, width = own.shape
    normal = vectors is not None
    shape = jax.ShapeDtypeStruct((count, rows, 2 * width), BF16)
    half = pl.BlockSpec((None, rows, width), lambda i, at: (i, 0, 0))
    full = pl.BlockSpec((None, rows, 2 * width), lambda i, at: (i, 0, 0))
    vector = pl.BlockSpec((1, 2 * width), lambda i, at: (0, 0))
    return scalar_call(
        functools.partial(join_kernel, normal),
        at,
        (count,),
        [half, half] + [vector] * (2 if normal else 0),
        [full, full] if normal else full,
        [shape, shape] if normal else shape,
        "join",
        2,
    )(at, own, other, *(vectors or ()))


def seed_kernel(at_ref, own_ref, other_ref, weight_ref, cot_ref, seed_ref, sums_ref, sums):
    rows, width = own_ref.shape
    scale = weight_ref[pl.program_id(0)]
    sums[...] = jnp.zeros_like(sums)
    for k, ref in enumerate((own_ref, other_ref)):
        place = at_ref[2] if k == 0 else 1 - at_ref[2]
        to = pl.ds(pl.multiple_of(place * width, width), width)

        def body(at):
            value = ref[at, :]
            low = (value.astype(F32) * scale).astype(BF16)
            cot_ref[at, to] = value
            seed_ref[at, to] = low
            low = low.astype(F32)
            sums[:, to] += jnp.sum(low.reshape(low.shape[0] // 8, 8, width), axis=0)

        row_chunks(rows, body)
    sums_ref[...] = jnp.sum(sums[...], axis=0, keepdims=True)


def seed_of(at, own, other, weight):
    count, rows, width = own.shape
    shape = jax.ShapeDtypeStruct
    half = pl.BlockSpec((None, rows, width), lambda i, at: (i, 0, 0))
    full = pl.BlockSpec((None, rows, 2 * width), lambda i, at: (i, 0, 0))
    return scalar_call(
        seed_kernel,
        at,
        (count,),
        [half, half, pl.BlockSpec(memory_space=pltpu.SMEM)],
        [full, full, pl.BlockSpec((None, 1, 2 * width), lambda i, at: (i, 0, 0))],
        [shape((count, rows, 2 * width), BF16)] * 2 + [shape((count, 1, 2 * width), F32)],
        "seed",
        2,
        scratch=[pltpu.VMEM((8, 2 * width), F32)],
    )(at, own, other, weight)


def stay(value):
    return pltpu.with_memory_space_constraint(value, pltpu.HBM)


def stack_kernel(body_rows, own_ref, *refs):
    out_ref = refs[-1]
    total = own_ref[...].astype(F32)
    for k, ref in enumerate(refs[:-1]):
        out_ref[k * body_rows : (k + 1) * body_rows, :] = ref[:body_rows, :]
        total = total + ref[body_rows:, :].astype(F32)
    out_ref[(len(refs) - 1) * body_rows :, :] = total.astype(BF16)


def stack(own_tail, arrays):
    vmem = pl.BlockSpec(memory_space=pltpu.VMEM)
    more, lanes = own_tail.shape
    body = arrays[0].shape[0] - more
    return pl.pallas_call(
        functools.partial(stack_kernel, body),
        in_specs=[vmem] * (1 + len(arrays)),
        out_specs=vmem,
        out_shape=jax.ShapeDtypeStruct((len(arrays) * body + more, lanes), BF16),
        compiler_params=pltpu.CompilerParams(vmem_limit_bytes=16 << 20),
        cost_estimate=cost(1),
        name="stack",
    )(own_tail, *arrays)


def unpack_kernel(n_row, at_ref, in_ref, merge_ref, expand_ref):
    z = pl.program_id(0)
    rows, run = merge_ref.shape
    near = expand_ref.shape[0]
    merge_ref[...] = in_ref[:rows, :]
    for k in range(expand_ref.shape[1] // run):
        expand_ref[:, k * run : (k + 1) * run] = in_ref[rows + k * near : rows + (k + 1) * near, :]


def unpack(at, gathered, rows, near):
    n_row, total, run = gathered.shape
    wide = (total - rows) // near * run
    shape = jax.ShapeDtypeStruct
    return scalar_call(
        functools.partial(unpack_kernel, n_row),
        at,
        (n_row,),
        [pl.BlockSpec((None, total, run), lambda j, at: (at[1] ^ j, 0, 0))],
        [
            pl.BlockSpec((rows, run), lambda j, at: (0, at[1] ^ j)),
            pl.BlockSpec((None, near, wide), lambda j, at: (jnp.maximum(j - 1, 0), 0, 0)),
        ],
        [shape((rows, n_row * run), BF16), shape((n_row - 1, near, wide), BF16)],
        "unpack",
        1,
    )(at, stay(gathered))


def pick_kernel(at_ref, in_ref, out_ref):
    for q in range(out_ref.shape[0]):
        out_ref[q] = in_ref[...]


def others(at, gathered):
    n_dp, n_row = lax.axis_size("dp"), gathered.shape[0]
    block = (None,) + gathered.shape[1:]
    return scalar_call(
        pick_kernel,
        at,
        (n_row - 1,),
        [pl.BlockSpec(block, lambda j, at: (at[1] ^ (j + 1), 0, 0))],
        pl.BlockSpec((n_dp,) + block, lambda j, at: (0, j, 0, 0)),
        jax.ShapeDtypeStruct((n_dp, n_row - 1) + gathered.shape[1:], gathered.dtype),
        "others",
        1,
    )(at, stay(gathered))


def place_kernel(at_ref, own_ref, rest_ref, out_ref, sems):
    n_dp, others, run, near = rest_ref.shape
    copies = [
        pltpu.make_async_copy(
            own_ref,
            out_ref.at[:, pl.ds(pl.multiple_of(at_ref[1] * near, near), near)],
            sems.at[0],
        )
    ]
    for q in range(n_dp):
        for j in range(others):
            to = pl.ds(pl.multiple_of((at_ref[1] ^ (j + 1)) * near, near), near)
            copies.append(
                pltpu.make_async_copy(
                    rest_ref.at[q, j], out_ref.at[q * run : (q + 1) * run, to], sems.at[len(copies)]
                )
            )
    for copy in copies:
        copy.start()
    for copy in copies:
        copy.wait()


def place(at, own, rest):
    n_dp, others, run, near = rest.shape
    return pl.pallas_call(
        place_kernel,
        in_specs=[pl.BlockSpec(memory_space=pltpu.SMEM)] + [pl.BlockSpec(memory_space=pl.ANY)] * 2,
        out_specs=pl.BlockSpec(memory_space=pltpu.VMEM),
        out_shape=jax.ShapeDtypeStruct((n_dp * run, (others + 1) * near), own.dtype),
        scratch_shapes=[pltpu.SemaphoreType.DMA((1 + n_dp * others,))],
        compiler_params=pltpu.CompilerParams(vmem_limit_bytes=8 << 20),
        cost_estimate=cost(1),
        name="place",
    )(at, stay(own), stay(rest))


def add_kernel(in_ref, out_ref):
    out_ref[...] = jnp.sum(in_ref[...].astype(F32), axis=0).astype(BF16)


def add(blocks):
    n, rows, lanes = blocks.shape
    step = rows // 4 if rows % 64 == 0 else rows
    return pl.pallas_call(
        add_kernel,
        grid=(rows // step,),
        in_specs=[pl.BlockSpec((n, step, lanes), lambda i: (0, i, 0))],
        out_specs=pl.BlockSpec((step, lanes), lambda i: (i, 0)),
        out_shape=jax.ShapeDtypeStruct((rows, lanes), BF16),
        compiler_params=pltpu.CompilerParams(vmem_limit_bytes=24 << 20),
        cost_estimate=cost(1),
        name="add",
    )(blocks)


def half_kernel(at_ref, in_ref, out_ref):
    out_ref[...] = in_ref[...]


def half(at, value, own):
    count, rows, model = value.shape
    place = (lambda at: at[2]) if own else (lambda at: 1 - at[2])
    return scalar_call(
        half_kernel,
        at,
        (count,),
        [pl.BlockSpec((None, rows, model // 2), lambda i, at: (i, 0, place(at)))],
        pl.BlockSpec((None, rows, model // 2), lambda i, at: (i, 0, 0)),
        jax.ShapeDtypeStruct((count, rows, model // 2), value.dtype),
        "half",
        1,
    )(at, value)


def close_kernel(at_ref, m_ref, a_ref, b_ref, bias_ref, out_ref):
    def body(at):
        share = a_ref[at, :].astype(F32) + b_ref[at, :].astype(F32)
        out_ref[at, :] = (m_ref[at, :] + (share + bias_ref[...])).astype(BF16)

    row_chunks(out_ref.shape[0], body)


def close(at, middle, part, other, bias, length):
    count, rows, width = other.shape
    mine = pl.BlockSpec((None, rows, width), lambda i, at: (i, 0, at[2]))
    plain = pl.BlockSpec((None, rows, width), lambda i, at: (i, 0, 0))
    return scalar_call(
        close_kernel,
        at,
        (count,),
        [mine, mine, plain, pl.BlockSpec((1, width), lambda i, at: (0, 0))],
        pl.BlockSpec((None, length, width), lambda i, at: (i, 0, 0)),
        jax.ShapeDtypeStruct((count, length, width), BF16),
        "close",
        1,
    )(at, middle, part, other, bias)


def spread_kernel(n_dp, at_ref, *refs):
    out_ref = refs[-1]
    run = out_ref.shape[2] // n_dp
    for p in range(n_dp):
        to = pl.ds(pl.multiple_of((at_ref[0] ^ p) * run, run), run)
        for k in range(3):
            out_ref[k, :, to] = refs[p][:, k * run : (k + 1) * run].astype(F32)


def spread(at, parts):
    n_dp = len(parts)
    rows, three = parts[0].shape
    run = three // 3
    vmem = pl.BlockSpec((rows, three), lambda i, at: (0, 0))
    return scalar_call(
        functools.partial(spread_kernel, n_dp),
        at,
        (1,),
        [vmem] * n_dp,
        pl.BlockSpec((3, rows, n_dp * run), lambda i, at: (0, 0, 0)),
        jax.ShapeDtypeStruct((3, rows, n_dp * run), F32),
        "spread",
        1,
    )(at, *parts)


def head_mask(rows, width, h):
    lane = lax.broadcasted_iota(jnp.int32, (rows, width), 1)
    return (lane >= h * HEAD_DIM) & (lane < (h + 1) * HEAD_DIM)


def mix_kernel(length, n_row, at_ref, n_ref, own_ref, rest_ref, bias_ref, *refs):
    mixed_ref, o_ref, weight_ref, exact_ref, stats_ref, lanes_ref = refs[-6:]
    rows = n_ref.shape[0]
    width = o_ref.shape[1]
    count = width // HEAD_DIM
    near = own_ref.shape[1]
    chunk = rows

    @pl.when(pl.program_id(0) == 0)
    def _():
        for j in range(n_row):
            to = pl.ds(pl.multiple_of((at_ref[1] ^ j) * near, near), near)
            for k in range(3):
                start = ((j - 1) * 3 + k) * near
                piece = own_ref[k] if j == 0 else rest_ref[start : start + near, :]
                weight_ref[to, k * width : (k + 1) * width] = piece

    for start in range(0, rows, chunk):
        size = min(chunk, rows - start)
        at = pl.ds(start, size)
        mixed = nn(n_ref[at, :], weight_ref[...]) + bias_ref[...]
        mixed_ref[at, :width] = (mixed[:, :width] * HEAD_DIM**-0.5).astype(BF16)
        mixed_ref[at, width:] = mixed[:, width:].astype(BF16)
    plain = length // 128 * 128
    k = mixed_ref[:, width : 2 * width]
    v = mixed_ref[:, 2 * width :]
    for start in range(0, rows, chunk):
        size = min(chunk, rows - start)
        at = pl.ds(start, size)
        q = mixed_ref[at, :width]
        result, stats = None, jnp.zeros((size, 128), F32)
        place = lax.broadcasted_iota(jnp.int32, (size, 128), 1)
        for h in range(count):
            mask = head_mask(size, width, h)
            query = jnp.where(mask, q, jnp.zeros_like(q))
            near, far = nt(query, k[:plain]), nt(query, k[plain:])
            key = lax.broadcasted_iota(jnp.int32, far.shape, 1) + plain
            far = jnp.where(key < length, far, -1e30)
            top = jnp.maximum(jnp.max(near, axis=1, keepdims=True), jnp.max(far, axis=1, keepdims=True))
            near, far = jnp.exp(near - top), jnp.exp(far - top)
            total = jnp.sum(near, axis=1, keepdims=True) + jnp.sum(far, axis=1, keepdims=True)
            out = (nn(near.astype(BF16), v[:plain]) + nn(far.astype(BF16), v[plain:])) / total
            result = out if result is None else jnp.where(mask, out, result)
            stats = jnp.where(place == h, top + jnp.log(total), stats)
        o_ref[at, :] = result.astype(BF16)
        exact_ref[at, :] = result
        lanes_ref[at, :] = stats
    row = lax.broadcasted_iota(jnp.int32, (8, 128), 0)
    lane = lax.broadcasted_iota(jnp.int32, (8, 128), 1)
    stats_ref[...] = turned(jnp.where(row == lane, 1.0, 0.0), lanes_ref[...])


def turned(select, value):
    return lax.dot_general(
        select, value, (((1,), (1,)), ((), ())), precision=lax.Precision.HIGHEST, preferred_element_type=F32
    )


def mix_back_kernel(length, at_ref, m_ref, up_ref, exact_ref, stats_ref, *refs):
    d_ref, sums_ref, probs, grads, q_all, up_all = refs[-6:]
    rows, width = up_ref.shape
    count = width // HEAD_DIM
    lanes = probs.shape[1] // count
    chunk = 256
    row = lax.broadcasted_iota(jnp.int32, (8, width), 0)
    lane = lax.broadcasted_iota(jnp.int32, (8, width), 1)
    select = jnp.where((lane >= row * HEAD_DIM) & (lane < (row + 1) * HEAD_DIM), 1.0, 0.0)
    delta = turned(select, up_ref[...].astype(F32) * exact_ref[...])
    for h in range(count):
        base = h * lanes
        if rows < lanes:
            probs[:, pl.ds(base + rows, lanes - rows)] = jnp.zeros((rows, lanes - rows), BF16)
            grads[:, pl.ds(base + rows, lanes - rows)] = jnp.zeros((rows, lanes - rows), BF16)
            q_all[pl.ds(base + rows, lanes - rows), :] = jnp.zeros((lanes - rows, width), BF16)
            up_all[pl.ds(base + rows, lanes - rows), :] = jnp.zeros((lanes - rows, width), BF16)
        for start in range(0, rows, chunk):
            size = min(chunk, rows - start)
            mask = head_mask(size, width, h)
            q = m_ref[pl.ds(start, size), :width]
            up = up_ref[pl.ds(start, size), :]
            q = jnp.where(mask, q, jnp.zeros_like(q))
            up = jnp.where(mask, up, jnp.zeros_like(up))
            q_all[pl.ds(base + start, size), :] = q
            up_all[pl.ds(base + start, size), :] = up
            total = stats_ref[h : h + 1, start : start + size]
            mean = delta[h : h + 1, start : start + size]
            for first in range(0, rows, KEYS):
                keys = pl.ds(first, min(KEYS, rows - first))
                share = jnp.exp(nt(m_ref[keys, width : 2 * width], q) - total)
                if first + KEYS > length:
                    key = lax.broadcasted_iota(jnp.int32, share.shape, 0) + first
                    share = jnp.where(key < length, share, 0.0)
                prob_grad = nt(m_ref[keys, 2 * width :], up)
                probs[keys, pl.ds(base + start, size)] = share.astype(BF16)
                grads[keys, pl.ds(base + start, size)] = (share * (prob_grad - mean)).astype(BF16)
    dv = nn(probs[...], up_all[...]).astype(BF16)
    dk = nn(grads[...], q_all[...]).astype(BF16)
    flipped = m_ref[:, width : 2 * width].astype(F32).T.astype(BF16)
    pieces = []
    for h in range(count):
        pieces.append(nn(flipped[h * HEAD_DIM : (h + 1) * HEAD_DIM, :], grads[:, pl.ds(h * lanes, rows)]))
    dq = jnp.concatenate(pieces, axis=0).T if count > 1 else pieces[0].T
    dq = (dq.astype(BF16).astype(F32) * HEAD_DIM**-0.5).astype(BF16)
    for at, value in enumerate((dq, dk, dv)):
        d_ref[:, at * width : (at + 1) * width] = value
        sums_ref[:, at * width : (at + 1) * width] = jnp.sum(value.astype(F32), axis=0, keepdims=True)


def mix(length, g, at, normed, own, rest, bias, attended, weight, width):
    count, rows, model = normed.shape
    n_row = model // own.shape[1]
    wide = rest.shape[1]
    shape = jax.ShapeDtypeStruct
    more = [] if attended is None else [attended, weight]
    place = (lambda at: at[0] ^ g) if own.shape[2] > wide else (lambda at: 0)
    return scalar_call(
        functools.partial(mix_kernel, length, n_row),
        at,
        (count,),
        [
            pl.BlockSpec((None, rows, model), lambda i, at: (i, 0, 0)),
            pl.BlockSpec((3, own.shape[1], wide), lambda i, at: (0, 0, place(at))),
            pl.BlockSpec(rest.shape, lambda i, at: (0, 0)),
            pl.BlockSpec((None, 1, 3 * wide), lambda i, at: (place(at), 0, 0)),
        ]
        + [pl.BlockSpec(memory_space=pl.ANY)] * len(more),
        [
            pl.BlockSpec((None, rows, 3 * wide), lambda i, at: (i, 0, 0)),
            pl.BlockSpec((None, rows, wide), lambda i, at: (i, 0, place(at))),
            pl.BlockSpec((model, 3 * wide), lambda i, at: (0, g)),
            pl.BlockSpec((None, rows, wide), lambda i, at: (i, 0, 0)),
            pl.BlockSpec((None, 8, rows), lambda i, at: (i, 0, 0)),
        ],
        [
            shape((count, rows, 3 * wide), BF16),
            shape((count, rows, width), BF16),
            shape((model, 3 * width), BF16),
            shape((count, rows, wide), F32),
            shape((count, 8, rows), F32),
        ],
        "mix",
        2,
        scratch=[pltpu.VMEM((rows, 128), F32)],
        aliases={5: 1, 6: 2} if more else {},
    )(at, normed, own, rest, bias, *more)


def mix_back(length, g, groups, at, mixed, up, exact, stats, grads):
    count, rows, three = mixed.shape
    wide = three // 3
    lanes = -(-rows // 128) * 128 * (wide // HEAD_DIM)
    shape = jax.ShapeDtypeStruct
    place = (lambda at: at[0] ^ g) if groups > 1 else (lambda at: 0)
    more = [] if grads is None else [grads]
    return scalar_call(
        functools.partial(mix_back_kernel, length),
        at,
        (count,),
        [
            pl.BlockSpec((None, rows, three), lambda i, at: (i, 0, 0)),
            pl.BlockSpec((None, rows, wide), lambda i, at: (i, 0, place(at))),
            pl.BlockSpec((None, rows, wide), lambda i, at: (i, 0, 0)),
            pl.BlockSpec((None, 8, rows), lambda i, at: (i, 0, 0)),
        ]
        + [pl.BlockSpec(memory_space=pl.ANY)] * len(more),
        [
            pl.BlockSpec((None, rows, three), lambda i, at: (i, 0, g)),
            pl.BlockSpec((None, 1, three), lambda i, at: (i, 0, 0)),
        ],
        [shape((count, rows, groups * three), BF16), shape((count, 1, three), F32)],
        "mix_back",
        2,
        scratch=[
            pltpu.VMEM((rows, lanes), BF16),
            pltpu.VMEM((rows, lanes), BF16),
            pltpu.VMEM((lanes, wide), BF16),
            pltpu.VMEM((lanes, wide), BF16),
        ],
        aliases={5: 0} if more else {},
    )(at, stay(mixed), stay(up), stay(exact), stats, *more)


def up_kernel(n_row, at_ref, n_ref, own_ref, rest_ref, bias_ref, *refs):
    act_ref, slope_ref, weight_ref = refs[-3:]
    rows = n_ref.shape[0]
    near = own_ref.shape[0]

    @pl.when(pl.program_id(0) == 0)
    def _():
        for j in range(n_row):
            to = pl.ds(pl.multiple_of((at_ref[1] ^ j) * near, near), near)
            weight_ref[to, :] = own_ref[...] if j == 0 else rest_ref[j - 1]

    for start in range(0, rows, 256):
        at = pl.ds(start, min(256, rows - start))
        hidden = nn(n_ref[at, :], weight_ref[...]) + bias_ref[...]
        gate = 0.5 + 0.5 * jnp.tanh(0.851 * hidden)
        act = hidden * gate
        act_ref[at, :] = act.astype(BF16)
        slope_ref[at, :] = (gate + 1.702 * act * (1.0 - gate)).astype(BF16)


def up(p, at, normed, own, rest, bias, before):
    run = rest.shape[2]
    units = own.shape[1]
    count, rows, model = normed.shape
    shape = jax.ShapeDtypeStruct
    place = (lambda at: at[0] ^ p) if units > run else (lambda at: 0)
    block = pl.BlockSpec((None, rows, run), lambda i, at: (i, 0, place(at)))
    return scalar_call(
        functools.partial(up_kernel, model // own.shape[0]),
        at,
        (count,),
        [
            pl.BlockSpec((None, rows, model), lambda i, at: (i, 0, 0)),
            pl.BlockSpec((own.shape[0], run), lambda i, at: (0, place(at))),
            pl.BlockSpec(rest.shape, lambda i, at: (0, 0, 0)),
            pl.BlockSpec((1, run), lambda i, at: (0, place(at))),
        ]
        + [pl.BlockSpec(memory_space=pl.ANY)] * len(before),
        [block, block, pl.BlockSpec((model, run), lambda i, at: (0, place(at)))],
        [shape((count, rows, units), BF16)] * 2 + [shape((model, units), BF16)],
        "expand",
        1,
        limit=32,
        aliases={5: 0, 6: 1, 7: 2} if before else {},
    )(at, normed, own, rest, bias, *before)


def statistics(value):
    centered = value - jnp.mean(value, axis=-1, keepdims=True)
    inverse = lax.rsqrt(jnp.mean(centered * centered, axis=-1, keepdims=True) + 1e-05)
    return centered * inverse, inverse


def shards(
    images,
    cotangent,
    micro_batch,
    heads_weight,
    heads_bias,
    merge_weight,
    merge_bias,
    expand_weight,
    expand_bias,
    shrink_weight,
    shrink_bias,
    norm_gains,
    norm_shifts,
):
    n_dp, n_row = lax.axis_size("dp"), lax.axis_size("row")
    count, length, width = images.shape
    model = width * lax.axis_size("col")
    rows = -(-length // 16) * 16
    pad = ((0, 0), (0, rows - length), (0, 0))
    units = expand_weight.shape[1]
    run = width // n_dp
    split = run % HEAD_DIM == 0
    groups = n_dp if split else 1
    wide = width // groups
    at = jnp.stack([lax.axis_index(axis) for axis in ("dp", "row", "col")]).astype(jnp.int32)

    heads_own = jnp.transpose(heads_weight, (1, 0, 2))
    heads_send = own_part(heads_own, 2).reshape(-1, run)
    all_slots = count * n_dp * n_row
    assert all_slots <= 256 and run >= MICRO
    member = (micro_batch[:, None] == jnp.arange(run, dtype=jnp.int32)[None, :]).astype(F32)
    tail_own = jnp.broadcast_to(jnp.sum(member, axis=0), (16, run)).astype(BF16)
    heads_send = jnp.concatenate([heads_send, tail_own])
    heads_send, images, cotangent, norm_gains = lax.optimization_barrier(
        (heads_send, images, cotangent, norm_gains)
    )
    heads_rows = [peer(heads_send, "row", j) for j in range(1, n_row)]

    params = jnp.concatenate([norm_gains, norm_shifts, merge_bias[None], shrink_bias[None]], axis=0)
    params_tail = jnp.pad(params, ((0, rows - length - params.shape[0]), (0, 0)))
    x_own = jnp.concatenate([images, jnp.broadcast_to(params_tail, (count,) + params_tail.shape)], axis=1)
    cot_own = jnp.pad(cotangent, pad)
    pair = lax.axis_size("col") == 2
    if pair:
        x_other = peer(x_own, "col", 1)
        params = col_join(params, x_other[0, length : length + 6])
    else:
        x = col_full(x_own, 2)
        params = x[0, length : length + 6]
    gain_one, gain_two, shift_one, shift_two, merge_bias_full, _ = (
        params[k].astype(F32) for k in range(6)
    )
    if pair:
        x, normed = join(at, x_own, x_other, (gain_one[None], shift_one[None]))
    else:
        xhat, _ = statistics(x.astype(F32))
        normed = (xhat * gain_one + shift_one).astype(BF16)
    bias3 = jnp.stack([heads_bias[0], jnp.zeros_like(heads_bias[0]), heads_bias[1]]).astype(F32)
    bias3 = bias3.reshape(3, groups, wide).transpose(1, 0, 2).reshape(groups, 1, 3 * wide)

    heads_rows, normed, x, cot_own, expand_send, shrink_send = (
        lax.optimization_barrier(
            (
                heads_rows,
                normed,
                x,
                cot_own,
                own_part(expand_weight, 1),
                own_part(shrink_weight, 0),
            )
        )
    )
    heads_parts = dp_parts(stack(tail_own, heads_rows))
    lanes = merge_weight.shape[1]
    joined = expand_send.shape[1] % lanes == 0
    if joined:
        pieces = [expand_send[:, k : k + lanes] for k in range(0, expand_send.shape[1], lanes)]
        gathered = lax.all_gather(jnp.concatenate([merge_weight, *pieces]), "row")
    else:
        merge_full = lax.all_gather(merge_weight, "row", axis=1, tiled=True)
        expand_rows = lax.all_gather(expand_send, "row")
    shrink_rows = lax.all_gather(shrink_send, "row")
    totals = [piece[-1:, :MICRO].astype(F32) for piece in heads_parts]
    while len(totals) > 1:
        totals = [totals[k] + totals[k + 1] for k in range(0, len(totals), 2)]
    batch_weight = all_slots / (MICRO * totals[0])
    slot_weight = jnp.sum(member[:, :MICRO] * batch_weight, axis=1)
    if not split:
        heads_parts = [xor_order(lax.concatenate(heads_parts, 1), 1, "dp")]

    cot_other = peer(cot_own, "col", 1) if pair else None

    mixed, exact, stats = [None] * groups, [None] * groups, [None] * groups
    attended = heads_full = None
    for g in range(groups):
        mixed[g], attended, heads_full, exact[g], stats[g] = mix(
            length, g, at, normed, heads_own, heads_parts[g], bias3, attended, heads_full, width
        )

    if joined:
        attended, gathered = lax.optimization_barrier((attended, gathered))
        merge_full, expand_rows = unpack(at, gathered, width, expand_weight.shape[0])
        expand_rest = dp_parts(expand_rows)
    else:
        expand_rest = dp_parts(others(at, expand_rows)[0])
    shrink_rows = others(at, shrink_rows)
    attended, expand_rest[1:3], shrink_rows = lax.optimization_barrier(
        (attended, expand_rest[1:3], shrink_rows)
    )
    shrink_all = lax.all_to_all(shrink_rows, "dp", 0, 0)
    merge_part = jnp.einsum("itf,fd->itd", attended, merge_full, preferred_element_type=F32)
    share_a, share_b = col_shares(merge_part.astype(BF16))
    middle, normed_two = norm_of_sum(
        x, share_a, share_b, jnp.stack([merge_bias_full, gain_two, shift_two])
    )

    if (units // n_dp) % 128:
        expand_rest = [xor_order(lax.concatenate(expand_rest, 2), 2, "dp")]
    made = ()
    for p, piece in enumerate(expand_rest):
        made = up(p, at, normed_two, expand_weight, piece, expand_bias.astype(F32)[None], made)
    activated, slope, expand_full = made

    if pair:
        cot, seed_low, seed_sums = seed_of(at, cot_own, cot_other, slot_weight)
    else:
        cot = col_full(cot_own, 2)
        seed_low = (cot.astype(F32) * slot_weight[:, None, None]).astype(BF16)
        seed_sums = jnp.sum(seed_low.astype(F32), axis=1, keepdims=True)

    shrink_grad = jnp.einsum("ith,itd->hd", activated, seed_low, preferred_element_type=F32)
    shrink_grad = shrink_grad.astype(BF16)
    shrink_sum = scatter_row(shrink_grad, 1)
    shrink_grad, seed_low, shrink_all = lax.optimization_barrier((shrink_grad, seed_low, shrink_all))
    shrink_full = place(at, shrink_weight, shrink_all)
    act_grad = jnp.einsum("itd,hd->ith", seed_low, shrink_full, preferred_element_type=F32)
    hidden_grad = (act_grad * slope.astype(F32)).astype(BF16)
    hidden_sums = jnp.sum(hidden_grad.astype(F32), axis=(0, 1))
    expand_grad = jnp.einsum("ith,itd->hd", hidden_grad, normed_two, preferred_element_type=F32)
    expand_grad, hidden_grad, hidden_sums = lax.optimization_barrier(
        (expand_grad.astype(BF16), hidden_grad, hidden_sums)
    )
    expand_sum = dp_sum(expand_grad)
    norm_part = jnp.einsum("ith,dh->itd", hidden_grad, expand_full, preferred_element_type=F32)
    norm_part = norm_part.astype(BF16)
    share_a, share_b = col_shares(norm_part)
    middle_grad, branch_grad, sums_two = norm_back(
        at, cot, middle, share_a, share_b, gain_two, slot_weight, None
    )

    attended_grad = jnp.einsum(
        "itd,fd->itf", branch_grad, merge_full, preferred_element_type=F32
    ).astype(BF16)
    merge_grad = jnp.einsum("itf,itd->fd", attended, branch_grad, preferred_element_type=F32)
    merge_grad, attended_grad = lax.optimization_barrier((merge_grad.astype(BF16), attended_grad))
    mixed_grad, mixed_sums, heads_grads = None, [None] * groups, [None] * groups
    merge_sum, heads_in = scatter_row(merge_grad, 1), [None] * groups
    part = units // n_dp
    order = list(range(1, groups)) + [0]
    for turn, g in enumerate(order):
        if turn == max(groups - 2, 0):
            attended_grad, expand_sum, shrink_sum = lax.optimization_barrier(
                (attended_grad, expand_sum, shrink_sum)
            )
            expand_sum = scatter_row(expand_sum, 1)
        if g == 0:
            attended_grad, merge_sum, heads_in[1:2] = lax.optimization_barrier(
                (attended_grad, merge_sum, heads_in[1:2])
            )
            both = jnp.concatenate(
                [shrink_sum.reshape(n_dp, part, -1), merge_sum.reshape(n_dp, run, -1)], axis=1
            )
            both = dp_sum(both.reshape(units + width, -1))
        mixed_grad, mixed_sums[g] = mix_back(
            length, g, groups, at, mixed[g], attended_grad, exact[g], stats[g], mixed_grad
        )
        piece = mixed_grad[:, :, g * 3 * wide : (g + 1) * 3 * wide]
        heads_grads[g] = jnp.einsum("itd,itf->df", normed, piece, preferred_element_type=F32).astype(BF16)
        if g:
            attended_grad, heads_grads[g] = lax.optimization_barrier((attended_grad, heads_grads[g]))
            heads_in[g] = peer(heads_grads[g], "dp", g)
    if not split:
        whole = xor_order(heads_grads[0].reshape(model, 3, width), 2, "dp")
        heads_grads = [cut(whole, 2, n_dp, p).reshape(model, 3 * run) for p in range(n_dp)]
        heads_in = [None] + [peer(heads_grads[p], "dp", p) for p in range(1, n_dp)]
    heads_sum = heads_grads[0].astype(F32)
    for piece in heads_in[1:]:
        heads_sum = heads_sum + piece.astype(F32)
    heads_sum = heads_sum.astype(BF16)
    heads_sum = sum_parts([cut(heads_sum, 0, n_row, j) for j in range(n_row)], "row", at[1])
    mixed_grad, activated, both, expand_sum = lax.optimization_barrier(
        (mixed_grad, activated, both, expand_sum)
    )
    first_part = jnp.einsum("itf,df->itd", mixed_grad, heads_full, preferred_element_type=F32)
    share_a, share_b = col_shares(first_part.astype(BF16))
    packed = dp_all(jnp.concatenate([both, expand_sum]))
    shrink_part = jnp.einsum("ith,hd->itd", activated, shrink_full, preferred_element_type=F32).astype(BF16)
    shrink_part, heads_sum = lax.optimization_barrier((shrink_part, heads_sum))
    own = (length, width) if pair else (rows, model)
    place_of = at if pair else at * jnp.array([1, 1, 0], jnp.int32)
    input_grad, sums_one = norm_back(
        place_of, middle_grad, x, share_a, share_b, gain_one, slot_weight, own
    )

    if pair:
        other = peer(half(at, shrink_part, False), "col", 1)
        output = close(at, middle, shrink_part, other, shrink_bias.astype(F32)[None], length)
    else:
        branch_two = col_own(lax.psum(shrink_part, "col").astype(F32), 2)
        output = (col_own(middle, 2) + (branch_two + shrink_bias.astype(F32))).astype(BF16)[:, :length]
        input_grad = col_own(input_grad, 2)[:, :length]
    packed, sums_one = lax.optimization_barrier((packed, sums_one))
    heads_out = dp_parts(heads_sum)
    heads_out, packed, sums_one = lax.optimization_barrier((heads_out, packed, sums_one))

    sums_one, sums_two = jnp.sum(sums_one, axis=0), jnp.sum(sums_two, axis=0)
    model_sums = jnp.stack(
        [sums_one[0], sums_two[0], sums_one[1], sums_two[1], sums_two[2], jnp.sum(seed_sums, axis=(0, 1))]
    )
    model_sums = col_own(model_sums, 1)
    mixed_sums = jnp.sum(jnp.concatenate(mixed_sums, axis=1), axis=0)
    mixed_sums = mixed_sums.reshape(groups, 3, wide).transpose(1, 0, 2).reshape(3, width)
    heads_bias_grad = mixed_sums[0::2]
    if split:
        heads_bias_grad = xor_order(heads_bias_grad, 1, "dp")
    small = sum_all(jnp.concatenate([model_sums.ravel(), heads_bias_grad.ravel(), hidden_sums]))
    shrink_sum = packed[:, :part].reshape(units, -1).astype(F32)
    merge_sum = packed[:, part : part + run].reshape(width, -1).astype(F32)
    expand_sum = packed[:, part + run :].reshape(units, -1).T.astype(F32)
    if run % 128:
        heads_sum = [piece.reshape(-1, 3, run) for piece in heads_out]
        heads_sum = xor_order(jnp.concatenate(heads_sum, axis=2), 2, "dp").astype(F32)
    else:
        heads_sum = jnp.transpose(spread(at, heads_out), (1, 0, 2))

    model_sums = small[: 6 * width].reshape(6, width)
    return (
        output,
        input_grad,
        heads_sum,
        small[6 * width : 8 * width].reshape(2, width),
        merge_sum,
        model_sums[4],
        expand_sum,
        small[8 * width :],
        shrink_sum,
        model_sums[5],
        model_sums[0:2],
        model_sums[2:4],
    )


def solution(mesh):
    placed = (
        P(("dp", "row"), None, "col"),
        P(("dp", "row"), None, "col"),
        P(("dp", "row")),
        P("row", None, "col"),
        P(None, "col"),
        P("col", "row"),
        P("col"),
        P("row", "col"),
        P("col"),
        P("col", "row"),
        P("col"),
        P(None, "col"),
        P(None, "col"),
    )
    return jax.shard_map(
        shards,
        mesh=mesh,
        in_specs=placed,
        out_specs=(
            P(("dp", "row"), None, "col"),
            P(("dp", "row"), None, "col"),
            P("row", None, "col"),
            P(None, "col"),
            P("col", "row"),
            P("col"),
            P("row", "col"),
            P("col"),
            P("col", "row"),
            P("col"),
            P(None, "col"),
            P(None, "col"),
        ),
        check_vma=False,
    )
```

profile of v0, /device:TPU:0, one launch (start us, length us, event | category | flops | bytes accessed | tf_op | source)
XLA Modules:
  0.0 397.3 jit_solution(8852050101994276976)
XLA Ops:
  13.2 4.7 %collective-permute-start.2 = (bf16[784,128]{1,0:T(8,128)(2,1)}, bf16[784,128]{1,0:T(8,128)(2,1)}, u32[]{:S(2)}, u32[]{:S(2)}) collective-permute-start(bf16[784,128]{1,0:T(8,128)(2,1)} %pad_maximum_fusion.5), channel_id=1, source_target_pairs={{0,6},{2,4},{4,2},{6,0},{1,7},{3,5},{5,3},{7,1},{8,14},{10,12},{12... | collective-permute-start | bytes 602120 | tf_op jit(solution)/shard_map/ppermute | solution.py:21
  23.0 3.5 join.1
  26.5 9.3 %collective-permute-done.1.refs_1_ = bf16[784,128]{1,0:T(8,128)(2,1)} collective-permute-done((bf16[784,128]{1,0:T(8,128)(2,1)}, bf16[784,128]{1,0:T(8,128)(2,1)}, u32[]{:S(2)}, u32[]{:S(2)}) %collective-permute-start.1) | collective-permute-done | bytes 200736 | tf_op jit(solution)/shard_map/ppermute | solution.py:21
  43.6 6.2 %mix.4 = (bf16[2,592,384]{2,1,0:T(8,128)(2,1)}, bf16[2,592,512]{2,1,0:T(8,128)(2,1)}, bf16[1024,1536]{1,0:T(8,128)(2,1)}, f32[2,592,128]{2,1,0:T(8,128)}, f32[2,8,592]{2,1,0:T(8,128)}) custom-call(s32[3]{0:T(128)S(1)} %pad_add_fusion.at_ref, bf16[2,592,1024]{2,1,0:T(8,128)(2,1)S(1)} %copy-done.2, bf16[3,256,512]{2,1,0:T(8,128)(2,1)S(1)} %bitcast.119, ...), custom_call_target="tpu_custom_call" | custom-call | flops 20000000 | bytes 1024 | tf_op jit(solution)/shard_map/mix/pallas_call | solution.py:636
  49.9 5.2 %collective-permute-done.6.rest_ref = bf16[2320,128]{1,0:T(8,128)(2,1)S(1)} collective-permute-done((bf16[2320,128]{1,0:T(8,128)(2,1)S(1)}, bf16[2320,128]{1,0:T(8,128)(2,1)S(1)}, u32[]{:S(2)}, u32[]{:S(2)}) %collective-permute-start.6) | collective-permute-done | bytes 593952 | tf_op jit(solution)/shard_map/ppermute | solution.py:21
  55.1 6.3 %mix.5 = (bf16[2,592,384]{2,1,0:T(8,128)(2,1)}, bf16[2,592,512]{2,1,0:T(8,128)(2,1)}, bf16[1024,1536]{1,0:T(8,128)(2,1)}, f32[2,592,128]{2,1,0:T(8,128)}, f32[2,8,592]{2,1,0:T(8,128)}) custom-call(s32[3]{0:T(128)S(1)} %pad_add_fusion.at_ref, bf16[2,592,1024]{2,1,0:T(8,128)(2,1)S(1)} %copy-done.2, ...), custom_call_target="tpu_custom_call", output_to_operand_aliasing={{1}: (5, {}), {2}: (6, {})} | custom-call | flops 20000000 | bytes 1024 | tf_op jit(solution)/shard_map/mix/pallas_call | solution.py:636
  61.4 6.3 %collective-permute-done.5.rest_ref = bf16[2320,128]{1,0:T(8,128)(2,1)S(1)} collective-permute-done((bf16[2320,128]{1,0:T(8,128)(2,1)S(1)}, bf16[2320,128]{1,0:T(8,128)(2,1)S(1)}, u32[]{:S(2)}, u32[]{:S(2)}) %collective-permute-start.5) | collective-permute-done | bytes 593952 | tf_op jit(solution)/shard_map/ppermute | solution.py:21
  67.7 6.2 %mix.6 = (bf16[2,592,384]{2,1,0:T(8,128)(2,1)}, bf16[2,592,512]{2,1,0:T(8,128)(2,1)}, bf16[1024,1536]{1,0:T(8,128)(2,1)}, f32[2,592,128]{2,1,0:T(8,128)}, f32[2,8,592]{2,1,0:T(8,128)}) custom-call(s32[3]{0:T(128)S(1)} %pad_add_fusion.at_ref, bf16[2,592,1024]{2,1,0:T(8,128)(2,1)S(1)} %copy-done.2, ...), custom_call_target="tpu_custom_call", output_to_operand_aliasing={{1}: (5, {}), {2}: (6, {})} | custom-call | flops 20000000 | bytes 1024 | tf_op jit(solution)/shard_map/mix/pallas_call | solution.py:636
  73.9 6.3 %mix.7 = (bf16[2,592,384]{2,1,0:T(8,128)(2,1)}, bf16[2,592,512]{2,1,0:T(8,128)(2,1)}, bf16[1024,1536]{1,0:T(8,128)(2,1)}, f32[2,592,128]{2,1,0:T(8,128)}, f32[2,8,592]{2,1,0:T(8,128)}) custom-call(s32[3]{0:T(128)S(1)} %pad_add_fusion.at_ref, bf16[2,592,1024]{2,1,0:T(8,128)(2,1)S(1)} %copy-done.2, ...), custom_call_target="tpu_custom_call", output_to_operand_aliasing={{1}: (5, {}), {2}: (6, {})} | custom-call | flops 20000000 | bytes 1024 | tf_op jit(solution)/shard_map/mix/pallas_call | solution.py:636
  81.0 1.9 all-gather.5.cloned.1.call-done
  83.0 4.2 %unpack.1 = (bf16[512,1024]{1,0:T(8,128)(2,1)}, bf16[3,256,512]{2,1,0:T(8,128)(2,1)}) custom-call(s32[3]{0:T(128)S(1)} %pad_add_fusion.at_ref, bf16[4,1024,256]{2,1,0:T(8,128)(2,1)} %bitcast.130), custom_call_target="tpu_custom_call" | custom-call | flops 10000000 | bytes 1024 | tf_op jit(solution)/shard_map/unpack/pallas_call | solution.py:356
  90.1 21.1 %all-gather.7.cloned.1.call-done = bf16[2048,256]{1,0:T(8,128)(2,1)} async-done(((bf16[512,256]{1,0:T(8,128)(2,1)}), bf16[2048,256]{1,0:T(8,128)(2,1)}) %all-gather.7.cloned.1.call-update) | async-done | bytes 1048592 | tf_op jit(solution)/shard_map/all_gather | solution.py:838
  111.2 3.9 others.1
  115.2 2.9 convolution_convert_fusion.a_ref
  118.6 2.4 collective-permute-start.11
  121.1 4.7 %all-to-all-start = ((bf16[4,3,512,256]{3,2,1,0:T(8,128)(2,1)}), bf16[4,3,512,256]{3,2,1,0:T(8,128)(2,1)}, u32[]{:S(2)}, u32[]{:S(2)}) async-start(bf16[4,3,512,256]{3,2,1,0:T(8,128)(2,1)} %others.1), calls=%async_computation | async-start | bytes 6291456 | tf_op jit(solution)/shard_map/all_to_all | solution.py:866
  126.9 4.4 %seed.1 = (bf16[2,592,1024]{2,1,0:T(8,128)(2,1)}, bf16[2,592,1024]{2,1,0:T(8,128)(2,1)}, f32[2,1,1024]{2,1,0:T(1,128)}) custom-call(s32[3]{0:T(128)S(1)} %pad_add_fusion.at_ref, bf16[2,592,512]{2,1,0:T(8,128)(2,1)} %pad.9.own_ref, bf16[2,592,512]{2,1,0:T(8,128)(2,1)} %collective-permute-done.10.other_ref, f32[2]{0:T(128)S(1)} %multiply_reduce_fusion.weight_ref), custom_call_target="tpu_custom_call" | custom-call | flops 20000000 | bytes 1024 | tf_op jit(solution)/shard_map/seed/pallas_call | solution.py:302
  131.4 5.6 %norm_two.1 = (f32[2,592,1024]{2,1,0:T(8,128)}, bf16[2,592,1024]{2,1,0:T(8,128)(2,1)}) custom-call(bf16[2,592,1024]{2,1,0:T(8,128)(2,1)S(1)} %copy-done.8, bf16[2,592,1024]{2,1,0:T(8,128)(2,1)} %convolution_convert_fusion.a_ref, bf16[2,592,1024]{2,1,0:T(8,128)(2,1)} %collective-permute-done.9.b_ref, f32[3,1024]{1,0:T(4,128)S(1)} %pad_maximum_fusion.6.params_ref), custom_call_target="tpu_custom_call" | custom-call | flops 20000000 | bytes 1024 | tf_op jit(solution)/shard_map/norm_two/pallas_call | solution.py:169
  138.7 5.6 %expand.4 = (bf16[2,592,2048]{2,1,0:T(8,128)(2,1)}, bf16[2,592,2048]{2,1,0:T(8,128)(2,1)}, bf16[1024,2048]{1,0:T(8,128)(2,1)}) custom-call(s32[3]{0:T(128)S(1)} %pad_add_fusion.at_ref, bf16[2,592,1024]{2,1,0:T(8,128)(2,1)S(1)} %copy-done, bf16[256,2048]{1,0:T(8,128)(2,1)S(1)} %copy-done.5, bf16[3,256,512]{2,1,0:T(8,128)(2,1)} %get-tuple-element.138.rest_ref, ...), custom_call_target="tpu_custom_call" | custom-call | flops 10000000 | bytes 1024 | tf_op jit(solution)/shard_map/expand/pallas_call | solution.py:730
  144.3 4.4 %expand.5 = (bf16[2,592,2048]{2,1,0:T(8,128)(2,1)}, bf16[2,592,2048]{2,1,0:T(8,128)(2,1)}, bf16[1024,2048]{1,0:T(8,128)(2,1)}) custom-call(s32[3]{0:T(128)S(1)} %pad_add_fusion.at_ref, bf16[2,592,1024]{2,1,0:T(8,128)(2,1)S(1)} %copy-done.1, bf16[256,2048]{1,0:T(8,128)(2,1)S(1)} %copy-done.5, ...), custom_call_target="tpu_custom_call", output_to_operand_aliasing={{0}: (5, {}), {1}: (6, {}), {2}: (7, {})} | custom-call | flops 10000000 | bytes 1024 | tf_op jit(solution)/shard_map/expand/pallas_call | solution.py:730
  148.8 4.5 %expand.6 = (bf16[2,592,2048]{2,1,0:T(8,128)(2,1)}, bf16[2,592,2048]{2,1,0:T(8,128)(2,1)}, bf16[1024,2048]{1,0:T(8,128)(2,1)}) custom-call(s32[3]{0:T(128)S(1)} %pad_add_fusion.at_ref, bf16[2,592,1024]{2,1,0:T(8,128)(2,1)S(1)} %copy-done.1, bf16[256,2048]{1,0:T(8,128)(2,1)S(1)} %copy-done.5, ...), custom_call_target="tpu_custom_call", output_to_operand_aliasing={{0}: (5, {}), {1}: (6, {}), {2}: (7, {})} | custom-call | flops 10000000 | bytes 1024 | tf_op jit(solution)/shard_map/expand/pallas_call | solution.py:730
  153.2 5.7 %expand.7 = (bf16[2,592,2048]{2,1,0:T(8,128)(2,1)}, bf16[2,592,2048]{2,1,0:T(8,128)(2,1)}, bf16[1024,2048]{1,0:T(8,128)(2,1)}) custom-call(s32[3]{0:T(128)S(1)} %pad_add_fusion.at_ref, bf16[2,592,1024]{2,1,0:T(8,128)(2,1)S(1)} %copy-done.1, bf16[256,2048]{1,0:T(8,128)(2,1)S(1)} %copy-done.5, ...), custom_call_target="tpu_custom_call", output_to_operand_aliasing={{0}: (5, {}), {1}: (6, {}), {2}: (7, {})} | custom-call | flops 10000000 | bytes 1024 | tf_op jit(solution)/shard_map/expand/pallas_call | solution.py:730
  158.9 9.7 %bitcast_convert_fusion.1 = bf16[2048,1024]{1,0:T(8,128)(2,1)} fusion(bf16[2,592,2048]{2,1,0:T(8,128)(2,1)} %get-tuple-element.194, bf16[2,592,1024]{2,1,0:T(8,128)(2,1)S(1)} %copy-done.44), kind=kOutput, calls=%fused_computation.3 | convolution fusion | flops 4968153088 | bytes 11468800 | tf_op jit(solution)/shard_map/ith,itd->hd/dot_general | solution.py:887
  168.7 4.4 %all-to-all-done.rest_ref = bf16[4,3,512,256]{3,2,1,0:T(8,128)(2,1)} async-done(((bf16[4,3,512,256]{3,2,1,0:T(8,128)(2,1)}), bf16[4,3,512,256]{3,2,1,0:T(8,128)(2,1)}, u32[]{:S(2)}, u32[]{:S(2)}) %all-to-all-start) | async-done | bytes 3145760 | tf_op jit(solution)/shard_map/all_to_all | solution.py:866
  173.1 3.8 place.1
  177.0 7.9 %fusion.4 = f32[2,592,2048]{2,1,0:T(8,128)} fusion(bf16[2,592,1024]{2,1,0:T(8,128)(2,1)S(1)} %copy-done.45, bf16[2048,1024]{1,0:T(8,128)(2,1)S(1)} %place.1), kind=kOutput, calls=%fused_computation.8 | convolution fusion | flops 4966055936 | bytes 16318464 | tf_op jit(solution)/shard_map/itd,hd->ith/dot_general | solution.py:892
  185.0 8.3 %convert_reduce_fusion = (f32[2048]{0:T(1024)S(1)}, bf16[2,592,2048]{2,1,0:T(8,128)(2,1)}) fusion(f32[2,592,2048]{2,1,0:T(8,128)} %fusion.4, bf16[2,592,2048]{2,1,0:T(8,128)(2,1)S(1)} %bitcast.128), kind=kLoop, calls=%fused_computation | loop fusion | flops 12122112 | bytes 19406848 | tf_op jit(solution)/shard_map/reduce_sum | solution.py:894
  193.2 9.9 %bitcast_convert_fusion = bf16[2048,1024]{1,0:T(8,128)(2,1)} fusion(bf16[2,592,2048]{2,1,0:T(8,128)(2,1)} %get-tuple-element.164, bf16[2,592,1024]{2,1,0:T(8,128)(2,1)S(1)} %copy-done.1), kind=kOutput, calls=%fused_computation.2 | convolution fusion | flops 4968153088 | bytes 11468800 | tf_op jit(solution)/shard_map/ith,itd->hd/dot_general | solution.py:895
  203.1 6.6 %fusion.14.a_ref = bf16[2,592,1024]{2,1,0:T(8,128)(2,1)} fusion(bf16[2,592,2048]{2,1,0:T(8,128)(2,1)S(1)} %copy-done.29, bf16[1024,2048]{1,0:T(8,128)(2,1)S(1)} %copy-done.25), kind=kOutput, calls=%fused_computation.16 | convolution fusion | flops 4967268352 | bytes 11468800 | tf_op jit(solution)/shard_map/ith,dh->itd/dot_general | solution.py:900
  209.7 5.0 %all-to-all-start.1 = ((bf16[4,512,1024]{2,1,0:T(8,128)(2,1)}), bf16[4,512,1024]{2,1,0:T(8,128)(2,1)}, u32[]{:S(2)}, u32[]{:S(2)}) async-start(bf16[4,512,1024]{2,1,0:T(8,128)(2,1)} %bitcast.129), calls=%async_computation.1 | async-start | bytes 8388608 | tf_op jit(solution)/shard_map/all_to_all | solution.py:66
  214.7 9.3 %norm_back.2 = (f32[2,592,1024]{2,1,0:T(8,128)}, bf16[2,592,1024]{2,1,0:T(8,128)(2,1)}, f32[2,3,1024]{2,1,0:T(4,128)}) custom-call(s32[3]{0:T(128)S(1)} %pad_add_fusion.at_ref, bf16[2,592,1024]{2,1,0:T(8,128)(2,1)S(1)} %copy-done.12, f32[2,592,1024]{2,1,0:T(8,128)} %get-tuple-element.142.v_ref.m_ref, bf16[2,592,1024]{2,1,0:T(8,128)(2,1)} %fusion.14.a_ref, ...), custom_call_target="tpu_custom_call" | custom-call | flops 20000000 | bytes 1024 | tf_op jit(solution)/shard_map/norm_back/pallas_call | solution.py:223
  224.0 4.3 %convolution_convert_fusion.1.up_ref = bf16[2,592,512]{2,1,0:T(8,128)(2,1)} fusion(bf16[2,592,1024]{2,1,0:T(8,128)(2,1)} %get-tuple-element.166, bf16[512,1024]{1,0:T(8,128)(2,1)S(1)} %copy-done.48), kind=kOutput, calls=%fused_computation.22 | convolution fusion | flops 1242120192 | bytes 4685824 | tf_op jit(solution)/shard_map/itd,fd->itf/dot_general | solution.py:907
  228.4 2.5 bitcast_convert_fusion.2
  230.9 8.0 %mix_back.4 = (bf16[2,592,1536]{2,1,0:T(8,128)(2,1)}, f32[2,1,384]{2,1,0:T(1,128)}) custom-call(s32[3]{0:T(128)S(1)} %pad_add_fusion.at_ref, bf16[2,592,384]{2,1,0:T(8,128)(2,1)} %get-tuple-element.168.m_ref, bf16[2,592,512]{2,1,0:T(8,128)(2,1)} %convolution_convert_fusion.1.up_ref, f32[2,592,128]{2,1,0:T(8,128)} %get-tuple-element.169.exact_ref, ...), custom_call_target="tpu_custom_call" | custom-call | flops 20000000 | bytes 1024 | tf_op jit(solution)/shard_map/mix_back/pallas_call | solution.py:675
  239.0 3.7 bitcast_convert_fusion.6
  242.7 1.9 collective-permute-start.13
  244.6 7.6 %mix_back.5 = (bf16[2,592,1536]{2,1,0:T(8,128)(2,1)}, f32[2,1,384]{2,1,0:T(1,128)}) custom-call(s32[3]{0:T(128)S(1)} %pad_add_fusion.at_ref, bf16[2,592,384]{2,1,0:T(8,128)(2,1)} %get-tuple-element.173.m_ref, bf16[2,592,512]{2,1,0:T(8,128)(2,1)} %convolution_convert_fusion.1.up_ref, ...), custom_call_target="tpu_custom_call", output_to_operand_aliasing={{0}: (5, {})} | custom-call | flops 20000000 | bytes 1024 | tf_op jit(solution)/shard_map/mix_back/pallas_call | solution.py:675
  252.2 3.6 bitcast_convert_fusion.5
  257.3 6.0 %all-to-all-done.1.in_ref = bf16[4,512,1024]{2,1,0:T(8,128)(2,1)} async-done(((bf16[4,512,1024]{2,1,0:T(8,128)(2,1)}), bf16[4,512,1024]{2,1,0:T(8,128)(2,1)}, u32[]{:S(2)}, u32[]{:S(2)}) %all-to-all-start.1) | async-done | bytes 4194336 | tf_op jit(solution)/shard_map/all_to_all | solution.py:66
  263.4 4.2 %add.144 = bf16[512,1024]{1,0:T(8,128)(2,1)} custom-call(bf16[4,512,1024]{2,1,0:T(8,128)(2,1)} %all-to-all-done.1.in_ref), custom_call_target="tpu_custom_call" | custom-call | flops 10000000 | bytes 1024 | tf_op jit(solution)/shard_map/add/pallas_call | solution.py:435
  267.6 7.6 %mix_back.6 = (bf16[2,592,1536]{2,1,0:T(8,128)(2,1)}, f32[2,1,384]{2,1,0:T(1,128)}) custom-call(s32[3]{0:T(128)S(1)} %pad_add_fusion.at_ref, bf16[2,592,384]{2,1,0:T(8,128)(2,1)} %get-tuple-element.180.m_ref, bf16[2,592,512]{2,1,0:T(8,128)(2,1)} %convolution_convert_fusion.1.up_ref, ...), custom_call_target="tpu_custom_call", output_to_operand_aliasing={{0}: (5, {})} | custom-call | flops 20000000 | bytes 1024 | tf_op jit(solution)/shard_map/mix_back/pallas_call | solution.py:675
  275.2 3.6 bitcast_convert_fusion.4
  280.0 2.5 pad_maximum_fusion
  282.4 4.5 %all-to-all-start.2 = ((bf16[4,640,256]{2,1,0:T(8,128)(2,1)}), bf16[4,640,256]{2,1,0:T(8,128)(2,1)}, u32[]{:S(2)}, u32[]{:S(2)}) async-start(bf16[4,640,256]{2,1,0:T(8,128)(2,1)} %pad_maximum_fusion), calls=%async_computation.4 | async-start | bytes 2621440 | tf_op jit(solution)/shard_map/all_to_all | solution.py:66
  286.9 7.6 %mix_back.7 = (bf16[2,592,1536]{2,1,0:T(8,128)(2,1)}, f32[2,1,384]{2,1,0:T(1,128)}) custom-call(s32[3]{0:T(128)S(1)} %pad_add_fusion.at_ref, bf16[2,592,384]{2,1,0:T(8,128)(2,1)} %get-tuple-element.143.m_ref, bf16[2,592,512]{2,1,0:T(8,128)(2,1)} %convolution_convert_fusion.1.up_ref, ...), custom_call_target="tpu_custom_call", output_to_operand_aliasing={{0}: (5, {})} | custom-call | flops 20000000 | bytes 1024 | tf_op jit(solution)/shard_map/mix_back/pallas_call | solution.py:675
  294.5 2.7 bitcast_convert_fusion.3
  297.3 3.3 collective-permute-done.15
  304.2 1.8 collective-permute-start.18
  306.3 6.6 %all-to-all-done.2.in_ref = bf16[4,640,256]{2,1,0:T(8,128)(2,1)} async-done(((bf16[4,640,256]{2,1,0:T(8,128)(2,1)}), bf16[4,640,256]{2,1,0:T(8,128)(2,1)}, u32[]{:S(2)}, u32[]{:S(2)}) %all-to-all-start.2) | async-done | bytes 1310752 | tf_op jit(solution)/shard_map/all_to_all | solution.py:66
  312.9 2.2 add.145
  315.1 5.4 %collective-permute-done.17 = bf16[256,384]{1,0:T(8,128)(2,1)S(1)} collective-permute-done((bf16[256,384]{1,0:T(8,128)(2,1)S(1)}, bf16[256,384]{1,0:T(8,128)(2,1)S(1)}, u32[]{:S(2)}, u32[]{:S(2)}) %collective-permute-start.17) | collective-permute-done | bytes 196640 | tf_op jit(solution)/shard_map/ppermute | solution.py:21
  323.2 4.8 %all-to-all-start.3 = ((bf16[4,1152,256]{2,1,0:T(8,128)(2,1)}), bf16[4,1152,256]{2,1,0:T(8,128)(2,1)}, u32[]{:S(2)}, u32[]{:S(2)}) async-start(bf16[4,1152,256]{2,1,0:T(8,128)(2,1)} %broadcast_in_dim.42), calls=%async_computation.6 | async-start | bytes 4718592 | tf_op jit(solution)/shard_map/all_to_all | solution.py:71
  328.0 7.5 %fusion.8.a_ref = bf16[2,592,1024]{2,1,0:T(8,128)(2,1)} fusion(bf16[2,592,1536]{2,1,0:T(8,128)(2,1)} %get-tuple-element.200, bf16[1024,1536]{1,0:T(8,128)(2,1)S(1)} %copy-done.26), kind=kOutput, calls=%fused_computation.14 | convolution fusion | flops 3725754368 | bytes 9207808 | tf_op jit(solution)/shard_map/itf,df->itd/dot_general | solution.py:950
  335.5 7.8 %fusion.11.in_ref.a_ref = bf16[2,592,1024]{2,1,0:T(8,128)(2,1)S(1)} fusion(bf16[2,592,2048]{2,1,0:T(8,128)(2,1)} %get-tuple-element.194, bf16[2048,1024]{1,0:T(8,128)(2,1)S(1)} %copy-done.11), kind=kOutput, calls=%fused_computation.15 | convolution fusion | flops 4967268352 | bytes 11468800 | tf_op jit(solution)/shard_map/ith,hd->itd/dot_general | solution.py:953
  345.8 2.9 collective-permute-start.23
  349.4 2.4 copy-done.4
  351.8 3.1 close.1
  354.8 3.2 copy.66
  358.1 8.2 %norm_back.3 = (f32[2,577,512]{2,1,0:T(8,128)}, f32[2,2,1024]{2,1,0:T(2,128)}) custom-call(s32[3]{0:T(128)S(1)} %pad_add_fusion.at_ref, f32[2,592,1024]{2,1,0:T(8,128)} %get-tuple-element.199.base_ref, bf16[2,592,1024]{2,1,0:T(8,128)(2,1)S(1)} %copy-done.9, bf16[2,592,1024]{2,1,0:T(8,128)(2,1)} %fusion.8.a_ref, ...), custom_call_target="tpu_custom_call" | custom-call | flops 20000000 | bytes 1024 | tf_op jit(solution)/shard_map/norm_back/pallas_call | solution.py:223
  367.2 2.9 collective-permute-start.26
  375.3 1.9 collective-permute-start.29
  377.2 2.6 collective-permute-start.27
  380.6 3.2 copy.67
  385.7 1.9 spread.1
  (239 shorter events, 50.1 us)
Async XLA Ops:
  7.2 75.8 %all-gather.5.cloned.1.call-start = ((), (), s32[]{:S(2)}) async-start(), calls=%async_computation.10 | async-start | bytes 2621440 | tf_op jit(solution)/shard_map/all_gather | solution.py:834
  12.6 10.3 %collective-permute-start.3 = (bf16[2,592,512]{2,1,0:T(8,128)(2,1)S(1)}, bf16[2,592,512]{2,1,0:T(8,128)(2,1)S(1)}, u32[]{:S(2)}, u32[]{:S(2)}) collective-permute-start(bf16[2,592,512]{2,1,0:T(8,128)(2,1)S(1)} %pad_maximum_fusion.1.own_ref), channel_id=1, source_target_pairs={{0,1},{1,0},{2,3},{3,2},{4,5},{5,4},{6,7},{7,6},{8,9},{9,8},{10,11... | collective-permute-start | bytes 3637256 | tf_op jit(solution)/shard_map/ppermute | solution.py:21
  13.2 13.4 %collective-permute-start.2 = (bf16[784,128]{1,0:T(8,128)(2,1)}, bf16[784,128]{1,0:T(8,128)(2,1)}, u32[]{:S(2)}, u32[]{:S(2)}) collective-permute-start(bf16[784,128]{1,0:T(8,128)(2,1)} %pad_maximum_fusion.5), channel_id=1, source_target_pairs={{0,6},{2,4},{4,2},{6,0},{1,7},{3,5},{5,3},{7,1},{8,14},{10,12},{12... | collective-permute-start | bytes 602120 | tf_op jit(solution)/shard_map/ppermute | solution.py:21
  17.8 18.0 %collective-permute-start.1 = (bf16[784,128]{1,0:T(8,128)(2,1)}, bf16[784,128]{1,0:T(8,128)(2,1)}, u32[]{:S(2)}, u32[]{:S(2)}) collective-permute-start(bf16[784,128]{1,0:T(8,128)(2,1)} %pad_maximum_fusion.5), channel_id=1, source_target_pairs={{0,4},{2,6},{4,0},{6,2},{1,5},{3,7},{5,1},{7,3},{8,12},{10,14},{12... | collective-permute-start | bytes 602120 | tf_op jit(solution)/shard_map/ppermute | solution.py:21
  17.8 18.0 %collective-permute-start = (bf16[784,128]{1,0:T(8,128)(2,1)}, bf16[784,128]{1,0:T(8,128)(2,1)}, u32[]{:S(2)}, u32[]{:S(2)}) collective-permute-start(bf16[784,128]{1,0:T(8,128)(2,1)} %pad_maximum_fusion.5), channel_id=1, source_target_pairs={{0,2},{2,0},{4,6},{6,4},{1,3},{3,1},{5,7},{7,5},{8,10},{10,8},{12,... | collective-permute-start | bytes 602120 | tf_op jit(solution)/shard_map/ppermute | solution.py:21
  22.9 13.0 %copy-start.31 = (bf16[512,256]{1,0:T(8,128)(2,1)S(1)}, bf16[512,256]{1,0:T(8,128)(2,1)}, u32[]{:S(2)}) copy-start(bf16[512,256]{1,0:T(8,128)(2,1)} %param.18) | copy-start | bytes 786436
  23.0 19.4 %copy-start.34 = (bf16[2,512]{1,0:T(2,128)(2,1)S(1)}, bf16[2,512]{1,0:T(2,128)(2,1)}, u32[]{:S(2)}) copy-start(bf16[2,512]{1,0:T(2,128)(2,1)} %param.17) | copy-start | bytes 6148
  26.5 15.9 %copy-start.2 = (bf16[2,592,1024]{2,1,0:T(8,128)(2,1)S(1)}, bf16[2,592,1024]{2,1,0:T(8,128)(2,1)}, u32[]{:S(2)}) copy-start(bf16[2,592,1024]{2,1,0:T(8,128)(2,1)} %get-tuple-element.124.n_ref) | copy-start | bytes 7274500
  36.7 74.5 %all-gather.7.cloned.1.call-start = ((), (), s32[]{:S(2)}) async-start(), calls=%async_computation.11 | async-start | bytes 1310720 | tf_op jit(solution)/shard_map/all_gather | solution.py:838
  37.4 17.7 %copy-start.7 = (bf16[256,3,512]{2,0,1:T(8,128)(2,1)S(1)}, bf16[256,3,512]{2,0,1:T(8,128)(2,1)}, u32[]{:S(2)}) copy-start(bf16[256,3,512]{2,0,1:T(8,128)(2,1)} %param.16) | copy-start | bytes 2359300
  38.7 22.7 %copy-start.13 = (bf16[2320,128]{1,0:T(8,128)(2,1)}, bf16[2320,128]{1,0:T(8,128)(2,1)S(1)}, u32[]{:S(2)}) copy-start(bf16[2320,128]{1,0:T(8,128)(2,1)S(1)} %stack.63.rest_ref) | copy-start | bytes 1781764
  38.7 16.4 %collective-permute-start.6 = (bf16[2320,128]{1,0:T(8,128)(2,1)S(1)}, bf16[2320,128]{1,0:T(8,128)(2,1)S(1)}, u32[]{:S(2)}, u32[]{:S(2)}) collective-permute-start(bf16[2320,128]{1,0:T(8,128)(2,1)S(1)} %stack.63.rest_ref), channel_id=1, source_target_pairs={{0,8},{8,0},{16,24},{24,16},{1,9},{9,1},{17,25},{25,17},{2,10},{10... | collective-permute-start | bytes 1781768 | tf_op jit(solution)/shard_map/ppermute | solution.py:21
  40.3 27.4 %collective-permute-start.5 = (bf16[2320,128]{1,0:T(8,128)(2,1)S(1)}, bf16[2320,128]{1,0:T(8,128)(2,1)S(1)}, u32[]{:S(2)}, u32[]{:S(2)}) collective-permute-start(bf16[2320,128]{1,0:T(8,128)(2,1)S(1)} %stack.63.rest_ref), channel_id=1, source_target_pairs={{0,16},{8,24},{16,0},{24,8},{1,17},{9,25},{17,1},{25,9},{2,18},{10... | collective-permute-start | bytes 1781768 | tf_op jit(solution)/shard_map/ppermute | solution.py:21
  41.8 32.2 %collective-permute-start.4 = (bf16[2320,128]{1,0:T(8,128)(2,1)S(1)}, bf16[2320,128]{1,0:T(8,128)(2,1)S(1)}, u32[]{:S(2)}, u32[]{:S(2)}) collective-permute-start(bf16[2320,128]{1,0:T(8,128)(2,1)S(1)} %stack.63.rest_ref), channel_id=1, source_target_pairs={{0,24},{8,16},{16,8},{24,0},{1,25},{9,17},{17,9},{25,1},{2,26},{10... | collective-permute-start | bytes 1781768 | tf_op jit(solution)/shard_map/ppermute | solution.py:21
  55.1 6.3 %copy-start.18 = (bf16[2320,128]{1,0:T(8,128)(2,1)}, bf16[2320,128]{1,0:T(8,128)(2,1)S(1)}, u32[]{:S(2)}) copy-start(bf16[2320,128]{1,0:T(8,128)(2,1)S(1)} %collective-permute-done.6.rest_ref) | copy-start | bytes 1781764
  67.7 6.2 %copy-start.19 = (bf16[2320,128]{1,0:T(8,128)(2,1)}, bf16[2320,128]{1,0:T(8,128)(2,1)S(1)}, u32[]{:S(2)}) copy-start(bf16[2320,128]{1,0:T(8,128)(2,1)S(1)} %collective-permute-done.5.rest_ref) | copy-start | bytes 1781764
  87.2 27.9 %collective-permute-start.8 = (bf16[3,256,512]{2,1,0:T(8,128)(2,1)}, bf16[3,256,512]{2,1,0:T(8,128)(2,1)S(1)}, u32[]{:S(2)}, u32[]{:S(2)}) collective-permute-start(bf16[3,256,512]{2,1,0:T(8,128)(2,1)} %get-tuple-element.138.rest_ref), channel_id=1, source_target_pairs={{0,16},{8,24},{16,0},{24,8},{1,17},{9,25},{17,1},{25,9},{2,18},{10... | collective-permute-start | bytes 2359304 | tf_op jit(solution)/shard_map/ppermute | solution.py:21
  88.7 26.5 %collective-permute-start.7 = (bf16[3,256,512]{2,1,0:T(8,128)(2,1)}, bf16[3,256,512]{2,1,0:T(8,128)(2,1)S(1)}, u32[]{:S(2)}, u32[]{:S(2)}) collective-permute-start(bf16[3,256,512]{2,1,0:T(8,128)(2,1)} %get-tuple-element.138.rest_ref), channel_id=1, source_target_pairs={{0,8},{8,0},{16,24},{24,16},{1,9},{9,1},{17,25},{25,17},{2,10},{10... | collective-permute-start | bytes 2359304 | tf_op jit(solution)/shard_map/ppermute | solution.py:21
  115.2 5.8 %copy-start.38 = (bf16[2048]{0:T(1024)(128)(2,1)S(1)}, bf16[2048]{0:T(1024)(128)(2,1)}, u32[]{:S(2)}) copy-start(bf16[2048]{0:T(1024)(128)(2,1)} %param.21) | copy-start | bytes 12292
  115.2 5.8 %copy-start.49 = (s32[2]{0:T(128)S(1)}, s32[2]{0:T(128)}, u32[]{:S(2)}) copy-start(s32[2]{0:T(128)} %param.15) | copy-start | bytes 28
  118.1 13.3 %collective-permute-start.9 = (bf16[2,592,1024]{2,1,0:T(8,128)(2,1)}, bf16[2,592,1024]{2,1,0:T(8,128)(2,1)}, u32[]{:S(2)}, u32[]{:S(2)}) collective-permute-start(bf16[2,592,1024]{2,1,0:T(8,128)(2,1)} %convolution_convert_fusion.a_ref), channel_id=1, source_target_pairs={{0,1},{1,0},{2,3},{3,2},{4,5},{5,4},{6,7},{7,6},{8,9},{9,8},{10,11... | collective-permute-start | bytes 7274504 | tf_op jit(solution)/shard_map/ppermute | solution.py:21
  118.1 8.8 %collective-permute-start.10 = (bf16[2,592,512]{2,1,0:T(8,128)(2,1)}, bf16[2,592,512]{2,1,0:T(8,128)(2,1)}, u32[]{:S(2)}, u32[]{:S(2)}) collective-permute-start(bf16[2,592,512]{2,1,0:T(8,128)(2,1)} %pad.9.own_ref), channel_id=1, source_target_pairs={{0,1},{1,0},{2,3},{3,2},{4,5},{5,4},{6,7},{7,6},{8,9},{9,8},{10,11... | collective-permute-start | bytes 3637256 | tf_op jit(solution)/shard_map/ppermute | solution.py:21
  118.6 34.6 %collective-permute-start.11 = (bf16[3,256,512]{2,1,0:T(8,128)(2,1)}, bf16[3,256,512]{2,1,0:T(8,128)(2,1)}, u32[]{:S(2)}, u32[]{:S(2)}) collective-permute-start(bf16[3,256,512]{2,1,0:T(8,128)(2,1)} %get-tuple-element.138.rest_ref), channel_id=1, source_target_pairs={{0,24},{8,16},{16,8},{24,0},{1,25},{9,17},{17,9},{25,1},{2,26},{10... | collective-permute-start | bytes 2359304 | tf_op jit(solution)/shard_map/ppermute | solution.py:21
  121.1 52.0 %all-to-all-start = ((bf16[4,3,512,256]{3,2,1,0:T(8,128)(2,1)}), bf16[4,3,512,256]{3,2,1,0:T(8,128)(2,1)}, u32[]{:S(2)}, u32[]{:S(2)}) async-start(bf16[4,3,512,256]{3,2,1,0:T(8,128)(2,1)} %others.1), calls=%async_computation | async-start | bytes 6291456 | tf_op jit(solution)/shard_map/all_to_all | solution.py:866
  125.8 141.8 %reduce-scatter.4.cloned.1.call-start = ((), (), s32[]{:S(2)}) async-start(), calls=%async_computation.7 | async-start | bytes 5242880 | tf_op jit(solution)/shard_map/reduce_scatter | solution.py:75
  131.4 12.9 %copy-start.17 = (bf16[3,256,512]{2,1,0:T(8,128)(2,1)S(1)}, bf16[3,256,512]{2,1,0:T(8,128)(2,1)}, u32[]{:S(2)}) copy-start(bf16[3,256,512]{2,1,0:T(8,128)(2,1)} %copy-done.16) | copy-start | bytes 2359300
  153.2 5.7 %copy-start.44 = (bf16[2,592,1024]{2,1,0:T(8,128)(2,1)S(1)}, bf16[2,592,1024]{2,1,0:T(8,128)(2,1)}, u32[]{:S(2)}) copy-start(bf16[2,592,1024]{2,1,0:T(8,128)(2,1)} %get-tuple-element.161) | copy-start | bytes 7274500
  173.1 11.8 %slice-start = ((s8[4849664]{0:T(1024)(128)(4,1)}), s8[4194304]{0:T(1024)(128)(4,1)S(1)}, s32[]{:S(2)}) async-start(s8[4849664]{0:T(1024)(128)(4,1)} %bitcast.127), calls=%async_computation.12 | async-start | bytes 8388608
  177.0 8.0 %copy-start.10 = (bf16[2048,1024]{1,0:T(8,128)(2,1)}, bf16[2048,1024]{1,0:T(8,128)(2,1)S(1)}, u32[]{:S(2)}) copy-start(bf16[2048,1024]{1,0:T(8,128)(2,1)S(1)} %place.1) | copy-start | bytes 12582916
  177.0 8.0 %slice-start.1 = ((s8[4849664]{0:T(1024)(128)(4,1)}), s8[655360]{0:T(1024)(128)(4,1)S(1)}, s32[]{:S(2)}) async-start(s8[4849664]{0:T(1024)(128)(4,1)} %bitcast.127), calls=%async_computation.13 | async-start | bytes 1310720
  193.2 9.9 %copy-start.25 = (bf16[1024,2048]{1,0:T(8,128)(2,1)S(1)}, bf16[1024,2048]{1,0:T(8,128)(2,1)}, u32[]{:S(2)}) copy-start(bf16[1024,2048]{1,0:T(8,128)(2,1)} %get-tuple-element.165) | copy-start | bytes 12582916
  193.2 9.9 %copy-start.29 = (bf16[2,592,2048]{2,1,0:T(8,128)(2,1)S(1)}, bf16[2,592,2048]{2,1,0:T(8,128)(2,1)}, u32[]{:S(2)}) copy-start(bf16[2,592,2048]{2,1,0:T(8,128)(2,1)} %get-tuple-element.164) | copy-start | bytes 14548996
  209.6 5.0 %collective-permute-start.12 = (bf16[2,592,1024]{2,1,0:T(8,128)(2,1)}, bf16[2,592,1024]{2,1,0:T(8,128)(2,1)}, u32[]{:S(2)}, u32[]{:S(2)}) collective-permute-start(bf16[2,592,1024]{2,1,0:T(8,128)(2,1)} %fusion.14.a_ref), channel_id=1, source_target_pairs={{0,1},{1,0},{2,3},{3,2},{4,5},{5,4},{6,7},{7,6},{8,9},{9,8},{10,11... | collective-permute-start | bytes 7274504 | tf_op jit(solution)/shard_map/ppermute | solution.py:21
  209.7 53.7 %all-to-all-start.1 = ((bf16[4,512,1024]{2,1,0:T(8,128)(2,1)}), bf16[4,512,1024]{2,1,0:T(8,128)(2,1)}, u32[]{:S(2)}, u32[]{:S(2)}) async-start(bf16[4,512,1024]{2,1,0:T(8,128)(2,1)} %bitcast.129), calls=%async_computation.1 | async-start | bytes 8388608 | tf_op jit(solution)/shard_map/all_to_all | solution.py:66
  214.6 65.3 %reduce-scatter.6.cloned.1.call-start = ((), (), s32[]{:S(2)}) async-start(), calls=%async_computation.8 | async-start | bytes 1310720 | tf_op jit(solution)/shard_map/reduce_scatter | solution.py:75
  214.7 9.3 %copy-start.48 = (bf16[512,1024]{1,0:T(8,128)(2,1)S(1)}, bf16[512,1024]{1,0:T(8,128)(2,1)}, u32[]{:S(2)}) copy-start(bf16[512,1024]{1,0:T(8,128)(2,1)} %get-tuple-element.141) | copy-start | bytes 3145732
  230.9 8.1 %copy-start.3 = (bf16[2,592,1024]{2,1,0:T(8,128)(2,1)S(1)}, bf16[2,592,1024]{2,1,0:T(8,128)(2,1)}, u32[]{:S(2)}) copy-start(bf16[2,592,1024]{2,1,0:T(8,128)(2,1)} %get-tuple-element.124.n_ref) | copy-start | bytes 7274500
  230.9 89.7 %reduce-scatter.8.cloned.1.call-start = ((), (), s32[]{:S(2)}) async-start(), calls=%async_computation.9 | async-start | bytes 1310720 | tf_op jit(solution)/shard_map/reduce_scatter | solution.py:75
  242.7 37.3 %collective-permute-start.13 = (bf16[1024,384]{1,0:T(8,128)(2,1)}, bf16[1024,384]{1,0:T(8,128)(2,1)S(1)}, u32[]{:S(2)}, u32[]{:S(2)}) collective-permute-start(bf16[1024,384]{1,0:T(8,128)(2,1)} %bitcast_convert_fusion.6), channel_id=1, source_target_pairs={{0,8},{8,0},{16,24},{24,16},{1,9},{9,1},{17,25},{25,17},{2,10},{10... | collective-permute-start | bytes 2359304 | tf_op jit(solution)/shard_map/ppermute | solution.py:21
  255.8 11.8 %copy-start.22 = (f32[2,8,592]{2,1,0:T(8,128)S(1)}, f32[2,8,592]{2,1,0:T(8,128)}, u32[]{:S(2)}) copy-start(f32[2,8,592]{2,1,0:T(8,128)} %get-tuple-element.182.stats_ref) | copy-start | bytes 113668
  255.8 41.4 %collective-permute-start.14 = (bf16[1024,384]{1,0:T(8,128)(2,1)}, bf16[1024,384]{1,0:T(8,128)(2,1)}, u32[]{:S(2)}, u32[]{:S(2)}) collective-permute-start(bf16[1024,384]{1,0:T(8,128)(2,1)} %bitcast_convert_fusion.5), channel_id=1, source_target_pairs={{0,16},{8,24},{16,0},{24,8},{1,17},{9,25},{17,1},{25,9},{2,18},{10... | collective-permute-start | bytes 2359304 | tf_op jit(solution)/shard_map/ppermute | solution.py:21
  278.8 21.8 %collective-permute-start.15 = (bf16[1024,384]{1,0:T(8,128)(2,1)}, bf16[1024,384]{1,0:T(8,128)(2,1)}, u32[]{:S(2)}, u32[]{:S(2)}) collective-permute-start(bf16[1024,384]{1,0:T(8,128)(2,1)} %bitcast_convert_fusion.4), channel_id=1, source_target_pairs={{0,24},{8,16},{16,8},{24,0},{1,25},{9,17},{17,9},{25,1},{2,26},{10... | collective-permute-start | bytes 2359304 | tf_op jit(solution)/shard_map/ppermute | solution.py:21
  280.0 7.0 %copy-start.21 = (f32[2,8,592]{2,1,0:T(8,128)S(1)}, f32[2,8,592]{2,1,0:T(8,128)}, u32[]{:S(2)}) copy-start(f32[2,8,592]{2,1,0:T(8,128)} %get-tuple-element.189.stats_ref) | copy-start | bytes 113668
  282.4 30.5 %all-to-all-start.2 = ((bf16[4,640,256]{2,1,0:T(8,128)(2,1)}), bf16[4,640,256]{2,1,0:T(8,128)(2,1)}, u32[]{:S(2)}, u32[]{:S(2)}) async-start(bf16[4,640,256]{2,1,0:T(8,128)(2,1)} %pad_maximum_fusion), calls=%async_computation.4 | async-start | bytes 2621440 | tf_op jit(solution)/shard_map/all_to_all | solution.py:66
  302.7 12.4 %collective-permute-start.16 = (bf16[256,384]{1,0:T(8,128)(2,1)S(1)}, bf16[256,384]{1,0:T(8,128)(2,1)S(1)}, u32[]{:S(2)}, u32[]{:S(2)}) collective-permute-start(bf16[256,384]{1,0:T(8,128)(2,1)S(1)} %get-tuple-element.266), channel_id=1, source_target_pairs={{0,2},{2,0},{4,6},{6,4},{1,3},{3,1},{5,7},{7,5},{8,10},{10,8},{12,... | collective-permute-start | bytes 589832 | tf_op jit(solution)/shard_map/ppermute | solution.py:21
  304.2 10.9 %collective-permute-start.18 = (bf16[256,384]{1,0:T(8,128)(2,1)S(1)}, bf16[256,384]{1,0:T(8,128)(2,1)S(1)}, u32[]{:S(2)}, u32[]{:S(2)}) collective-permute-start(bf16[256,384]{1,0:T(8,128)(2,1)S(1)} %get-tuple-element.267), channel_id=1, source_target_pairs={{0,6},{2,4},{4,2},{6,0},{1,7},{3,5},{5,3},{7,1},{8,14},{10,12},{12... | collective-permute-start | bytes 589832 | tf_op jit(solution)/shard_map/ppermute | solution.py:21
  306.0 14.5 %collective-permute-start.17 = (bf16[256,384]{1,0:T(8,128)(2,1)S(1)}, bf16[256,384]{1,0:T(8,128)(2,1)S(1)}, u32[]{:S(2)}, u32[]{:S(2)}) collective-permute-start(bf16[256,384]{1,0:T(8,128)(2,1)S(1)} %get-tuple-element.268), channel_id=1, source_target_pairs={{0,4},{2,6},{4,0},{6,2},{1,5},{3,7},{5,1},{7,3},{8,12},{10,14},{12... | collective-permute-start | bytes 589832 | tf_op jit(solution)/shard_map/ppermute | solution.py:21
  323.2 43.1 %all-to-all-start.3 = ((bf16[4,1152,256]{2,1,0:T(8,128)(2,1)}), bf16[4,1152,256]{2,1,0:T(8,128)(2,1)}, u32[]{:S(2)}, u32[]{:S(2)}) async-start(bf16[4,1152,256]{2,1,0:T(8,128)(2,1)} %broadcast_in_dim.42), calls=%async_computation.6 | async-start | bytes 4718592 | tf_op jit(solution)/shard_map/all_to_all | solution.py:71
  328.0 7.5 %copy-start.11 = (bf16[2048,1024]{1,0:T(8,128)(2,1)S(1)}, bf16[2048,1024]{1,0:T(8,128)(2,1)}, u32[]{:S(2)}) copy-start(bf16[2048,1024]{1,0:T(8,128)(2,1)} %copy-done.10) | copy-start | bytes 12582916
  335.5 22.6 %collective-permute-start.20 = (bf16[2,592,1024]{2,1,0:T(8,128)(2,1)}, bf16[2,592,1024]{2,1,0:T(8,128)(2,1)}, u32[]{:S(2)}, u32[]{:S(2)}) collective-permute-start(bf16[2,592,1024]{2,1,0:T(8,128)(2,1)} %fusion.8.a_ref), channel_id=1, source_target_pairs={{0,1},{1,0},{2,3},{3,2},{4,5},{5,4},{6,7},{7,6},{8,9},{9,8},{10,11... | collective-permute-start | bytes 7274504 | tf_op jit(solution)/shard_map/ppermute | solution.py:21
  345.1 4.3 %collective-permute-start.19 = (bf16[2,592,512]{2,1,0:T(8,128)(2,1)}, bf16[2,592,512]{2,1,0:T(8,128)(2,1)}, u32[]{:S(2)}, u32[]{:S(2)}) collective-permute-start(bf16[2,592,512]{2,1,0:T(8,128)(2,1)} %half.1), channel_id=1, source_target_pairs={{0,1},{1,0},{2,3},{3,2},{4,5},{5,4},{6,7},{7,6},{8,9},{9,8},{10,11... | collective-permute-start | bytes 3637256 | tf_op jit(solution)/shard_map/ppermute | solution.py:21
  345.7 9.2 %copy-start.32 = (f32[3,1024]{1,0:T(4,128)}, f32[3,1024]{1,0:T(4,128)S(1)}, u32[]{:S(2)}) copy-start(f32[3,1024]{1,0:T(4,128)S(1)} %reduce_sum.67) | copy-start | bytes 36868
  345.8 20.5 %collective-permute-start.23 = (bf16[256,384]{1,0:T(8,128)(2,1)S(1)}, bf16[256,384]{1,0:T(8,128)(2,1)S(1)}, u32[]{:S(2)}, u32[]{:S(2)}) collective-permute-start(bf16[256,384]{1,0:T(8,128)(2,1)S(1)} %fusion.25.refs_0_), channel_id=1, source_target_pairs={{0,24},{8,16},{16,8},{24,0},{1,25},{9,17},{17,9},{25,1},{2,26},{10... | collective-permute-start | bytes 589832 | tf_op jit(solution)/shard_map/ppermute | solution.py:21
  348.7 17.6 %collective-permute-start.22 = (bf16[256,384]{1,0:T(8,128)(2,1)S(1)}, bf16[256,384]{1,0:T(8,128)(2,1)S(1)}, u32[]{:S(2)}, u32[]{:S(2)}) collective-permute-start(bf16[256,384]{1,0:T(8,128)(2,1)S(1)} %fusion.25.refs_0_), channel_id=1, source_target_pairs={{0,16},{8,24},{16,0},{24,8},{1,17},{9,25},{17,1},{25,9},{2,18},{10... | collective-permute-start | bytes 589832 | tf_op jit(solution)/shard_map/ppermute | solution.py:21
  349.3 17.0 %collective-permute-start.21 = (bf16[256,384]{1,0:T(8,128)(2,1)S(1)}, bf16[256,384]{1,0:T(8,128)(2,1)S(1)}, u32[]{:S(2)}, u32[]{:S(2)}) collective-permute-start(bf16[256,384]{1,0:T(8,128)(2,1)S(1)} %fusion.25.refs_0_), channel_id=1, source_target_pairs={{0,8},{8,0},{16,24},{24,16},{1,9},{9,1},{17,25},{25,17},{2,10},{10... | collective-permute-start | bytes 589832 | tf_op jit(solution)/shard_map/ppermute | solution.py:21
  351.8 6.3 %copy-start.9 = (bf16[2,592,1024]{2,1,0:T(8,128)(2,1)S(1)}, bf16[2,592,1024]{2,1,0:T(8,128)(2,1)}, u32[]{:S(2)}) copy-start(bf16[2,592,1024]{2,1,0:T(8,128)(2,1)} %get-tuple-element.123.x_ref.v_ref) | copy-start | bytes 7274500
  358.1 9.0 %slice-start.2 = ((f32[3,1024]{1,0:T(4,128)}), f32[1,1024]{1,0:T(1,128)S(1)}, s32[]{:S(2)}) async-start(f32[3,1024]{1,0:T(4,128)} %copy-done.32), calls=%async_computation.14 | async-start | bytes 8192 | tf_op jit(solution)/shard_map/slice | solution.py:974
  367.2 8.1 %collective-permute-start.26 = (f32[6144]{0:T(1024)S(1)}, f32[6144]{0:T(1024)S(1)}, u32[]{:S(2)}, u32[]{:S(2)}) collective-permute-start(f32[6144]{0:T(1024)S(1)} %constant_dynamic-update-slice_fusion), channel_id=1, source_target_pairs={{0,24},{8,16},{16,8},{24,0},{1,25},{9,17},{17,9},{25,1},{2,26},{10... | collective-permute-start | bytes 73736 | tf_op jit(solution)/shard_map/ppermute | solution.py:21
  370.1 5.2 %collective-permute-start.25 = (f32[6144]{0:T(1024)S(1)}, f32[6144]{0:T(1024)S(1)}, u32[]{:S(2)}, u32[]{:S(2)}) collective-permute-start(f32[6144]{0:T(1024)S(1)} %constant_dynamic-update-slice_fusion), channel_id=1, source_target_pairs={{0,16},{8,24},{16,0},{24,8},{1,17},{9,25},{17,1},{25,9},{2,18},{10... | collective-permute-start | bytes 73736 | tf_op jit(solution)/shard_map/ppermute | solution.py:21
  370.6 4.7 %collective-permute-start.24 = (f32[6144]{0:T(1024)S(1)}, f32[6144]{0:T(1024)S(1)}, u32[]{:S(2)}, u32[]{:S(2)}) collective-permute-start(f32[6144]{0:T(1024)S(1)} %constant_dynamic-update-slice_fusion), channel_id=1, source_target_pairs={{0,8},{8,0},{16,24},{24,16},{1,9},{9,1},{17,25},{25,17},{2,10},{10... | collective-permute-start | bytes 73736 | tf_op jit(solution)/shard_map/ppermute | solution.py:21
  374.0 6.7 %copy-start.30 = (f32[2,577,512]{2,1,0:T(8,128)S(1)}, f32[2,577,512]{2,1,0:T(8,128)}, u32[]{:S(2)}) copy-start(f32[2,577,512]{2,1,0:T(8,128)} %get-tuple-element.247) | copy-start | bytes 7090180
  375.3 12.2 %collective-permute-start.29 = (f32[6144]{0:T(1024)S(1)}, f32[6144]{0:T(1024)S(1)}, u32[]{:S(2)}, u32[]{:S(2)}) collective-permute-start(f32[6144]{0:T(1024)S(1)} %add_add_fusion.1), channel_id=1, source_target_pairs={{0,6},{2,4},{4,2},{6,0},{1,7},{3,5},{5,3},{7,1},{8,14},{10,12},{12... | collective-permute-start | bytes 73736 | tf_op jit(solution)/shard_map/ppermute | solution.py:21
  377.2 10.3 %collective-permute-start.28 = (f32[6144]{0:T(1024)S(1)}, f32[6144]{0:T(1024)S(1)}, u32[]{:S(2)}, u32[]{:S(2)}) collective-permute-start(f32[6144]{0:T(1024)S(1)} %add_add_fusion.1), channel_id=1, source_target_pairs={{0,4},{2,6},{4,0},{6,2},{1,5},{3,7},{5,1},{7,3},{8,12},{10,14},{12... | collective-permute-start | bytes 73736 | tf_op jit(solution)/shard_map/ppermute | solution.py:21
  377.2 10.3 %collective-permute-start.27 = (f32[6144]{0:T(1024)S(1)}, f32[6144]{0:T(1024)S(1)}, u32[]{:S(2)}, u32[]{:S(2)}) collective-permute-start(f32[6144]{0:T(1024)S(1)} %add_add_fusion.1), channel_id=1, source_target_pairs={{0,2},{2,0},{4,6},{6,4},{1,3},{3,1},{5,7},{7,5},{8,10},{10,8},{12,... | collective-permute-start | bytes 73736 | tf_op jit(solution)/shard_map/ppermute | solution.py:21
  (28 other events, 97.6 us)
Sparse Core Ops, SparseCore 0:
  36.8 46.0 all-gather.4
  84.5 26.6 all-gather.6
  168.8 76.6 reduce-scatter.3
  248.4 27.6 reduce-scatter.5
  278.8 26.2 reduce-scatter.7
where the time goes:
time: 401 us; the launch traced here: 397 us
  Pallas kernels  133 us (33%)
  matrix products  72.8 us (18%)
  waiting for transfers between devices  70 us (17%)
  starting transfers between devices  55.1 us (14%)
  local copies, waits for them, and re-layouts  30.3 us (8%)
  other arithmetic  20.8 us (5%)
  between operations  14.9 us (4%)
    ppermute x30, starting transfers between devices, peer(): return lax.ppermute(value, axis, [(i, i ^ p) for i in range(n)])  35.4 us
    pallas_call x4, Pallas kernels, mix_back(): scalar_call(functools.partial(mix_back_kernel, length), at, (count,), [pl...  30.8 us
    ppermute x30, waiting for transfers between devices, peer(): return lax.ppermute(value, axis, [(i, i ^ p) for i in range(n)])  29.6 us
    pallas_call x4, Pallas kernels, mix(): scalar_call(functools.partial(mix_kernel, length, n_row), at, (count,), [...  25 us
    all_gather x1, waiting for transfers between devices, shards(): shrink_rows = lax.all_gather(shrink_send, 'row')  21.1 us
    pallas_call x4, Pallas kernels, up(): scalar_call(functools.partial(up_kernel, model // own.shape[0]), at, (cou...  20.2 us
    pallas_call x2, Pallas kernels, norm_back(): scalar_call(functools.partial(norm_back_kernel, second), at, (count,), [i...  17.5 us
    dot_general x4, matrix products, shards(): jnp.einsum('itd,itf->df', normed, piece, preferred_element_type=F32)  13.6 us
  transfers between devices with their start and end apart: 39, of which 10 were waited for; matrix products, arithmetic and copies ran while one was open for 26% of the time, Pallas kernels for 34%

commit v1 on v0

--- a/solution.py
+++ b/solution.py
@@ -118,7 +118,7 @@
 
 
 def cost(us, moved=1 << 20):
-    return pl.CostEstimate(flops=int(us * 1.0e7), bytes_accessed=1024, transcendentals=0)
+    return pl.CostEstimate(flops=int(us * 1.0e9), bytes_accessed=1024, transcendentals=0)
 
 
 def scalar_call(body, at, grid, in_specs, out_specs, out_shape, name, us, scratch=(), limit=24, aliases=None):
@@ -156,7 +156,7 @@
     def body(at):
         value = a_ref[at, :].astype(F32) + b_ref[at, :].astype(F32)
         value = x_ref[at, :].astype(F32) + (value + params_ref[0:1, :])
-        middle_ref[at, :] = value
+        middle_ref[at, :] = value.astype(BF16)
         xhat, _ = spread_of(value)
         normed_ref[at, :] = (xhat * params_ref[1:2, :] + params_ref[2:3, :]).astype(BF16)
 
@@ -171,15 +171,15 @@
         grid=(count,),
         in_specs=[image] * 3 + [pl.BlockSpec(params.shape, lambda i: (0, 0))],
         out_specs=[image] * 2,
-        out_shape=[pltpu.HBM(x.shape, F32), pltpu.HBM(x.shape, BF16)],
+        out_shape=[pltpu.HBM(x.shape, BF16)] * 2,
         compiler_params=pltpu.CompilerParams(vmem_limit_bytes=32 << 20),
-        cost_estimate=cost(2),
+        cost_estimate=cost(0.01),
         name="norm_two",
     )(x, share_a, share_b, params)
 
 
 def norm_back_kernel(second, at_ref, base_ref, v_ref, a_ref, b_ref, gain_ref, weight_ref, *refs):
-    grad_ref, *low_ref, sums_ref, scratch = refs
+    grad_ref, sums_ref, scratch = refs
     rows = v_ref.shape[0]
     totals = None
 
@@ -196,9 +196,8 @@
         grad = base + inverse * (scaled - first - xhat * other)
         parts = [jnp.sum(upstream * xhat, axis=0, keepdims=True), jnp.sum(upstream, axis=0, keepdims=True)]
         if second:
-            grad_ref[at, :] = grad
             low = grad.astype(BF16)
-            low_ref[0][at, :] = low
+            grad_ref[at, :] = low
             parts.append(jnp.sum(low.astype(F32), axis=0, keepdims=True))
         else:
             scratch[at, :] = grad
@@ -218,8 +217,8 @@
     shape = jax.ShapeDtypeStruct
     image = pl.BlockSpec((None, rows, model), lambda i, at: (i, 0, 0))
     sums = 3 if second else 2
-    outs = [image, image] if second else [pl.BlockSpec((None,) + own, lambda i, at: (i, 0, 0))]
-    shapes = [shape(v.shape, F32), shape(v.shape, BF16)] if second else [shape((count,) + own, F32)]
+    outs = [image] if second else [pl.BlockSpec((None,) + own, lambda i, at: (i, 0, 0))]
+    shapes = [shape(v.shape, BF16)] if second else [shape((count,) + own, F32)]
     return scalar_call(
         functools.partial(norm_back_kernel, second),
         at,
@@ -229,7 +228,7 @@
         outs + [pl.BlockSpec((None, sums, model), lambda i, at: (i, 0, 0))],
         shapes + [shape((count, sums, model), F32)],
         "norm_back",
-        2,
+        0.01,
         scratch=[pltpu.VMEM((8, 128) if second else (rows, model), F32)],
         limit=48,
     )(at, base, v, share_a, share_b, gain[None], weight)
@@ -270,7 +269,7 @@
         [full, full] if normal else full,
         [shape, shape] if normal else shape,
         "join",
-        2,
+        0.01,
     )(at, own, other, *(vectors or ()))
 
 
@@ -307,7 +306,7 @@
         [full, full, pl.BlockSpec((None, 1, 2 * width), lambda i, at: (i, 0, 0))],
         [shape((count, rows, 2 * width), BF16)] * 2 + [shape((count, 1, 2 * width), F32)],
         "seed",
-        2,
+        0.01,
         scratch=[pltpu.VMEM((8, 2 * width), F32)],
     )(at, own, other, weight)
 
@@ -335,94 +334,162 @@
         out_specs=vmem,
         out_shape=jax.ShapeDtypeStruct((len(arrays) * body + more, lanes), BF16),
         compiler_params=pltpu.CompilerParams(vmem_limit_bytes=16 << 20),
-        cost_estimate=cost(1),
+        cost_estimate=cost(0.01),
         name="stack",
     )(own_tail, *arrays)
 
 
-def unpack_kernel(n_row, at_ref, in_ref, merge_ref, expand_ref):
-    z = pl.program_id(0)
-    rows, run = merge_ref.shape
-    near = expand_ref.shape[0]
-    merge_ref[...] = in_ref[:rows, :]
-    for k in range(expand_ref.shape[1] // run):
-        expand_ref[:, k * run : (k + 1) * run] = in_ref[rows + k * near : rows + (k + 1) * near, :]
+def unpack_kernel(rows, at_ref, in_ref, out_ref):
+    run = in_ref.shape[1]
+    near = out_ref.shape[0]
+    for k in range(out_ref.shape[1] // run):
+        out_ref[:, k * run : (k + 1) * run] = in_ref[rows + k * near : rows + (k + 1) * near, :]
 
 
 def unpack(at, gathered, rows, near):
     n_row, total, run = gathered.shape
     wide = (total - rows) // near * run
+    return scalar_call(
+        functools.partial(unpack_kernel, rows),
+        at,
+        (n_row - 1,),
+        [pl.BlockSpec((None, total, run), lambda j, at: (at[1] ^ (j + 1), 0, 0))],
+        pl.BlockSpec((None, near, wide), lambda j, at: (j, 0, 0)),
+        jax.ShapeDtypeStruct((n_row - 1, near, wide), BF16),
+        "unpack",
+        0.01,
+    )(at, stay(gathered))
+
+
+def merge_kernel(at_ref, a_ref, g_ref, out_ref, weight_ref):
+    n_row, _, near = g_ref.shape
+
+    @pl.when(pl.program_id(0) == 0)
+    def _():
+        for z in range(n_row):
+            weight_ref[:, z * near : (z + 1) * near] = g_ref[z]
+
+    out_ref[...] = nn(a_ref[...], weight_ref[...]).astype(BF16)
+
+
+def merge(at, attended, gathered):
+    count, rows, width = attended.shape
+    n_row, _, near = gathered.shape
     shape = jax.ShapeDtypeStruct
     return scalar_call(
-        functools.partial(unpack_kernel, n_row),
-        at,
-        (n_row,),
-        [pl.BlockSpec((None, total, run), lambda j, at: (at[1] ^ j, 0, 0))],
+        merge_kernel,
+        at,
+        (count,),
         [
-            pl.BlockSpec((rows, run), lambda j, at: (0, at[1] ^ j)),
-            pl.BlockSpec((None, near, wide), lambda j, at: (jnp.maximum(j - 1, 0), 0, 0)),
+            pl.BlockSpec((None, rows, width), lambda i, at: (i, 0, 0)),
+            pl.BlockSpec((n_row, width, near), lambda i, at: (0, 0, 0), pipeline_mode=pl.Buffered(1)),
         ],
-        [shape((rows, n_row * run), BF16), shape((n_row - 1, near, wide), BF16)],
-        "unpack",
-        1,
-    )(at, stay(gathered))
+        [
+            pl.BlockSpec((None, rows, n_row * near), lambda i, at: (i, 0, 0)),
+            pl.BlockSpec((width, n_row * near), lambda i, at: (0, 0)),
+        ],
+        [shape((count, rows, n_row * near), BF16), shape((width, n_row * near), BF16)],
+        "merge",
+        0.01,
+    )(at, attended, stay(gathered))
+
+
+def product_kernel(a_ref, b_ref, out_ref):
+    total = None
+    for i in range(a_ref.shape[0]):
+        part = lax.dot_general(a_ref[i], b_ref[i], (((0,), (0,)), ((), ())), preferred_element_type=F32)
+        total = part if total is None else total + part
+    out_ref[...] = total.astype(BF16)
+
+
+def product(a, b, run, lanes=None, block=0, us=0.01):
+    count, rows, units = a.shape
+    lanes = b.shape[2] if lanes is None else lanes
+    run = run if run % 128 == 0 else units
+    return pl.pallas_call(
+        product_kernel,
+        grid=(units // run,),
+        in_specs=[
+            pl.BlockSpec((count, rows, run), lambda q: (0, 0, q)),
+            pl.BlockSpec((count, rows, lanes), lambda q: (0, 0, block), pipeline_mode=pl.Buffered(1)),
+        ],
+        out_specs=pl.BlockSpec((run, lanes), lambda q: (q, 0)),
+        out_shape=pltpu.HBM((units, lanes), BF16),
+        compiler_params=pltpu.CompilerParams(vmem_limit_bytes=40 << 20),
+        cost_estimate=cost(us),
+        name="product",
+    )(stay(a), stay(b))
 
 
 def pick_kernel(at_ref, in_ref, out_ref):
-    for q in range(out_ref.shape[0]):
-        out_ref[q] = in_ref[...]
+    out_ref[...] = in_ref[...]
 
 
 def others(at, gathered):
-    n_dp, n_row = lax.axis_size("dp"), gathered.shape[0]
+    n_row = gathered.shape[0]
     block = (None,) + gathered.shape[1:]
     return scalar_call(
         pick_kernel,
         at,
         (n_row - 1,),
         [pl.BlockSpec(block, lambda j, at: (at[1] ^ (j + 1), 0, 0))],
-        pl.BlockSpec((n_dp,) + block, lambda j, at: (0, j, 0, 0)),
-        jax.ShapeDtypeStruct((n_dp, n_row - 1) + gathered.shape[1:], gathered.dtype),
+        pl.BlockSpec(block, lambda j, at: (j, 0, 0)),
+        jax.ShapeDtypeStruct((n_row - 1,) + gathered.shape[1:], gathered.dtype),
         "others",
-        1,
+        0.01,
     )(at, stay(gathered))
 
 
-def place_kernel(at_ref, own_ref, rest_ref, out_ref, sems):
-    n_dp, others, run, near = rest_ref.shape
-    copies = [
-        pltpu.make_async_copy(
-            own_ref,
-            out_ref.at[:, pl.ds(pl.multiple_of(at_ref[1] * near, near), near)],
-            sems.at[0],
-        )
-    ]
-    for q in range(n_dp):
-        for j in range(others):
-            to = pl.ds(pl.multiple_of((at_ref[1] ^ (j + 1)) * near, near), near)
-            copies.append(
-                pltpu.make_async_copy(
-                    rest_ref.at[q, j], out_ref.at[q * run : (q + 1) * run, to], sems.at[len(copies)]
-                )
-            )
-    for copy in copies:
-        copy.start()
-    for copy in copies:
-        copy.wait()
-
-
-def place(at, own, rest):
-    n_dp, others, run, near = rest.shape
-    return pl.pallas_call(
-        place_kernel,
-        in_specs=[pl.BlockSpec(memory_space=pltpu.SMEM)] + [pl.BlockSpec(memory_space=pl.ANY)] * 2,
-        out_specs=pl.BlockSpec(memory_space=pltpu.VMEM),
-        out_shape=jax.ShapeDtypeStruct((n_dp * run, (others + 1) * near), own.dtype),
-        scratch_shapes=[pltpu.SemaphoreType.DMA((1 + n_dp * others,))],
-        compiler_params=pltpu.CompilerParams(vmem_limit_bytes=8 << 20),
-        cost_estimate=cost(1),
-        name="place",
-    )(at, stay(own), stay(rest))
+def down_back_kernel(n_dp, at_ref, seed_ref, slope_ref, own_ref, *refs):
+    rest, (grad_ref, sums_ref, weight_ref) = refs[:n_dp], refs[n_dp:]
+    others, _, near = rest[0].shape
+    for p in range(n_dp):
+
+        @pl.when(pl.program_id(0) == p)
+        def _(p=p):
+            for j in range(others + 1):
+                to = pl.ds(pl.multiple_of((at_ref[1] ^ j) * near, near), near)
+                weight_ref[:, to] = rest[p][j - 1] if j else own_ref[...]
+
+    sums = None
+    for i in range(seed_ref.shape[0]):
+        grad = (nt(seed_ref[i], weight_ref[...]) * slope_ref[i].astype(F32)).astype(BF16)
+        grad_ref[i] = grad
+        part = jnp.sum(grad.astype(F32), axis=0, keepdims=True)
+        sums = part if sums is None else sums + part
+    sums_ref[...] = sums
+
+
+def down_back(at, seed, slope, own, rest):
+    if rest[0].shape[1] % 128:
+        rest = [xor_order(lax.concatenate(rest, 1), 1, "dp")]
+    n_dp = len(rest)
+    others, run, near = rest[0].shape
+    count, rows, model = seed.shape
+    units = own.shape[0]
+    shape = jax.ShapeDtypeStruct
+    place = (lambda at, p: at[0] ^ p) if n_dp > 1 else (lambda at, p: 0)
+    block = pl.BlockSpec((count, rows, run), lambda p, at: (0, 0, place(at, p)))
+    return scalar_call(
+        functools.partial(down_back_kernel, n_dp),
+        at,
+        (n_dp,),
+        [
+            pl.BlockSpec(seed.shape, lambda p, at: (0, 0, 0), pipeline_mode=pl.Buffered(1)),
+            block,
+            pl.BlockSpec((run, near), lambda p, at: (place(at, p), 0)),
+        ]
+        + [pl.BlockSpec(a.shape, lambda p, at: (0, 0, 0), pipeline_mode=pl.Buffered(1)) for a in rest],
+        [
+            block,
+            pl.BlockSpec((1, run), lambda p, at: (0, place(at, p))),
+            pl.BlockSpec((run, model), lambda p, at: (place(at, p), 0)),
+        ],
+        [shape((count, rows, units), BF16), shape((1, units), F32), shape((units, model), BF16)],
+        "down_back",
+        0.01,
+        limit=40,
+    )(at, stay(seed), stay(slope), own, *[stay(a) for a in rest])
 
 
 def add_kernel(in_ref, out_ref):
@@ -439,7 +506,7 @@
         out_specs=pl.BlockSpec((step, lanes), lambda i: (i, 0)),
         out_shape=jax.ShapeDtypeStruct((rows, lanes), BF16),
         compiler_params=pltpu.CompilerParams(vmem_limit_bytes=24 << 20),
-        cost_estimate=cost(1),
+        cost_estimate=cost(0.01),
         name="add",
     )(blocks)
 
@@ -459,14 +526,14 @@
         pl.BlockSpec((None, rows, model // 2), lambda i, at: (i, 0, 0)),
         jax.ShapeDtypeStruct((count, rows, model // 2), value.dtype),
         "half",
-        1,
+        0.01,
     )(at, value)
 
 
 def close_kernel(at_ref, m_ref, a_ref, b_ref, bias_ref, out_ref):
     def body(at):
         share = a_ref[at, :].astype(F32) + b_ref[at, :].astype(F32)
-        out_ref[at, :] = (m_ref[at, :] + (share + bias_ref[...])).astype(BF16)
+        out_ref[at, :] = (m_ref[at, :].astype(F32) + (share + bias_ref[...])).astype(BF16)
 
     row_chunks(out_ref.shape[0], body)
 
@@ -483,7 +550,7 @@
         pl.BlockSpec((None, length, width), lambda i, at: (i, 0, 0)),
         jax.ShapeDtypeStruct((count, length, width), BF16),
         "close",
-        1,
+        0.01,
     )(at, middle, part, other, bias)
 
 
@@ -509,7 +576,7 @@
         pl.BlockSpec((3, rows, n_dp * run), lambda i, at: (0, 0, 0)),
         jax.ShapeDtypeStruct((3, rows, n_dp * run), F32),
         "spread",
-        1,
+        0.01,
     )(at, *parts)
 
 
@@ -659,7 +726,7 @@
             shape((count, 8, rows), F32),
         ],
         "mix",
-        2,
+        0.01,
         scratch=[pltpu.VMEM((rows, 128), F32)],
         aliases={5: 1, 6: 2} if more else {},
     )(at, normed, own, rest, bias, *more)
@@ -689,7 +756,7 @@
         ],
         [shape((count, rows, groups * three), BF16), shape((count, 1, three), F32)],
         "mix_back",
-        2,
+        0.01,
         scratch=[
             pltpu.VMEM((rows, lanes), BF16),
             pltpu.VMEM((rows, lanes), BF16),
@@ -720,7 +787,7 @@
         slope_ref[at, :] = (gate + 1.702 * act * (1.0 - gate)).astype(BF16)
 
 
-def up(p, at, normed, own, rest, bias, before):
+def up(p, at, normed, own, rest, bias, before, us):
     run = rest.shape[2]
     units = own.shape[1]
     count, rows, model = normed.shape
@@ -741,7 +808,7 @@
         [block, block, pl.BlockSpec((model, run), lambda i, at: (0, place(at)))],
         [shape((count, rows, units), BF16)] * 2 + [shape((model, units), BF16)],
         "expand",
-        1,
+        us,
         limit=32,
         aliases={5: 0, 6: 1, 7: 2} if before else {},
     )(at, normed, own, rest, bias, *before)
@@ -855,16 +922,12 @@
 
     if joined:
         attended, gathered = lax.optimization_barrier((attended, gathered))
-        merge_full, expand_rows = unpack(at, gathered, width, expand_weight.shape[0])
-        expand_rest = dp_parts(expand_rows)
+        expand_rest = dp_parts(unpack(at, gathered, width, expand_weight.shape[0]))
+        attended, expand_rest[0] = lax.optimization_barrier((attended, expand_rest[0]))
+        merge_part, merge_full = merge(at, attended, gathered)
     else:
-        expand_rest = dp_parts(others(at, expand_rows)[0])
-    shrink_rows = others(at, shrink_rows)
-    attended, expand_rest[1:3], shrink_rows = lax.optimization_barrier(
-        (attended, expand_rest[1:3], shrink_rows)
-    )
-    shrink_all = lax.all_to_all(shrink_rows, "dp", 0, 0)
-    merge_part = jnp.einsum("itf,fd->itd", attended, merge_full, preferred_element_type=F32)
+        expand_rest = dp_parts(others(at, expand_rows))
+        merge_part = jnp.einsum("itf,fd->itd", attended, merge_full, preferred_element_type=F32)
     share_a, share_b = col_shares(merge_part.astype(BF16))
     middle, normed_two = norm_of_sum(
         x, share_a, share_b, jnp.stack([merge_bias_full, gain_two, shift_two])
@@ -873,8 +936,13 @@
     if (units // n_dp) % 128:
         expand_rest = [xor_order(lax.concatenate(expand_rest, 2), 2, "dp")]
     made = ()
-    for p, piece in enumerate(expand_rest):
-        made = up(p, at, normed_two, expand_weight, piece, expand_bias.astype(F32)[None], made)
+    for p in range(len(expand_rest)):
+        if p == min(1, len(expand_rest) - 1):
+            made, shrink_rows = lax.optimization_barrier((made, shrink_rows))
+            shrink_rows = others(at, shrink_rows)
+            shrink_all = dp_parts(shrink_rows)
+            expand_rest[1:], _ = lax.optimization_barrier((expand_rest[1:], shrink_rows))
+        made = up(p, at, normed_two, expand_weight, expand_rest[p], expand_bias.astype(F32)[None], made, 1 if p == 1 else 0.01)
     activated, slope, expand_full = made
 
     if pair:
@@ -884,23 +952,18 @@
         seed_low = (cot.astype(F32) * slot_weight[:, None, None]).astype(BF16)
         seed_sums = jnp.sum(seed_low.astype(F32), axis=1, keepdims=True)
 
-    shrink_grad = jnp.einsum("ith,itd->hd", activated, seed_low, preferred_element_type=F32)
-    shrink_grad = shrink_grad.astype(BF16)
+    shrink_grad = product(activated, seed_low, units // n_dp, us=0.01)
+    shrink_grad, seed_low, shrink_all = lax.optimization_barrier((shrink_grad, seed_low, shrink_all))
+    hidden_grad, hidden_sums, shrink_full = down_back(at, seed_low, slope, shrink_weight, shrink_all)
+    hidden_grad, shrink_grad = lax.optimization_barrier((hidden_grad, shrink_grad))
     shrink_sum = scatter_row(shrink_grad, 1)
-    shrink_grad, seed_low, shrink_all = lax.optimization_barrier((shrink_grad, seed_low, shrink_all))
-    shrink_full = place(at, shrink_weight, shrink_all)
-    act_grad = jnp.einsum("itd,hd->ith", seed_low, shrink_full, preferred_element_type=F32)
-    hidden_grad = (act_grad * slope.astype(F32)).astype(BF16)
-    hidden_sums = jnp.sum(hidden_grad.astype(F32), axis=(0, 1))
-    expand_grad = jnp.einsum("ith,itd->hd", hidden_grad, normed_two, preferred_element_type=F32)
-    expand_grad, hidden_grad, hidden_sums = lax.optimization_barrier(
-        (expand_grad.astype(BF16), hidden_grad, hidden_sums)
-    )
+    expand_grad = product(hidden_grad, normed_two, units // n_dp)
+    expand_grad, hidden_grad = lax.optimization_barrier((expand_grad, hidden_grad))
     expand_sum = dp_sum(expand_grad)
     norm_part = jnp.einsum("ith,dh->itd", hidden_grad, expand_full, preferred_element_type=F32)
     norm_part = norm_part.astype(BF16)
     share_a, share_b = col_shares(norm_part)
-    middle_grad, branch_grad, sums_two = norm_back(
+    branch_grad, sums_two = norm_back(
         at, cot, middle, share_a, share_b, gain_two, slot_weight, None
     )
 
@@ -920,13 +983,7 @@
             )
             expand_sum = scatter_row(expand_sum, 1)
         if g == 0:
-            attended_grad, merge_sum, heads_in[1:2] = lax.optimization_barrier(
-                (attended_grad, merge_sum, heads_in[1:2])
-            )
-            both = jnp.concatenate(
-                [shrink_sum.reshape(n_dp, part, -1), merge_sum.reshape(n_dp, run, -1)], axis=1
-            )
-            both = dp_sum(both.reshape(units + width, -1))
+            attended_grad, heads_in[1:2] = lax.optimization_barrier((attended_grad, heads_in[1:2]))
         mixed_grad, mixed_sums[g] = mix_back(
             length, g, groups, at, mixed[g], attended_grad, exact[g], stats[g], mixed_grad
         )
@@ -935,6 +992,13 @@
         if g:
             attended_grad, heads_grads[g] = lax.optimization_barrier((attended_grad, heads_grads[g]))
             heads_in[g] = peer(heads_grads[g], "dp", g)
+    heads_grads[0], heads_in[1:], shrink_sum, merge_sum = lax.optimization_barrier(
+        (heads_grads[0], heads_in[1:], shrink_sum, merge_sum)
+    )
+    both = jnp.concatenate(
+        [shrink_sum.reshape(n_dp, part, -1), merge_sum.reshape(n_dp, run, -1)], axis=1
+    )
+    both = dp_sum(both.reshape(units + width, -1))
     if not split:
         whole = xor_order(heads_grads[0].reshape(model, 3, width), 2, "dp")
         heads_grads = [cut(whole, 2, n_dp, p).reshape(model, 3 * run) for p in range(n_dp)]
@@ -944,18 +1008,17 @@
         heads_sum = heads_sum + piece.astype(F32)
     heads_sum = heads_sum.astype(BF16)
     heads_sum = sum_parts([cut(heads_sum, 0, n_row, j) for j in range(n_row)], "row", at[1])
-    mixed_grad, activated, both, expand_sum = lax.optimization_barrier(
-        (mixed_grad, activated, both, expand_sum)
-    )
     first_part = jnp.einsum("itf,df->itd", mixed_grad, heads_full, preferred_element_type=F32)
-    share_a, share_b = col_shares(first_part.astype(BF16))
+    first_part = first_part.astype(BF16)
+    first_part, activated = lax.optimization_barrier((first_part, activated))
+    share_a, share_b = col_shares(first_part)
     packed = dp_all(jnp.concatenate([both, expand_sum]))
     shrink_part = jnp.einsum("ith,hd->itd", activated, shrink_full, preferred_element_type=F32).astype(BF16)
     shrink_part, heads_sum = lax.optimization_barrier((shrink_part, heads_sum))
     own = (length, width) if pair else (rows, model)
     place_of = at if pair else at * jnp.array([1, 1, 0], jnp.int32)
     input_grad, sums_one = norm_back(
-        place_of, middle_grad, x, share_a, share_b, gain_one, slot_weight, own
+        place_of, branch_grad, x, share_a, share_b, gain_one, slot_weight, own
     )
 
     if pair:
@@ -963,7 +1026,7 @@
         output = close(at, middle, shrink_part, other, shrink_bias.astype(F32)[None], length)
     else:
         branch_two = col_own(lax.psum(shrink_part, "col").astype(F32), 2)
-        output = (col_own(middle, 2) + (branch_two + shrink_bias.astype(F32))).astype(BF16)[:, :length]
+        output = (col_own(middle, 2).astype(F32) + (branch_two + shrink_bias.astype(F32))).astype(BF16)[:, :length]
         input_grad = col_own(input_grad, 2)[:, :length]
     packed, sums_one = lax.optimization_barrier((packed, sums_one))
     heads_out = dp_parts(heads_sum)
@@ -979,7 +1042,7 @@
     heads_bias_grad = mixed_sums[0::2]
     if split:
         heads_bias_grad = xor_order(heads_bias_grad, 1, "dp")
-    small = sum_all(jnp.concatenate([model_sums.ravel(), heads_bias_grad.ravel(), hidden_sums]))
+    small = sum_all(jnp.concatenate([model_sums.ravel(), heads_bias_grad.ravel(), hidden_sums[0]]))
     shrink_sum = packed[:, :part].reshape(units, -1).astype(F32)
     merge_sum = packed[:, part : part + run].reshape(width, -1).astype(F32)
     expand_sum = packed[:, part + run :].reshape(units, -1).T.astype(F32)

time: 401 us -> 392 us (0.978)
  Pallas kernels: 133 us -> 163 us
  matrix products: 72.8 us -> 45.2 us
  waiting for transfers between devices: 70 us -> 60.1 us
  local copies, waits for them, and re-layouts: 30.3 us -> 38.7 us
  other arithmetic: 20.8 us -> 12.6 us
    pallas_call x2 -> x5, Pallas kernels: 8.09 us -> 42.1 us  [the longest x2 21.5 us: product(): pl.pallas_call(product_kernel, grid=(units // run,), in_specs=[pl.BlockSp...]
    dot_general x4 -> x0, matrix products: 30.4 us -> none  [the longest x1 9.85 us: shards(): jnp.einsum('ith,itd->hd', hidden_grad, normed_two, preferred_element_type...]
    reduce_scatter x3, waiting for transfers between devices: 0.02 us -> 14.5 us  [scatter_row(): lax.psum_scatter(value, 'row', scatter_dimension=model_dim, tiled=True)]
    all_gather x1, waiting for transfers between devices: 21.1 us -> 7.97 us  [shards(): shrink_rows = lax.all_gather(shrink_send, 'row')]
    reduce_sum x1 -> x0, other arithmetic: 8.26 us -> none  [shards(): hidden_sums = jnp.sum(hidden_grad.astype(F32), axis=(0, 1))]
    unnamed x110 -> x106, local copies, waits for them, and re-layouts: 12.7 us -> 20.4 us
    all_to_all x2, waiting for transfers between devices: 12.7 us -> 6.01 us  [dp_sum(): return add(lax.all_to_all(blocks, 'dp', 0, 0))]
    all_to_all x1 -> x0, starting transfers between devices: 4.65 us -> none  [shards(): shrink_all = lax.all_to_all(shrink_rows, 'dp', 0, 0)]
  transfers between devices with their start and end apart: 39 -> 41, of which waited for: 10 -> 14; matrix products, arithmetic and copies ran while one was open for 26% -> 19% of each run, Pallas kernels for 34% -> 37%
where the time goes in v1:
time: 392 us; the launch traced here: 388 us
  Pallas kernels  163 us (42%)
  waiting for transfers between devices  60.1 us (15%)
  starting transfers between devices  53 us (14%)
  matrix products  45.2 us (12%)
  local copies, waits for them, and re-layouts  38.7 us (10%)
  between operations  14.8 us (4%)
  other arithmetic  12.6 us (3%)
    ppermute x33, starting transfers between devices, peer(): return lax.ppermute(value, axis, [(i, i ^ p) for i in range(n)])  39.1 us
    pallas_call x4, Pallas kernels, mix_back(): scalar_call(functools.partial(mix_back_kernel, length), at, (count,), [pl...  30.8 us
    ppermute x33, waiting for transfers between devices, peer(): return lax.ppermute(value, axis, [(i, i ^ p) for i in range(n)])  25.6 us
    pallas_call x4, Pallas kernels, mix(): scalar_call(functools.partial(mix_kernel, length, n_row), at, (count,), [...  25 us
    pallas_call x4, Pallas kernels, up(): scalar_call(functools.partial(up_kernel, model // own.shape[0]), at, (cou...  22 us
    pallas_call x2, Pallas kernels, product(): pl.pallas_call(product_kernel, grid=(units // run,), in_specs=[pl.BlockSp...  21.5 us
    unnamed x106, local copies, waits for them, and re-layouts  20.4 us
    pallas_call x2, Pallas kernels, norm_back(): scalar_call(functools.partial(norm_back_kernel, second), at, (count,), [i...  15.4 us
  transfers between devices with their start and end apart: 41, of which 14 were waited for; matrix products, arithmetic and copies ran while one was open for 19% of the time, Pallas kernels for 37%

profile of v1, /device:TPU:0, one launch (start us, length us, event | category | flops | bytes accessed | tf_op | source)
XLA Modules:
  0.0 387.7 jit_solution(1143678561208944254)
XLA Ops:
  13.2 2.6 collective-permute-start
  15.8 2.6 collective-permute-start.1
  22.9 3.6 join.1
  26.5 7.0 %collective-permute-done.1.refs_1_ = bf16[784,128]{1,0:T(8,128)(2,1)} collective-permute-done((bf16[784,128]{1,0:T(8,128)(2,1)}, bf16[784,128]{1,0:T(8,128)(2,1)}, u32[]{:S(2)}, u32[]{:S(2)}) %collective-permute-start.1) | collective-permute-done | bytes 200736 | tf_op jit(solution)/shard_map/ppermute | solution.py:21
  40.8 6.2 %mix.4 = (bf16[2,592,384]{2,1,0:T(8,128)(2,1)}, bf16[2,592,512]{2,1,0:T(8,128)(2,1)}, bf16[1024,1536]{1,0:T(8,128)(2,1)}, f32[2,592,128]{2,1,0:T(8,128)}, f32[2,8,592]{2,1,0:T(8,128)}) custom-call(s32[3]{0:T(128)S(1)} %pad_add_fusion.at_ref, bf16[2,592,1024]{2,1,0:T(8,128)(2,1)S(1)} %copy-done.2, bf16[3,256,512]{2,1,0:T(8,128)(2,1)S(1)} %bitcast.106, ...), custom_call_target="tpu_custom_call" | custom-call | flops 10000000 | bytes 1024 | tf_op jit(solution)/shard_map/mix/pallas_call | solution.py:703
  47.0 5.3 %collective-permute-done.6.rest_ref = bf16[2320,128]{1,0:T(8,128)(2,1)S(1)} collective-permute-done((bf16[2320,128]{1,0:T(8,128)(2,1)S(1)}, bf16[2320,128]{1,0:T(8,128)(2,1)S(1)}, u32[]{:S(2)}, u32[]{:S(2)}) %collective-permute-start.6) | collective-permute-done | bytes 593952 | tf_op jit(solution)/shard_map/ppermute | solution.py:21
  52.3 6.2 %mix.5 = (bf16[2,592,384]{2,1,0:T(8,128)(2,1)}, bf16[2,592,512]{2,1,0:T(8,128)(2,1)}, bf16[1024,1536]{1,0:T(8,128)(2,1)}, f32[2,592,128]{2,1,0:T(8,128)}, f32[2,8,592]{2,1,0:T(8,128)}) custom-call(s32[3]{0:T(128)S(1)} %pad_add_fusion.at_ref, bf16[2,592,1024]{2,1,0:T(8,128)(2,1)S(1)} %copy-done.2, ...), custom_call_target="tpu_custom_call", output_to_operand_aliasing={{1}: (5, {}), {2}: (6, {})} | custom-call | flops 10000000 | bytes 1024 | tf_op jit(solution)/shard_map/mix/pallas_call | solution.py:703
  58.6 5.4 %collective-permute-done.5.rest_ref = bf16[2320,128]{1,0:T(8,128)(2,1)S(1)} collective-permute-done((bf16[2320,128]{1,0:T(8,128)(2,1)S(1)}, bf16[2320,128]{1,0:T(8,128)(2,1)S(1)}, u32[]{:S(2)}, u32[]{:S(2)}) %collective-permute-start.5) | collective-permute-done | bytes 593952 | tf_op jit(solution)/shard_map/ppermute | solution.py:21
  63.9 6.2 %mix.6 = (bf16[2,592,384]{2,1,0:T(8,128)(2,1)}, bf16[2,592,512]{2,1,0:T(8,128)(2,1)}, bf16[1024,1536]{1,0:T(8,128)(2,1)}, f32[2,592,128]{2,1,0:T(8,128)}, f32[2,8,592]{2,1,0:T(8,128)}) custom-call(s32[3]{0:T(128)S(1)} %pad_add_fusion.at_ref, bf16[2,592,1024]{2,1,0:T(8,128)(2,1)S(1)} %copy-done.2, ...), custom_call_target="tpu_custom_call", output_to_operand_aliasing={{1}: (5, {}), {2}: (6, {})} | custom-call | flops 10000000 | bytes 1024 | tf_op jit(solution)/shard_map/mix/pallas_call | solution.py:703
  70.2 6.3 %mix.7 = (bf16[2,592,384]{2,1,0:T(8,128)(2,1)}, bf16[2,592,512]{2,1,0:T(8,128)(2,1)}, bf16[1024,1536]{1,0:T(8,128)(2,1)}, f32[2,592,128]{2,1,0:T(8,128)}, f32[2,8,592]{2,1,0:T(8,128)}) custom-call(s32[3]{0:T(128)S(1)} %pad_add_fusion.at_ref, bf16[2,592,1024]{2,1,0:T(8,128)(2,1)S(1)} %copy-done.2, ...), custom_call_target="tpu_custom_call", output_to_operand_aliasing={{1}: (5, {}), {2}: (6, {})} | custom-call | flops 10000000 | bytes 1024 | tf_op jit(solution)/shard_map/mix/pallas_call | solution.py:703
  77.3 5.9 %all-gather.5.cloned.1.call-done = bf16[4096,256]{1,0:T(8,128)(2,1)} async-done(((bf16[1024,256]{1,0:T(8,128)(2,1)}), bf16[4096,256]{1,0:T(8,128)(2,1)}) %all-gather.5.cloned.1.call-update) | async-done | bytes 2097168 | tf_op jit(solution)/shard_map/all_gather | solution.py:901
  83.2 3.6 unpack.1.rest_ref
  86.9 4.6 %merge.1 = (bf16[2,592,1024]{2,1,0:T(8,128)(2,1)}, bf16[512,1024]{1,0:T(8,128)(2,1)}) custom-call(s32[3]{0:T(128)S(1)} %pad_add_fusion.at_ref, bf16[2,592,512]{2,1,0:T(8,128)(2,1)S(1)} %copy-done.4, bf16[4,1024,256]{2,1,0:T(8,128)(2,1)} %bitcast.116), custom_call_target="tpu_custom_call" | custom-call | flops 10000000 | bytes 1024 | tf_op jit(solution)/shard_map/merge/pallas_call | solution.py:379
  96.3 1.8 copy-done.9
  98.1 1.7 copy-done.15
  99.8 3.5 norm_two.1
  105.0 5.5 %expand.4 = (bf16[2,592,2048]{2,1,0:T(8,128)(2,1)}, bf16[2,592,2048]{2,1,0:T(8,128)(2,1)}, bf16[1024,2048]{1,0:T(8,128)(2,1)}) custom-call(s32[3]{0:T(128)S(1)} %pad_add_fusion.at_ref, bf16[2,592,1024]{2,1,0:T(8,128)(2,1)S(1)} %copy-done, bf16[256,2048]{1,0:T(8,128)(2,1)S(1)} %copy-done.6, bf16[3,256,512]{2,1,0:T(8,128)(2,1)} %unpack.1.rest_ref, ...), custom_call_target="tpu_custom_call" | custom-call | flops 10000000 | bytes 1024 | tf_op jit(solution)/shard_map/expand/pallas_call | solution.py:797
  110.5 8.0 %all-gather.7.cloned.1.call-done = bf16[2048,256]{1,0:T(8,128)(2,1)} async-done(((bf16[512,256]{1,0:T(8,128)(2,1)}), bf16[2048,256]{1,0:T(8,128)(2,1)}) %all-gather.7.cloned.1.call-update) | async-done | bytes 1048592 | tf_op jit(solution)/shard_map/all_gather | solution.py:905
  118.5 3.4 others.1.refs_0_
  124.8 5.1 %collective-permute-done.10.rest_ref = bf16[3,256,512]{2,1,0:T(8,128)(2,1)} collective-permute-done((bf16[3,256,512]{2,1,0:T(8,128)(2,1)}, bf16[3,256,512]{2,1,0:T(8,128)(2,1)}, u32[]{:S(2)}, u32[]{:S(2)}) %collective-permute-start.10) | collective-permute-done | bytes 786464 | tf_op jit(solution)/shard_map/ppermute | solution.py:21
  129.9 2.4 collective-permute-start.14
  133.2 4.5 %seed.1 = (bf16[2,592,1024]{2,1,0:T(8,128)(2,1)}, bf16[2,592,1024]{2,1,0:T(8,128)(2,1)}, f32[2,1,1024]{2,1,0:T(1,128)}) custom-call(s32[3]{0:T(128)S(1)} %pad_add_fusion.at_ref, bf16[2,592,512]{2,1,0:T(8,128)(2,1)} %pad.9.own_ref, bf16[2,592,512]{2,1,0:T(8,128)(2,1)} %collective-permute-done.8.other_ref, f32[2]{0:T(128)S(1)} %multiply_reduce_fusion.weight_ref), custom_call_target="tpu_custom_call" | custom-call | flops 10000000 | bytes 1024 | tf_op jit(solution)/shard_map/seed/pallas_call | solution.py:301
  137.7 5.5 %expand.5 = (bf16[2,592,2048]{2,1,0:T(8,128)(2,1)}, bf16[2,592,2048]{2,1,0:T(8,128)(2,1)}, bf16[1024,2048]{1,0:T(8,128)(2,1)}) custom-call(s32[3]{0:T(128)S(1)} %pad_add_fusion.at_ref, bf16[2,592,1024]{2,1,0:T(8,128)(2,1)S(1)} %copy-done.1, bf16[256,2048]{1,0:T(8,128)(2,1)S(1)} %copy-done.6, ...), custom_call_target="tpu_custom_call", output_to_operand_aliasing={{0}: (5, {}), {1}: (6, {}), {2}: (7, {})} | custom-call | flops 1000000000 | bytes 1024 | tf_op jit(solution)/shard_map/expand/pallas_call | solution.py:797
  143.2 5.5 %expand.6 = (bf16[2,592,2048]{2,1,0:T(8,128)(2,1)}, bf16[2,592,2048]{2,1,0:T(8,128)(2,1)}, bf16[1024,2048]{1,0:T(8,128)(2,1)}) custom-call(s32[3]{0:T(128)S(1)} %pad_add_fusion.at_ref, bf16[2,592,1024]{2,1,0:T(8,128)(2,1)S(1)} %copy-done.1, bf16[256,2048]{1,0:T(8,128)(2,1)S(1)} %copy-done.6, ...), custom_call_target="tpu_custom_call", output_to_operand_aliasing={{0}: (5, {}), {1}: (6, {}), {2}: (7, {})} | custom-call | flops 10000000 | bytes 1024 | tf_op jit(solution)/shard_map/expand/pallas_call | solution.py:797
  148.7 5.5 %expand.7 = (bf16[2,592,2048]{2,1,0:T(8,128)(2,1)}, bf16[2,592,2048]{2,1,0:T(8,128)(2,1)}, bf16[1024,2048]{1,0:T(8,128)(2,1)}) custom-call(s32[3]{0:T(128)S(1)} %pad_add_fusion.at_ref, bf16[2,592,1024]{2,1,0:T(8,128)(2,1)S(1)} %copy-done.1, bf16[256,2048]{1,0:T(8,128)(2,1)S(1)} %copy-done.6, ...), custom_call_target="tpu_custom_call", output_to_operand_aliasing={{0}: (5, {}), {1}: (6, {}), {2}: (7, {})} | custom-call | flops 10000000 | bytes 1024 | tf_op jit(solution)/shard_map/expand/pallas_call | solution.py:797
  154.2 10.5 %product.2 = bf16[2048,1024]{1,0:T(8,128)(2,1)} custom-call(bf16[2,592,2048]{2,1,0:T(8,128)(2,1)} %get-tuple-element.218.a_ref, bf16[2,592,1024]{2,1,0:T(8,128)(2,1)} %get-tuple-element.180.b_ref.seed_ref), custom_call_target="tpu_custom_call" | custom-call | flops 10000000 | bytes 1024 | tf_op jit(solution)/shard_map/product/pallas_call | solution.py:409
  164.9 12.3 %down_back.1 = (bf16[2,592,2048]{2,1,0:T(8,128)(2,1)}, f32[1,2048]{1,0:T(1,128)}, bf16[2048,1024]{1,0:T(8,128)(2,1)}) custom-call(s32[3]{0:T(128)S(1)} %pad_add_fusion.at_ref, bf16[2,592,1024]{2,1,0:T(8,128)(2,1)} %get-tuple-element.180.b_ref.seed_ref, bf16[2,592,2048]{2,1,0:T(8,128)(2,1)} %get-tuple-element.181.slope_ref, bf16[2048,256]{1,0:T(8,128)(2,1)S(1)} %copy-done.20, ...), custom_call_target="tpu_custom_call" | custom-call | flops 10000000 | bytes 1024 | tf_op jit(solution)/shard_map/down_back/pallas_call | solution.py:473
  177.3 11.0 %product.3 = bf16[2048,1024]{1,0:T(8,128)(2,1)} custom-call(bf16[2,592,2048]{2,1,0:T(8,128)(2,1)} %get-tuple-element.189.a_ref, bf16[2,592,1024]{2,1,0:T(8,128)(2,1)} %get-tuple-element.159.n_ref.b_ref), custom_call_target="tpu_custom_call" | custom-call | flops 10000000 | bytes 1024 | tf_op jit(solution)/shard_map/product/pallas_call | solution.py:409
  188.3 7.0 %fusion.9.a_ref = bf16[2,592,1024]{2,1,0:T(8,128)(2,1)} fusion(bf16[2,592,2048]{2,1,0:T(8,128)(2,1)S(1)} %copy-done.29, bf16[1024,2048]{1,0:T(8,128)(2,1)S(1)} %copy-done.28), kind=kOutput, calls=%fused_computation.8 | convolution fusion | flops 4967268352 | bytes 11468800 | tf_op jit(solution)/shard_map/ith,dh->itd/dot_general | solution.py:963
  195.3 5.1 %all-to-all-start = ((bf16[4,512,1024]{2,1,0:T(8,128)(2,1)}), bf16[4,512,1024]{2,1,0:T(8,128)(2,1)}, u32[]{:S(2)}, u32[]{:S(2)}) async-start(bf16[4,512,1024]{2,1,0:T(8,128)(2,1)} %bitcast.114), calls=%async_computation | async-start | bytes 8388608 | tf_op jit(solution)/shard_map/all_to_all | solution.py:66
  202.2 7.9 %norm_back.2 = (bf16[2,592,1024]{2,1,0:T(8,128)(2,1)}, f32[2,3,1024]{2,1,0:T(4,128)}) custom-call(s32[3]{0:T(128)S(1)} %pad_add_fusion.at_ref, bf16[2,592,1024]{2,1,0:T(8,128)(2,1)S(1)} %copy-done.18, bf16[2,592,1024]{2,1,0:T(8,128)(2,1)S(1)} %copy-done.11, bf16[2,592,1024]{2,1,0:T(8,128)(2,1)} %fusion.9.a_ref, ...), custom_call_target="tpu_custom_call" | custom-call | flops 10000000 | bytes 1024 | tf_op jit(solution)/shard_map/norm_back/pallas_call | solution.py:222
  210.2 4.3 %convolution_convert_fusion.up_ref = bf16[2,592,512]{2,1,0:T(8,128)(2,1)} fusion(bf16[2,592,1024]{2,1,0:T(8,128)(2,1)} %get-tuple-element.191.base_ref, bf16[512,1024]{1,0:T(8,128)(2,1)S(1)} %copy-done.49), kind=kOutput, calls=%fused_computation.15 | convolution fusion | flops 1242120192 | bytes 4685824 | tf_op jit(solution)/shard_map/itd,fd->itf/dot_general | solution.py:970
  214.5 2.5 bitcast_convert_fusion
  217.1 7.8 %mix_back.4 = (bf16[2,592,1536]{2,1,0:T(8,128)(2,1)}, f32[2,1,384]{2,1,0:T(1,128)}) custom-call(s32[3]{0:T(128)S(1)} %pad_add_fusion.at_ref, bf16[2,592,384]{2,1,0:T(8,128)(2,1)} %get-tuple-element.194.m_ref, bf16[2,592,512]{2,1,0:T(8,128)(2,1)} %convolution_convert_fusion.up_ref, f32[2,592,128]{2,1,0:T(8,128)} %get-tuple-element.195.exact_ref, ...), custom_call_target="tpu_custom_call" | custom-call | flops 10000000 | bytes 1024 | tf_op jit(solution)/shard_map/mix_back/pallas_call | solution.py:742
  224.9 3.7 bitcast_convert_fusion.4
  228.5 7.6 %mix_back.5 = (bf16[2,592,1536]{2,1,0:T(8,128)(2,1)}, f32[2,1,384]{2,1,0:T(1,128)}) custom-call(s32[3]{0:T(128)S(1)} %pad_add_fusion.at_ref, bf16[2,592,384]{2,1,0:T(8,128)(2,1)} %get-tuple-element.199.m_ref, bf16[2,592,512]{2,1,0:T(8,128)(2,1)} %convolution_convert_fusion.up_ref, ...), custom_call_target="tpu_custom_call", output_to_operand_aliasing={{0}: (5, {})} | custom-call | flops 10000000 | bytes 1024 | tf_op jit(solution)/shard_map/mix_back/pallas_call | solution.py:742
  236.1 3.6 bitcast_convert_fusion.3
  239.7 2.0 collective-permute-start.16
  243.2 6.0 %all-to-all-done.in_ref = bf16[4,512,1024]{2,1,0:T(8,128)(2,1)} async-done(((bf16[4,512,1024]{2,1,0:T(8,128)(2,1)}), bf16[4,512,1024]{2,1,0:T(8,128)(2,1)}, u32[]{:S(2)}, u32[]{:S(2)}) %all-to-all-start) | async-done | bytes 4194336 | tf_op jit(solution)/shard_map/all_to_all | solution.py:66
  249.2 4.2 %add.144 = bf16[512,1024]{1,0:T(8,128)(2,1)} custom-call(bf16[4,512,1024]{2,1,0:T(8,128)(2,1)} %all-to-all-done.in_ref), custom_call_target="tpu_custom_call" | custom-call | flops 10000000 | bytes 1024 | tf_op jit(solution)/shard_map/add/pallas_call | solution.py:502
  253.4 7.6 %mix_back.6 = (bf16[2,592,1536]{2,1,0:T(8,128)(2,1)}, f32[2,1,384]{2,1,0:T(1,128)}) custom-call(s32[3]{0:T(128)S(1)} %pad_add_fusion.at_ref, bf16[2,592,384]{2,1,0:T(8,128)(2,1)} %get-tuple-element.207.m_ref, bf16[2,592,512]{2,1,0:T(8,128)(2,1)} %convolution_convert_fusion.up_ref, ...), custom_call_target="tpu_custom_call", output_to_operand_aliasing={{0}: (5, {})} | custom-call | flops 10000000 | bytes 1024 | tf_op jit(solution)/shard_map/mix_back/pallas_call | solution.py:742
  261.0 3.6 bitcast_convert_fusion.2
  265.6 7.8 %mix_back.7 = (bf16[2,592,1536]{2,1,0:T(8,128)(2,1)}, f32[2,1,384]{2,1,0:T(1,128)}) custom-call(s32[3]{0:T(128)S(1)} %pad_add_fusion.at_ref, bf16[2,592,384]{2,1,0:T(8,128)(2,1)} %get-tuple-element.156.m_ref, bf16[2,592,512]{2,1,0:T(8,128)(2,1)} %convolution_convert_fusion.up_ref, ...), custom_call_target="tpu_custom_call", output_to_operand_aliasing={{0}: (5, {})} | custom-call | flops 10000000 | bytes 1024 | tf_op jit(solution)/shard_map/mix_back/pallas_call | solution.py:742
  273.4 3.7 bitcast_convert_fusion.1
  277.2 5.3 %reduce-scatter.6.cloned.1.call-done = bf16[512,256]{1,0:T(8,128)(2,1)} async-done(((bf16[512,1024]{1,0:T(8,128)(2,1)}), bf16[512,256]{1,0:T(8,128)(2,1)}) %reduce-scatter.6.cloned.1.call-update) | async-done | bytes 262160 | tf_op jit(solution)/shard_map/reduce_scatter | solution.py:75
  282.5 1.8 collective-permute-done.18
  284.2 2.1 pad_maximum_fusion
  286.3 3.5 all-to-all-start.1
  289.9 8.5 %fusion.6.a_ref = bf16[2,592,1024]{2,1,0:T(8,128)(2,1)} fusion(bf16[2,592,1536]{2,1,0:T(8,128)(2,1)} %get-tuple-element.216, bf16[1024,1536]{1,0:T(8,128)(2,1)} %get-tuple-element.217), kind=kOutput, calls=%fused_computation.7 | convolution fusion | flops 3725754368 | bytes 9207808 | tf_op jit(solution)/shard_map/itf,df->itd/dot_general | solution.py:1011
  298.4 1.8 add_convert_fusion
  302.4 2.0 collective-permute-start.20
  306.0 9.2 %reduce-scatter.8.cloned.1.call-done = bf16[512,256]{1,0:T(8,128)(2,1)} async-done(((bf16[512,1024]{1,0:T(8,128)(2,1)}), bf16[512,256]{1,0:T(8,128)(2,1)}) %reduce-scatter.8.cloned.1.call-update) | async-done | bytes 262160 | tf_op jit(solution)/shard_map/reduce_scatter | solution.py:75
  317.8 4.8 %all-to-all-start.2 = ((bf16[4,1152,256]{2,1,0:T(8,128)(2,1)}), bf16[4,1152,256]{2,1,0:T(8,128)(2,1)}, u32[]{:S(2)}, u32[]{:S(2)}) async-start(bf16[4,1152,256]{2,1,0:T(8,128)(2,1)} %broadcast_in_dim.42), calls=%async_computation.5 | async-start | bytes 4718592 | tf_op jit(solution)/shard_map/all_to_all | solution.py:71
  322.6 8.3 %fusion.12.in_ref.a_ref = bf16[2,592,1024]{2,1,0:T(8,128)(2,1)S(1)} fusion(bf16[2,592,2048]{2,1,0:T(8,128)(2,1)} %get-tuple-element.218.a_ref, bf16[2048,1024]{1,0:T(8,128)(2,1)} %get-tuple-element.219), kind=kOutput, calls=%fused_computation.9 | convolution fusion | flops 4967268352 | bytes 11468800 | tf_op jit(solution)/shard_map/ith,hd->itd/dot_general | solution.py:1016
  332.4 1.7 half.1
  335.8 2.1 collective-permute-start.24
  341.2 3.6 close.1
  344.7 3.2 copy.66
  347.9 7.5 %norm_back.3 = (f32[2,577,512]{2,1,0:T(8,128)}, f32[2,2,1024]{2,1,0:T(2,128)}) custom-call(s32[3]{0:T(128)S(1)} %pad_add_fusion.at_ref, bf16[2,592,1024]{2,1,0:T(8,128)(2,1)S(1)} %copy-done.17, bf16[2,592,1024]{2,1,0:T(8,128)(2,1)S(1)} %copy-done.10, bf16[2,592,1024]{2,1,0:T(8,128)(2,1)} %fusion.6.a_ref, ...), custom_call_target="tpu_custom_call" | custom-call | flops 10000000 | bytes 1024 | tf_op jit(solution)/shard_map/norm_back/pallas_call | solution.py:222
  355.4 4.9 %copy.67 = f32[2,577,512]{2,0,1:T(2,128)} copy(f32[2,577,512]{2,1,0:T(8,128)} %get-tuple-element.277) | data formatting | bytes 4726784
  360.5 2.0 collective-permute-start.27
  368.8 3.4 collective-permute-start.31
  374.0 1.8 copy.68
  375.8 1.9 spread.1
  (236 shorter events, 57.3 us)
Async XLA Ops:
  7.2 76.0 %all-gather.5.cloned.1.call-start = ((), (), s32[]{:S(2)}) async-start(), calls=%async_computation.9 | async-start | bytes 2621440 | tf_op jit(solution)/shard_map/all_gather | solution.py:901
  12.6 10.2 %collective-permute-start.3 = (bf16[2,592,512]{2,1,0:T(8,128)(2,1)S(1)}, bf16[2,592,512]{2,1,0:T(8,128)(2,1)S(1)}, u32[]{:S(2)}, u32[]{:S(2)}) collective-permute-start(bf16[2,592,512]{2,1,0:T(8,128)(2,1)S(1)} %pad_maximum_fusion.1.own_ref), channel_id=1, source_target_pairs={{0,1},{1,0},{2,3},{3,2},{4,5},{5,4},{6,7},{7,6},{8,9},{9,8},{10,11... | collective-permute-start | bytes 3637256 | tf_op jit(solution)/shard_map/ppermute | solution.py:21
  13.2 13.3 %collective-permute-start = (bf16[784,128]{1,0:T(8,128)(2,1)}, bf16[784,128]{1,0:T(8,128)(2,1)}, u32[]{:S(2)}, u32[]{:S(2)}) collective-permute-start(bf16[784,128]{1,0:T(8,128)(2,1)} %pad_maximum_fusion.5), channel_id=1, source_target_pairs={{0,2},{2,0},{4,6},{6,4},{1,3},{3,1},{5,7},{7,5},{8,10},{10,8},{12,... | collective-permute-start | bytes 602120 | tf_op jit(solution)/shard_map/ppermute | solution.py:21
  15.8 17.7 %collective-permute-start.1 = (bf16[784,128]{1,0:T(8,128)(2,1)}, bf16[784,128]{1,0:T(8,128)(2,1)}, u32[]{:S(2)}, u32[]{:S(2)}) collective-permute-start(bf16[784,128]{1,0:T(8,128)(2,1)} %pad_maximum_fusion.5), channel_id=1, source_target_pairs={{0,4},{2,6},{4,0},{6,2},{1,5},{3,7},{5,1},{7,3},{8,12},{10,14},{12... | collective-permute-start | bytes 602120 | tf_op jit(solution)/shard_map/ppermute | solution.py:21
  18.4 15.1 %collective-permute-start.2 = (bf16[784,128]{1,0:T(8,128)(2,1)}, bf16[784,128]{1,0:T(8,128)(2,1)}, u32[]{:S(2)}, u32[]{:S(2)}) collective-permute-start(bf16[784,128]{1,0:T(8,128)(2,1)} %pad_maximum_fusion.5), channel_id=1, source_target_pairs={{0,6},{2,4},{4,2},{6,0},{1,7},{3,5},{5,3},{7,1},{8,14},{10,12},{12... | collective-permute-start | bytes 602120 | tf_op jit(solution)/shard_map/ppermute | solution.py:21
  22.8 10.7 %copy-start.34 = (bf16[512,256]{1,0:T(8,128)(2,1)S(1)}, bf16[512,256]{1,0:T(8,128)(2,1)}, u32[]{:S(2)}) copy-start(bf16[512,256]{1,0:T(8,128)(2,1)} %param.18) | copy-start | bytes 786436
  22.9 16.6 %copy-start.39 = (bf16[2,512]{1,0:T(2,128)(2,1)S(1)}, bf16[2,512]{1,0:T(2,128)(2,1)}, u32[]{:S(2)}) copy-start(bf16[2,512]{1,0:T(2,128)(2,1)} %param.17) | copy-start | bytes 6148
  26.5 13.1 %copy-start.2 = (bf16[2,592,1024]{2,1,0:T(8,128)(2,1)S(1)}, bf16[2,592,1024]{2,1,0:T(8,128)(2,1)}, u32[]{:S(2)}) copy-start(bf16[2,592,1024]{2,1,0:T(8,128)(2,1)} %get-tuple-element.139.n_ref) | copy-start | bytes 7274500
  34.4 84.1 %all-gather.7.cloned.1.call-start = ((), (), s32[]{:S(2)}) async-start(), calls=%async_computation.10 | async-start | bytes 1310720 | tf_op jit(solution)/shard_map/all_gather | solution.py:905
  34.6 17.7 %copy-start.8 = (bf16[256,3,512]{2,0,1:T(8,128)(2,1)S(1)}, bf16[256,3,512]{2,0,1:T(8,128)(2,1)}, u32[]{:S(2)}) copy-start(bf16[256,3,512]{2,0,1:T(8,128)(2,1)} %param.16) | copy-start | bytes 2359300
  35.9 22.7 %copy-start.19 = (bf16[2320,128]{1,0:T(8,128)(2,1)}, bf16[2320,128]{1,0:T(8,128)(2,1)S(1)}, u32[]{:S(2)}) copy-start(bf16[2320,128]{1,0:T(8,128)(2,1)S(1)} %stack.63.rest_ref) | copy-start | bytes 1781764
  35.9 16.4 %collective-permute-start.6 = (bf16[2320,128]{1,0:T(8,128)(2,1)S(1)}, bf16[2320,128]{1,0:T(8,128)(2,1)S(1)}, u32[]{:S(2)}, u32[]{:S(2)}) collective-permute-start(bf16[2320,128]{1,0:T(8,128)(2,1)S(1)} %stack.63.rest_ref), channel_id=1, source_target_pairs={{0,8},{8,0},{16,24},{24,16},{1,9},{9,1},{17,25},{25,17},{2,10},{10... | collective-permute-start | bytes 1781768 | tf_op jit(solution)/shard_map/ppermute | solution.py:21
  37.4 26.5 %collective-permute-start.5 = (bf16[2320,128]{1,0:T(8,128)(2,1)S(1)}, bf16[2320,128]{1,0:T(8,128)(2,1)S(1)}, u32[]{:S(2)}, u32[]{:S(2)}) collective-permute-start(bf16[2320,128]{1,0:T(8,128)(2,1)S(1)} %stack.63.rest_ref), channel_id=1, source_target_pairs={{0,16},{8,24},{16,0},{24,8},{1,17},{9,25},{17,1},{25,9},{2,18},{10... | collective-permute-start | bytes 1781768 | tf_op jit(solution)/shard_map/ppermute | solution.py:21
  39.0 31.2 %collective-permute-start.4 = (bf16[2320,128]{1,0:T(8,128)(2,1)S(1)}, bf16[2320,128]{1,0:T(8,128)(2,1)S(1)}, u32[]{:S(2)}, u32[]{:S(2)}) collective-permute-start(bf16[2320,128]{1,0:T(8,128)(2,1)S(1)} %stack.63.rest_ref), channel_id=1, source_target_pairs={{0,24},{8,16},{16,8},{24,0},{1,25},{9,17},{17,9},{25,1},{2,26},{10... | collective-permute-start | bytes 1781768 | tf_op jit(solution)/shard_map/ppermute | solution.py:21
  77.3 9.6 %copy-start.4 = (bf16[2,592,512]{2,1,0:T(8,128)(2,1)S(1)}, bf16[2,592,512]{2,1,0:T(8,128)(2,1)}, u32[]{:S(2)}) copy-start(bf16[2,592,512]{2,1,0:T(8,128)(2,1)} %get-tuple-element.153.a_ref) | copy-start | bytes 3637252
  86.9 6.9 %copy-start.43 = (bf16[2048]{0:T(1024)(128)(2,1)S(1)}, bf16[2048]{0:T(1024)(128)(2,1)}, u32[]{:S(2)}) copy-start(bf16[2048]{0:T(1024)(128)(2,1)} %param.21) | copy-start | bytes 12292
  91.5 4.8 %collective-permute-start.7 = (bf16[2,592,1024]{2,1,0:T(8,128)(2,1)}, bf16[2,592,1024]{2,1,0:T(8,128)(2,1)S(1)}, u32[]{:S(2)}, u32[]{:S(2)}) collective-permute-start(bf16[2,592,1024]{2,1,0:T(8,128)(2,1)} %get-tuple-element.154.a_ref), channel_id=1, source_target_pairs={{0,1},{1,0},{2,3},{3,2},{4,5},{5,4},{6,7},{7,6},{8,9},{9,8},{10,11... | collective-permute-start | bytes 7274504 | tf_op jit(solution)/shard_map/ppermute | solution.py:21
  91.5 161.9 %reduce-scatter.4.cloned.1.call-start = ((), (), s32[]{:S(2)}) async-start(), calls=%async_computation.6 | async-start | bytes 5242880 | tf_op jit(solution)/shard_map/reduce_scatter | solution.py:75
  91.8 31.6 %collective-permute-start.8 = (bf16[2,592,512]{2,1,0:T(8,128)(2,1)}, bf16[2,592,512]{2,1,0:T(8,128)(2,1)}, u32[]{:S(2)}, u32[]{:S(2)}) collective-permute-start(bf16[2,592,512]{2,1,0:T(8,128)(2,1)} %pad.9.own_ref), channel_id=1, source_target_pairs={{0,1},{1,0},{2,3},{3,2},{4,5},{5,4},{6,7},{7,6},{8,9},{9,8},{10,11... | collective-permute-start | bytes 3637256 | tf_op jit(solution)/shard_map/ppermute | solution.py:21
  92.3 37.6 %collective-permute-start.10 = (bf16[3,256,512]{2,1,0:T(8,128)(2,1)}, bf16[3,256,512]{2,1,0:T(8,128)(2,1)}, u32[]{:S(2)}, u32[]{:S(2)}) collective-permute-start(bf16[3,256,512]{2,1,0:T(8,128)(2,1)} %unpack.1.rest_ref), channel_id=1, source_target_pairs={{0,16},{8,24},{16,0},{24,8},{1,17},{9,25},{17,1},{25,9},{2,18},{10... | collective-permute-start | bytes 2359304 | tf_op jit(solution)/shard_map/ppermute | solution.py:21
  93.8 43.8 %collective-permute-start.11 = (bf16[3,256,512]{2,1,0:T(8,128)(2,1)}, bf16[3,256,512]{2,1,0:T(8,128)(2,1)}, u32[]{:S(2)}, u32[]{:S(2)}) collective-permute-start(bf16[3,256,512]{2,1,0:T(8,128)(2,1)} %unpack.1.rest_ref), channel_id=1, source_target_pairs={{0,24},{8,16},{16,8},{24,0},{1,25},{9,17},{17,9},{25,1},{2,26},{10... | collective-permute-start | bytes 2359304 | tf_op jit(solution)/shard_map/ppermute | solution.py:21
  95.3 42.4 %collective-permute-start.9 = (bf16[3,256,512]{2,1,0:T(8,128)(2,1)}, bf16[3,256,512]{2,1,0:T(8,128)(2,1)}, u32[]{:S(2)}, u32[]{:S(2)}) collective-permute-start(bf16[3,256,512]{2,1,0:T(8,128)(2,1)} %unpack.1.rest_ref), channel_id=1, source_target_pairs={{0,8},{8,0},{16,24},{24,16},{1,9},{9,1},{17,25},{25,17},{2,10},{10... | collective-permute-start | bytes 2359304 | tf_op jit(solution)/shard_map/ppermute | solution.py:21
  105.0 27.3 %copy-start.50 = (s32[2]{0:T(128)S(1)}, s32[2]{0:T(128)}, u32[]{:S(2)}) copy-start(s32[2]{0:T(128)} %param.15) | copy-start | bytes 28
  110.5 27.2 %copy-start.1 = (bf16[2,592,1024]{2,1,0:T(8,128)(2,1)S(1)}, bf16[2,592,1024]{2,1,0:T(8,128)(2,1)}, u32[]{:S(2)}) copy-start(bf16[2,592,1024]{2,1,0:T(8,128)(2,1)} %get-tuple-element.159.n_ref.b_ref) | copy-start | bytes 7274500
  121.9 42.8 %collective-permute-start.12 = (bf16[3,512,256]{2,1,0:T(8,128)(2,1)}, bf16[3,512,256]{2,1,0:T(8,128)(2,1)}, u32[]{:S(2)}, u32[]{:S(2)}) collective-permute-start(bf16[3,512,256]{2,1,0:T(8,128)(2,1)} %others.1.refs_0_), channel_id=1, source_target_pairs={{0,8},{8,0},{16,24},{24,16},{1,9},{9,1},{17,25},{25,17},{2,10},{10... | collective-permute-start | bytes 2359304 | tf_op jit(solution)/shard_map/ppermute | solution.py:21
  123.3 41.3 %collective-permute-start.13 = (bf16[3,512,256]{2,1,0:T(8,128)(2,1)}, bf16[3,512,256]{2,1,0:T(8,128)(2,1)}, u32[]{:S(2)}, u32[]{:S(2)}) collective-permute-start(bf16[3,512,256]{2,1,0:T(8,128)(2,1)} %others.1.refs_0_), channel_id=1, source_target_pairs={{0,16},{8,24},{16,0},{24,8},{1,17},{9,25},{17,1},{25,9},{2,18},{10... | collective-permute-start | bytes 2359304 | tf_op jit(solution)/shard_map/ppermute | solution.py:21
  129.9 35.0 %collective-permute-start.14 = (bf16[3,512,256]{2,1,0:T(8,128)(2,1)}, bf16[3,512,256]{2,1,0:T(8,128)(2,1)}, u32[]{:S(2)}, u32[]{:S(2)}) collective-permute-start(bf16[3,512,256]{2,1,0:T(8,128)(2,1)} %others.1.refs_0_), channel_id=1, source_target_pairs={{0,24},{8,16},{16,8},{24,0},{1,25},{9,17},{17,9},{25,1},{2,26},{10... | collective-permute-start | bytes 2359304 | tf_op jit(solution)/shard_map/ppermute | solution.py:21
  154.2 10.7 %copy-start.20 = (bf16[2048,256]{1,0:T(8,128)(2,1)S(1)}, bf16[2048,256]{1,0:T(8,128)(2,1)}, u32[]{:S(2)}) copy-start(bf16[2048,256]{1,0:T(8,128)(2,1)} %own_ref.9) | copy-start | bytes 3145732
  177.2 11.1 %copy-start.28 = (bf16[1024,2048]{1,0:T(8,128)(2,1)S(1)}, bf16[1024,2048]{1,0:T(8,128)(2,1)}, u32[]{:S(2)}) copy-start(bf16[1024,2048]{1,0:T(8,128)(2,1)} %get-tuple-element.190) | copy-start | bytes 12582916
  177.3 11.0 %copy-start.29 = (bf16[2,592,2048]{2,1,0:T(8,128)(2,1)S(1)}, bf16[2,592,2048]{2,1,0:T(8,128)(2,1)}, u32[]{:S(2)}) copy-start(bf16[2,592,2048]{2,1,0:T(8,128)(2,1)} %get-tuple-element.189.a_ref) | copy-start | bytes 14548996
  195.3 5.2 %collective-permute-start.15 = (bf16[2,592,1024]{2,1,0:T(8,128)(2,1)}, bf16[2,592,1024]{2,1,0:T(8,128)(2,1)}, u32[]{:S(2)}, u32[]{:S(2)}) collective-permute-start(bf16[2,592,1024]{2,1,0:T(8,128)(2,1)} %fusion.9.a_ref), channel_id=1, source_target_pairs={{0,1},{1,0},{2,3},{3,2},{4,5},{5,4},{6,7},{7,6},{8,9},{9,8},{10,11... | collective-permute-start | bytes 7274504 | tf_op jit(solution)/shard_map/ppermute | solution.py:21
  195.3 53.9 %all-to-all-start = ((bf16[4,512,1024]{2,1,0:T(8,128)(2,1)}), bf16[4,512,1024]{2,1,0:T(8,128)(2,1)}, u32[]{:S(2)}, u32[]{:S(2)}) async-start(bf16[4,512,1024]{2,1,0:T(8,128)(2,1)} %bitcast.114), calls=%async_computation | async-start | bytes 8388608 | tf_op jit(solution)/shard_map/all_to_all | solution.py:66
  200.4 82.1 %reduce-scatter.6.cloned.1.call-start = ((), (), s32[]{:S(2)}) async-start(), calls=%async_computation.7 | async-start | bytes 1310720 | tf_op jit(solution)/shard_map/reduce_scatter | solution.py:75
  202.2 7.9 %copy-start.49 = (bf16[512,1024]{1,0:T(8,128)(2,1)S(1)}, bf16[512,1024]{1,0:T(8,128)(2,1)}, u32[]{:S(2)}) copy-start(bf16[512,1024]{1,0:T(8,128)(2,1)} %get-tuple-element.192) | copy-start | bytes 3145732
  217.0 7.9 %copy-start.3 = (bf16[2,592,1024]{2,1,0:T(8,128)(2,1)S(1)}, bf16[2,592,1024]{2,1,0:T(8,128)(2,1)}, u32[]{:S(2)}) copy-start(bf16[2,592,1024]{2,1,0:T(8,128)(2,1)} %get-tuple-element.139.n_ref) | copy-start | bytes 7274500
  217.0 98.2 %reduce-scatter.8.cloned.1.call-start = ((), (), s32[]{:S(2)}) async-start(), calls=%async_computation.8 | async-start | bytes 1310720 | tf_op jit(solution)/shard_map/reduce_scatter | solution.py:75
  239.7 13.7 %copy-start.25 = (f32[2,8,592]{2,1,0:T(8,128)S(1)}, f32[2,8,592]{2,1,0:T(8,128)}, u32[]{:S(2)}) copy-start(f32[2,8,592]{2,1,0:T(8,128)} %get-tuple-element.209.stats_ref) | copy-start | bytes 113668
  239.7 25.9 %collective-permute-start.16 = (bf16[1024,384]{1,0:T(8,128)(2,1)}, bf16[1024,384]{1,0:T(8,128)(2,1)S(1)}, u32[]{:S(2)}, u32[]{:S(2)}) collective-permute-start(bf16[1024,384]{1,0:T(8,128)(2,1)} %bitcast_convert_fusion.4), channel_id=1, source_target_pairs={{0,8},{8,0},{16,24},{24,16},{1,9},{9,1},{17,25},{25,17},{2,10},{10... | collective-permute-start | bytes 2359304 | tf_op jit(solution)/shard_map/ppermute | solution.py:21
  241.7 35.5 %collective-permute-start.17 = (bf16[1024,384]{1,0:T(8,128)(2,1)}, bf16[1024,384]{1,0:T(8,128)(2,1)}, u32[]{:S(2)}, u32[]{:S(2)}) collective-permute-start(bf16[1024,384]{1,0:T(8,128)(2,1)} %bitcast_convert_fusion.3), channel_id=1, source_target_pairs={{0,16},{8,24},{16,0},{24,8},{1,17},{9,25},{17,1},{25,9},{2,18},{10... | collective-permute-start | bytes 2359304 | tf_op jit(solution)/shard_map/ppermute | solution.py:21
  264.6 19.6 %collective-permute-start.18 = (bf16[1024,384]{1,0:T(8,128)(2,1)}, bf16[1024,384]{1,0:T(8,128)(2,1)}, u32[]{:S(2)}, u32[]{:S(2)}) collective-permute-start(bf16[1024,384]{1,0:T(8,128)(2,1)} %bitcast_convert_fusion.2), channel_id=1, source_target_pairs={{0,24},{8,16},{16,8},{24,0},{1,25},{9,17},{17,9},{25,1},{2,26},{10... | collective-permute-start | bytes 2359304 | tf_op jit(solution)/shard_map/ppermute | solution.py:21
  265.6 7.9 %copy-start.31 = (bf16[1024,384]{1,0:T(8,128)(2,1)}, bf16[1024,384]{1,0:T(8,128)(2,1)S(1)}, u32[]{:S(2)}) copy-start(bf16[1024,384]{1,0:T(8,128)(2,1)S(1)} %collective-permute-done.16) | copy-start | bytes 2359300
  273.4 10.8 %copy-start.30 = (bf16[2048,256]{1,0:T(8,128)(2,1)S(1)}, bf16[2048,256]{1,0:T(8,128)(2,1)}, u32[]{:S(2)}) copy-start(bf16[2048,256]{1,0:T(8,128)(2,1)} %reduce-scatter.4.cloned.1.call-done) | copy-start | bytes 3145732
  286.3 19.3 %all-to-all-start.1 = ((bf16[4,640,256]{2,1,0:T(8,128)(2,1)}), bf16[4,640,256]{2,1,0:T(8,128)(2,1)S(1)}, u32[]{:S(2)}, u32[]{:S(2)}) async-start(bf16[4,640,256]{2,1,0:T(8,128)(2,1)} %pad_maximum_fusion), calls=%async_computation.3 | async-start | bytes 2621440 | tf_op jit(solution)/shard_map/all_to_all | solution.py:66
  289.9 8.5 %copy-start.32 = (bf16[1024,384]{1,0:T(8,128)(2,1)S(1)}, bf16[1024,384]{1,0:T(8,128)(2,1)}, u32[]{:S(2)}) copy-start(bf16[1024,384]{1,0:T(8,128)(2,1)} %copy-done.31) | copy-start | bytes 2359300
  289.9 8.5 %copy-start.33 = (bf16[1024,384]{1,0:T(8,128)(2,1)S(1)}, bf16[1024,384]{1,0:T(8,128)(2,1)}, u32[]{:S(2)}) copy-start(bf16[1024,384]{1,0:T(8,128)(2,1)} %bitcast_convert_fusion.1) | copy-start | bytes 2359300
  298.4 49.5 %collective-permute-start.23 = (bf16[2,592,1024]{2,1,0:T(8,128)(2,1)}, bf16[2,592,1024]{2,1,0:T(8,128)(2,1)}, u32[]{:S(2)}, u32[]{:S(2)}) collective-permute-start(bf16[2,592,1024]{2,1,0:T(8,128)(2,1)} %fusion.6.a_ref), channel_id=1, source_target_pairs={{0,1},{1,0},{2,3},{3,2},{4,5},{5,4},{6,7},{7,6},{8,9},{9,8},{10,11... | collective-permute-start | bytes 7274504 | tf_op jit(solution)/shard_map/ppermute | solution.py:21
  301.3 29.8 %collective-permute-start.19 = (bf16[256,384]{1,0:T(8,128)(2,1)}, bf16[256,384]{1,0:T(8,128)(2,1)}, u32[]{:S(2)}, u32[]{:S(2)}) collective-permute-start(bf16[256,384]{1,0:T(8,128)(2,1)} %get-tuple-element.294), channel_id=1, source_target_pairs={{0,2},{2,0},{4,6},{6,4},{1,3},{3,1},{5,7},{7,5},{8,10},{10,8},{12,... | collective-permute-start | bytes 589832 | tf_op jit(solution)/shard_map/ppermute | solution.py:21
  302.4 28.6 %collective-permute-start.20 = (bf16[256,384]{1,0:T(8,128)(2,1)}, bf16[256,384]{1,0:T(8,128)(2,1)}, u32[]{:S(2)}, u32[]{:S(2)}) collective-permute-start(bf16[256,384]{1,0:T(8,128)(2,1)} %get-tuple-element.296), channel_id=1, source_target_pairs={{0,4},{2,6},{4,0},{6,2},{1,5},{3,7},{5,1},{7,3},{8,12},{10,14},{12... | collective-permute-start | bytes 589832 | tf_op jit(solution)/shard_map/ppermute | solution.py:21
  304.4 26.6 %collective-permute-start.21 = (bf16[256,384]{1,0:T(8,128)(2,1)}, bf16[256,384]{1,0:T(8,128)(2,1)}, u32[]{:S(2)}, u32[]{:S(2)}) collective-permute-start(bf16[256,384]{1,0:T(8,128)(2,1)} %get-tuple-element.295), channel_id=1, source_target_pairs={{0,6},{2,4},{4,2},{6,0},{1,7},{3,5},{5,3},{7,1},{8,14},{10,12},{12... | collective-permute-start | bytes 589832 | tf_op jit(solution)/shard_map/ppermute | solution.py:21
  317.8 42.5 %all-to-all-start.2 = ((bf16[4,1152,256]{2,1,0:T(8,128)(2,1)}), bf16[4,1152,256]{2,1,0:T(8,128)(2,1)}, u32[]{:S(2)}, u32[]{:S(2)}) async-start(bf16[4,1152,256]{2,1,0:T(8,128)(2,1)} %broadcast_in_dim.42), calls=%async_computation.5 | async-start | bytes 4718592 | tf_op jit(solution)/shard_map/all_to_all | solution.py:71
  331.0 8.5 %copy-start.12 = (bf16[2,592,1024]{2,1,0:T(8,128)(2,1)S(1)}, bf16[2,592,1024]{2,1,0:T(8,128)(2,1)}, u32[]{:S(2)}) copy-start(bf16[2,592,1024]{2,1,0:T(8,128)(2,1)} %get-tuple-element.155.v_ref.m_ref) | copy-start | bytes 7274500
  335.6 3.9 collective-permute-start.22
  335.7 9.0 %copy-start.35 = (f32[3,1024]{1,0:T(4,128)}, f32[3,1024]{1,0:T(4,128)S(1)}, u32[]{:S(2)}) copy-start(f32[3,1024]{1,0:T(4,128)S(1)} %reduce_sum.57) | copy-start | bytes 36868
  335.8 24.5 %collective-permute-start.24 = (bf16[256,384]{1,0:T(8,128)(2,1)S(1)}, bf16[256,384]{1,0:T(8,128)(2,1)S(1)}, u32[]{:S(2)}, u32[]{:S(2)}) collective-permute-start(bf16[256,384]{1,0:T(8,128)(2,1)S(1)} %fusion.22.refs_0_), channel_id=1, source_target_pairs={{0,8},{8,0},{16,24},{24,16},{1,9},{9,1},{17,25},{25,17},{2,10},{10... | collective-permute-start | bytes 589832 | tf_op jit(solution)/shard_map/ppermute | solution.py:21
  337.9 22.4 %collective-permute-start.25 = (bf16[256,384]{1,0:T(8,128)(2,1)S(1)}, bf16[256,384]{1,0:T(8,128)(2,1)S(1)}, u32[]{:S(2)}, u32[]{:S(2)}) collective-permute-start(bf16[256,384]{1,0:T(8,128)(2,1)S(1)} %fusion.22.refs_0_), channel_id=1, source_target_pairs={{0,16},{8,24},{16,0},{24,8},{1,17},{9,25},{17,1},{25,9},{2,18},{10... | collective-permute-start | bytes 589832 | tf_op jit(solution)/shard_map/ppermute | solution.py:21
  339.4 21.0 %collective-permute-start.26 = (bf16[256,384]{1,0:T(8,128)(2,1)S(1)}, bf16[256,384]{1,0:T(8,128)(2,1)S(1)}, u32[]{:S(2)}, u32[]{:S(2)}) collective-permute-start(bf16[256,384]{1,0:T(8,128)(2,1)S(1)} %fusion.22.refs_0_), channel_id=1, source_target_pairs={{0,24},{8,16},{16,8},{24,0},{1,25},{9,17},{17,9},{25,1},{2,26},{10... | collective-permute-start | bytes 589832 | tf_op jit(solution)/shard_map/ppermute | solution.py:21
  341.2 6.8 %copy-start.10 = (bf16[2,592,1024]{2,1,0:T(8,128)(2,1)S(1)}, bf16[2,592,1024]{2,1,0:T(8,128)(2,1)}, u32[]{:S(2)}) copy-start(bf16[2,592,1024]{2,1,0:T(8,128)(2,1)} %get-tuple-element.138.x_ref.v_ref) | copy-start | bytes 7274500
  341.2 6.8 %copy-start.17 = (bf16[2,592,1024]{2,1,0:T(8,128)(2,1)S(1)}, bf16[2,592,1024]{2,1,0:T(8,128)(2,1)}, u32[]{:S(2)}) copy-start(bf16[2,592,1024]{2,1,0:T(8,128)(2,1)} %get-tuple-element.191.base_ref) | copy-start | bytes 7274500
  360.5 8.0 %collective-permute-start.27 = (f32[6144]{0:T(1024)S(1)}, f32[6144]{0:T(1024)S(1)}, u32[]{:S(2)}, u32[]{:S(2)}) collective-permute-start(f32[6144]{0:T(1024)S(1)} %pad_maximum_fusion.6), channel_id=1, source_target_pairs={{0,8},{8,0},{16,24},{24,16},{1,9},{9,1},{17,25},{25,17},{2,10},{10... | collective-permute-start | bytes 73736 | tf_op jit(solution)/shard_map/ppermute | solution.py:21
  362.5 6.0 %collective-permute-start.28 = (f32[6144]{0:T(1024)S(1)}, f32[6144]{0:T(1024)S(1)}, u32[]{:S(2)}, u32[]{:S(2)}) collective-permute-start(f32[6144]{0:T(1024)S(1)} %pad_maximum_fusion.6), channel_id=1, source_target_pairs={{0,16},{8,24},{16,0},{24,8},{1,17},{9,25},{17,1},{25,9},{2,18},{10... | collective-permute-start | bytes 73736 | tf_op jit(solution)/shard_map/ppermute | solution.py:21
  364.0 4.7 %collective-permute-start.29 = (f32[6144]{0:T(1024)S(1)}, f32[6144]{0:T(1024)S(1)}, u32[]{:S(2)}, u32[]{:S(2)}) collective-permute-start(f32[6144]{0:T(1024)S(1)} %pad_maximum_fusion.6), channel_id=1, source_target_pairs={{0,24},{8,16},{16,8},{24,0},{1,25},{9,17},{17,9},{25,1},{2,26},{10... | collective-permute-start | bytes 73736 | tf_op jit(solution)/shard_map/ppermute | solution.py:21
  368.7 9.0 %collective-permute-start.30 = (f32[6144]{0:T(1024)S(1)}, f32[6144]{0:T(1024)S(1)}, u32[]{:S(2)}, u32[]{:S(2)}) collective-permute-start(f32[6144]{0:T(1024)S(1)} %add_add_fusion.1), channel_id=1, source_target_pairs={{0,2},{2,0},{4,6},{6,4},{1,3},{3,1},{5,7},{7,5},{8,10},{10,8},{12,... | collective-permute-start | bytes 73736 | tf_op jit(solution)/shard_map/ppermute | solution.py:21
  368.8 8.9 %collective-permute-start.31 = (f32[6144]{0:T(1024)S(1)}, f32[6144]{0:T(1024)S(1)}, u32[]{:S(2)}, u32[]{:S(2)}) collective-permute-start(f32[6144]{0:T(1024)S(1)} %add_add_fusion.1), channel_id=1, source_target_pairs={{0,4},{2,6},{4,0},{6,2},{1,5},{3,7},{5,1},{7,3},{8,12},{10,14},{12... | collective-permute-start | bytes 73736 | tf_op jit(solution)/shard_map/ppermute | solution.py:21
  372.2 5.6 %collective-permute-start.32 = (f32[6144]{0:T(1024)S(1)}, f32[6144]{0:T(1024)S(1)}, u32[]{:S(2)}, u32[]{:S(2)}) collective-permute-start(f32[6144]{0:T(1024)S(1)} %add_add_fusion.1), channel_id=1, source_target_pairs={{0,6},{2,4},{4,2},{6,0},{1,7},{3,5},{5,3},{7,1},{8,14},{10,12},{12... | collective-permute-start | bytes 73736 | tf_op jit(solution)/shard_map/ppermute | solution.py:21
  (29 other events, 112.5 us)
Sparse Core Ops, SparseCore 0:
  34.5 48.6 all-gather.4
  91.6 26.7 all-gather.6
  177.4 74.5 reduce-scatter.3
  254.8 27.6 reduce-scatter.5
  285.2 29.9 reduce-scatter.7

commit v2 on v1

--- a/solution.py
+++ b/solution.py
@@ -175,7 +175,7 @@
         compiler_params=pltpu.CompilerParams(vmem_limit_bytes=32 << 20),
         cost_estimate=cost(0.01),
         name="norm_two",
-    )(x, share_a, share_b, params)
+    )(stay(x), stay(share_a), stay(share_b), params)
 
 
 def norm_back_kernel(second, at_ref, base_ref, v_ref, a_ref, b_ref, gain_ref, weight_ref, *refs):
@@ -231,7 +231,7 @@
         0.01,
         scratch=[pltpu.VMEM((8, 128) if second else (rows, model), F32)],
         limit=48,
-    )(at, base, v, share_a, share_b, gain[None], weight)
+    )(at, stay(base), stay(v), stay(share_a), stay(share_b), gain[None], weight)
 
 
 def join_kernel(normal, at_ref, own_ref, other_ref, *refs):
@@ -551,7 +551,7 @@
         jax.ShapeDtypeStruct((count, length, width), BF16),
         "close",
         0.01,
-    )(at, middle, part, other, bias)
+    )(at, stay(middle), stay(part), other, bias)
 
 
 def spread_kernel(n_dp, at_ref, *refs):

time: 392 us -> 391 us (level)
  local copies, waits for them, and re-layouts: 38.7 us -> 31.7 us
  Pallas kernels: 163 us -> 167 us
    unnamed x106 -> x92, local copies, waits for them, and re-layouts: 20.4 us -> 13.3 us
  transfers between devices with their start and end apart: 41 -> 41, of which waited for: 14 -> 14; matrix products, arithmetic and copies ran while one was open for 19% -> 19% of each run, Pallas kernels for 37% -> 38%
where the time goes in v2:
time: 391 us; the launch traced here: 387 us
  Pallas kernels  167 us (43%)
  waiting for transfers between devices  62.6 us (16%)
  starting transfers between devices  52.9 us (14%)
  matrix products  44.2 us (11%)
  local copies, waits for them, and re-layouts  31.7 us (8%)
  between operations  14.8 us (4%)
  other arithmetic  13.3 us (3%)
    ppermute x33, starting transfers between devices, peer(): return lax.ppermute(value, axis, [(i, i ^ p) for i in range(n)])  39 us
    pallas_call x4, Pallas kernels, mix_back(): scalar_call(functools.partial(mix_back_kernel, length), at, (count,), [pl...  30.8 us
    ppermute x33, waiting for transfers between devices, peer(): return lax.ppermute(value, axis, [(i, i ^ p) for i in range(n)])  25.3 us
    pallas_call x4, Pallas kernels, mix(): scalar_call(functools.partial(mix_kernel, length, n_row), at, (count,), [...  25 us
    pallas_call x4, Pallas kernels, up(): scalar_call(functools.partial(up_kernel, model // own.shape[0]), at, (cou...  22 us
    pallas_call x2, Pallas kernels, product(): pl.pallas_call(product_kernel, grid=(units // run,), in_specs=[pl.BlockSp...  21.5 us
    pallas_call x2, Pallas kernels, norm_back(): scalar_call(functools.partial(norm_back_kernel, second), at, (count,), [i...  17 us
    reduce_scatter x3, waiting for transfers between devices, scatter_row(): lax.psum_scatter(value, 'row', scatter_dimension=model_dim, tiled=True)  15.1 us
  transfers between devices with their start and end apart: 41, of which 14 were waited for; matrix products, arithmetic and copies ran while one was open for 19% of the time, Pallas kernels for 38%

profile of v2, /device:TPU:0, one launch (start us, length us, event | category | flops | bytes accessed | tf_op | source)
XLA Modules:
  0.0 386.6 jit_solution(190080559973708958)
XLA Ops:
  13.2 2.6 collective-permute-start
  15.8 2.6 collective-permute-start.1
  21.1 1.7 constant_dynamic-slice_fusion
  22.9 3.5 join.1
  26.5 7.0 %collective-permute-done.1.refs_1_ = bf16[784,128]{1,0:T(8,128)(2,1)} collective-permute-done((bf16[784,128]{1,0:T(8,128)(2,1)}, bf16[784,128]{1,0:T(8,128)(2,1)}, u32[]{:S(2)}, u32[]{:S(2)}) %collective-permute-start.1) | collective-permute-done | bytes 200736 | tf_op jit(solution)/shard_map/ppermute | solution.py:21
  40.8 6.3 %mix.4 = (bf16[2,592,384]{2,1,0:T(8,128)(2,1)}, bf16[2,592,512]{2,1,0:T(8,128)(2,1)}, bf16[1024,1536]{1,0:T(8,128)(2,1)}, f32[2,592,128]{2,1,0:T(8,128)}, f32[2,8,592]{2,1,0:T(8,128)}) custom-call(s32[3]{0:T(128)S(1)} %pad_add_fusion.at_ref, bf16[2,592,1024]{2,1,0:T(8,128)(2,1)S(1)} %copy-done.2, bf16[3,256,512]{2,1,0:T(8,128)(2,1)S(1)} %bitcast.106, ...), custom_call_target="tpu_custom_call" | custom-call | flops 10000000 | bytes 1024 | tf_op jit(solution)/shard_map/mix/pallas_call | solution.py:703
  47.0 5.3 %collective-permute-done.6.rest_ref = bf16[2320,128]{1,0:T(8,128)(2,1)S(1)} collective-permute-done((bf16[2320,128]{1,0:T(8,128)(2,1)S(1)}, bf16[2320,128]{1,0:T(8,128)(2,1)S(1)}, u32[]{:S(2)}, u32[]{:S(2)}) %collective-permute-start.6) | collective-permute-done | bytes 593952 | tf_op jit(solution)/shard_map/ppermute | solution.py:21
  52.3 6.3 %mix.5 = (bf16[2,592,384]{2,1,0:T(8,128)(2,1)}, bf16[2,592,512]{2,1,0:T(8,128)(2,1)}, bf16[1024,1536]{1,0:T(8,128)(2,1)}, f32[2,592,128]{2,1,0:T(8,128)}, f32[2,8,592]{2,1,0:T(8,128)}) custom-call(s32[3]{0:T(128)S(1)} %pad_add_fusion.at_ref, bf16[2,592,1024]{2,1,0:T(8,128)(2,1)S(1)} %copy-done.2, ...), custom_call_target="tpu_custom_call", output_to_operand_aliasing={{1}: (5, {}), {2}: (6, {})} | custom-call | flops 10000000 | bytes 1024 | tf_op jit(solution)/shard_map/mix/pallas_call | solution.py:703
  58.6 5.3 %collective-permute-done.5.rest_ref = bf16[2320,128]{1,0:T(8,128)(2,1)S(1)} collective-permute-done((bf16[2320,128]{1,0:T(8,128)(2,1)S(1)}, bf16[2320,128]{1,0:T(8,128)(2,1)S(1)}, u32[]{:S(2)}, u32[]{:S(2)}) %collective-permute-start.5) | collective-permute-done | bytes 593952 | tf_op jit(solution)/shard_map/ppermute | solution.py:21
  63.9 6.2 %mix.6 = (bf16[2,592,384]{2,1,0:T(8,128)(2,1)}, bf16[2,592,512]{2,1,0:T(8,128)(2,1)}, bf16[1024,1536]{1,0:T(8,128)(2,1)}, f32[2,592,128]{2,1,0:T(8,128)}, f32[2,8,592]{2,1,0:T(8,128)}) custom-call(s32[3]{0:T(128)S(1)} %pad_add_fusion.at_ref, bf16[2,592,1024]{2,1,0:T(8,128)(2,1)S(1)} %copy-done.2, ...), custom_call_target="tpu_custom_call", output_to_operand_aliasing={{1}: (5, {}), {2}: (6, {})} | custom-call | flops 10000000 | bytes 1024 | tf_op jit(solution)/shard_map/mix/pallas_call | solution.py:703
  70.2 6.3 %mix.7 = (bf16[2,592,384]{2,1,0:T(8,128)(2,1)}, bf16[2,592,512]{2,1,0:T(8,128)(2,1)}, bf16[1024,1536]{1,0:T(8,128)(2,1)}, f32[2,592,128]{2,1,0:T(8,128)}, f32[2,8,592]{2,1,0:T(8,128)}) custom-call(s32[3]{0:T(128)S(1)} %pad_add_fusion.at_ref, bf16[2,592,1024]{2,1,0:T(8,128)(2,1)S(1)} %copy-done.2, ...), custom_call_target="tpu_custom_call", output_to_operand_aliasing={{1}: (5, {}), {2}: (6, {})} | custom-call | flops 10000000 | bytes 1024 | tf_op jit(solution)/shard_map/mix/pallas_call | solution.py:703
  77.3 6.0 %all-gather.5.cloned.1.call-done = bf16[4096,256]{1,0:T(8,128)(2,1)} async-done(((bf16[1024,256]{1,0:T(8,128)(2,1)}), bf16[4096,256]{1,0:T(8,128)(2,1)}) %all-gather.5.cloned.1.call-update) | async-done | bytes 2097168 | tf_op jit(solution)/shard_map/all_gather | solution.py:901
  83.2 3.6 unpack.1.rest_ref
  86.9 4.6 %merge.1 = (bf16[2,592,1024]{2,1,0:T(8,128)(2,1)}, bf16[512,1024]{1,0:T(8,128)(2,1)}) custom-call(s32[3]{0:T(128)S(1)} %pad_add_fusion.at_ref, bf16[2,592,512]{2,1,0:T(8,128)(2,1)S(1)} %copy-done.4, bf16[4,1024,256]{2,1,0:T(8,128)(2,1)} %bitcast.116), custom_call_target="tpu_custom_call" | custom-call | flops 10000000 | bytes 1024 | tf_op jit(solution)/shard_map/merge/pallas_call | solution.py:379
  96.4 5.6 %norm_two.1 = (bf16[2,592,1024]{2,1,0:T(8,128)(2,1)}, bf16[2,592,1024]{2,1,0:T(8,128)(2,1)}) custom-call(bf16[2,592,1024]{2,1,0:T(8,128)(2,1)} %get-tuple-element.138.x_ref.v_ref, bf16[2,592,1024]{2,1,0:T(8,128)(2,1)} %get-tuple-element.154.a_ref, bf16[2,592,1024]{2,1,0:T(8,128)(2,1)} %collective-permute-done.7.b_ref, f32[3,1024]{1,0:T(4,128)S(1)} %pad_maximum_fusion.7.params_ref), custom_call_target="tpu_custom_call" | custom-call | flops 10000000 | bytes 1024 | tf_op jit(solution)/shard_map/norm_two/pallas_call | solution.py:169
  102.1 1.7 copy-done
  103.8 5.5 %expand.4 = (bf16[2,592,2048]{2,1,0:T(8,128)(2,1)}, bf16[2,592,2048]{2,1,0:T(8,128)(2,1)}, bf16[1024,2048]{1,0:T(8,128)(2,1)}) custom-call(s32[3]{0:T(128)S(1)} %pad_add_fusion.at_ref, bf16[2,592,1024]{2,1,0:T(8,128)(2,1)S(1)} %copy-done, bf16[256,2048]{1,0:T(8,128)(2,1)S(1)} %copy-done.6, bf16[3,256,512]{2,1,0:T(8,128)(2,1)} %unpack.1.rest_ref, ...), custom_call_target="tpu_custom_call" | custom-call | flops 10000000 | bytes 1024 | tf_op jit(solution)/shard_map/expand/pallas_call | solution.py:797
  109.3 9.2 %all-gather.7.cloned.1.call-done = bf16[2048,256]{1,0:T(8,128)(2,1)} async-done(((bf16[512,256]{1,0:T(8,128)(2,1)}), bf16[2048,256]{1,0:T(8,128)(2,1)}) %all-gather.7.cloned.1.call-update) | async-done | bytes 1048592 | tf_op jit(solution)/shard_map/all_gather | solution.py:905
  118.5 3.4 others.1.refs_0_
  124.8 5.1 %collective-permute-done.10.rest_ref = bf16[3,256,512]{2,1,0:T(8,128)(2,1)} collective-permute-done((bf16[3,256,512]{2,1,0:T(8,128)(2,1)}, bf16[3,256,512]{2,1,0:T(8,128)(2,1)}, u32[]{:S(2)}, u32[]{:S(2)}) %collective-permute-start.10) | collective-permute-done | bytes 786464 | tf_op jit(solution)/shard_map/ppermute | solution.py:21
  129.9 2.4 collective-permute-start.14
  133.2 4.5 %seed.1 = (bf16[2,592,1024]{2,1,0:T(8,128)(2,1)}, bf16[2,592,1024]{2,1,0:T(8,128)(2,1)}, f32[2,1,1024]{2,1,0:T(1,128)}) custom-call(s32[3]{0:T(128)S(1)} %pad_add_fusion.at_ref, bf16[2,592,512]{2,1,0:T(8,128)(2,1)} %pad.9.own_ref, bf16[2,592,512]{2,1,0:T(8,128)(2,1)} %collective-permute-done.8.other_ref, f32[2]{0:T(128)S(1)} %multiply_reduce_fusion.weight_ref), custom_call_target="tpu_custom_call" | custom-call | flops 10000000 | bytes 1024 | tf_op jit(solution)/shard_map/seed/pallas_call | solution.py:301
  137.7 5.5 %expand.5 = (bf16[2,592,2048]{2,1,0:T(8,128)(2,1)}, bf16[2,592,2048]{2,1,0:T(8,128)(2,1)}, bf16[1024,2048]{1,0:T(8,128)(2,1)}) custom-call(s32[3]{0:T(128)S(1)} %pad_add_fusion.at_ref, bf16[2,592,1024]{2,1,0:T(8,128)(2,1)S(1)} %copy-done.1, bf16[256,2048]{1,0:T(8,128)(2,1)S(1)} %copy-done.6, ...), custom_call_target="tpu_custom_call", output_to_operand_aliasing={{0}: (5, {}), {1}: (6, {}), {2}: (7, {})} | custom-call | flops 1000000000 | bytes 1024 | tf_op jit(solution)/shard_map/expand/pallas_call | solution.py:797
  143.2 5.5 %expand.6 = (bf16[2,592,2048]{2,1,0:T(8,128)(2,1)}, bf16[2,592,2048]{2,1,0:T(8,128)(2,1)}, bf16[1024,2048]{1,0:T(8,128)(2,1)}) custom-call(s32[3]{0:T(128)S(1)} %pad_add_fusion.at_ref, bf16[2,592,1024]{2,1,0:T(8,128)(2,1)S(1)} %copy-done.1, bf16[256,2048]{1,0:T(8,128)(2,1)S(1)} %copy-done.6, ...), custom_call_target="tpu_custom_call", output_to_operand_aliasing={{0}: (5, {}), {1}: (6, {}), {2}: (7, {})} | custom-call | flops 10000000 | bytes 1024 | tf_op jit(solution)/shard_map/expand/pallas_call | solution.py:797
  148.7 5.5 %expand.7 = (bf16[2,592,2048]{2,1,0:T(8,128)(2,1)}, bf16[2,592,2048]{2,1,0:T(8,128)(2,1)}, bf16[1024,2048]{1,0:T(8,128)(2,1)}) custom-call(s32[3]{0:T(128)S(1)} %pad_add_fusion.at_ref, bf16[2,592,1024]{2,1,0:T(8,128)(2,1)S(1)} %copy-done.1, bf16[256,2048]{1,0:T(8,128)(2,1)S(1)} %copy-done.6, ...), custom_call_target="tpu_custom_call", output_to_operand_aliasing={{0}: (5, {}), {1}: (6, {}), {2}: (7, {})} | custom-call | flops 10000000 | bytes 1024 | tf_op jit(solution)/shard_map/expand/pallas_call | solution.py:797
  154.2 10.5 %product.2 = bf16[2048,1024]{1,0:T(8,128)(2,1)} custom-call(bf16[2,592,2048]{2,1,0:T(8,128)(2,1)} %get-tuple-element.218.a_ref, bf16[2,592,1024]{2,1,0:T(8,128)(2,1)} %get-tuple-element.180.b_ref.seed_ref), custom_call_target="tpu_custom_call" | custom-call | flops 10000000 | bytes 1024 | tf_op jit(solution)/shard_map/product/pallas_call | solution.py:409
  164.9 12.3 %down_back.1 = (bf16[2,592,2048]{2,1,0:T(8,128)(2,1)}, f32[1,2048]{1,0:T(1,128)}, bf16[2048,1024]{1,0:T(8,128)(2,1)}) custom-call(s32[3]{0:T(128)S(1)} %pad_add_fusion.at_ref, bf16[2,592,1024]{2,1,0:T(8,128)(2,1)} %get-tuple-element.180.b_ref.seed_ref, bf16[2,592,2048]{2,1,0:T(8,128)(2,1)} %get-tuple-element.181.slope_ref, bf16[2048,256]{1,0:T(8,128)(2,1)S(1)} %copy-done.11, ...), custom_call_target="tpu_custom_call" | custom-call | flops 10000000 | bytes 1024 | tf_op jit(solution)/shard_map/down_back/pallas_call | solution.py:473
  177.3 11.1 %product.3 = bf16[2048,1024]{1,0:T(8,128)(2,1)} custom-call(bf16[2,592,2048]{2,1,0:T(8,128)(2,1)} %get-tuple-element.189.a_ref, bf16[2,592,1024]{2,1,0:T(8,128)(2,1)} %get-tuple-element.159.n_ref.b_ref), custom_call_target="tpu_custom_call" | custom-call | flops 10000000 | bytes 1024 | tf_op jit(solution)/shard_map/product/pallas_call | solution.py:409
  188.3 5.8 %fusion.9.a_ref = bf16[2,592,1024]{2,1,0:T(8,128)(2,1)S(1)} fusion(bf16[2,592,2048]{2,1,0:T(8,128)(2,1)S(1)} %copy-done.20, bf16[1024,2048]{1,0:T(8,128)(2,1)S(1)} %copy-done.19), kind=kOutput, calls=%fused_computation.8 | convolution fusion | flops 4967268352 | bytes 11468800 | tf_op jit(solution)/shard_map/ith,dh->itd/dot_general | solution.py:963
  195.6 4.8 %all-to-all-start = ((bf16[4,512,1024]{2,1,0:T(8,128)(2,1)}), bf16[4,512,1024]{2,1,0:T(8,128)(2,1)}, u32[]{:S(2)}, u32[]{:S(2)}) async-start(bf16[4,512,1024]{2,1,0:T(8,128)(2,1)} %bitcast.114), calls=%async_computation | async-start | bytes 8388608 | tf_op jit(solution)/shard_map/all_to_all | solution.py:66
  200.5 8.8 %norm_back.2 = (bf16[2,592,1024]{2,1,0:T(8,128)(2,1)}, f32[2,3,1024]{2,1,0:T(4,128)}) custom-call(s32[3]{0:T(128)S(1)} %pad_add_fusion.at_ref, bf16[2,592,1024]{2,1,0:T(8,128)(2,1)} %get-tuple-element.158.base_ref, bf16[2,592,1024]{2,1,0:T(8,128)(2,1)} %get-tuple-element.155.v_ref.m_ref, bf16[2,592,1024]{2,1,0:T(8,128)(2,1)} %copy-done.22, ...), custom_call_target="tpu_custom_call" | custom-call | flops 10000000 | bytes 1024 | tf_op jit(solution)/shard_map/norm_back/pallas_call | solution.py:222
  209.3 4.4 %convolution_convert_fusion.up_ref = bf16[2,592,512]{2,1,0:T(8,128)(2,1)} fusion(bf16[2,592,1024]{2,1,0:T(8,128)(2,1)} %get-tuple-element.191.base_ref, bf16[512,1024]{1,0:T(8,128)(2,1)S(1)} %copy-done.42), kind=kOutput, calls=%fused_computation.15 | convolution fusion | flops 1242120192 | bytes 4685824 | tf_op jit(solution)/shard_map/itd,fd->itf/dot_general | solution.py:970
  213.7 2.5 bitcast_convert_fusion
  216.3 7.8 %mix_back.4 = (bf16[2,592,1536]{2,1,0:T(8,128)(2,1)}, f32[2,1,384]{2,1,0:T(1,128)}) custom-call(s32[3]{0:T(128)S(1)} %pad_add_fusion.at_ref, bf16[2,592,384]{2,1,0:T(8,128)(2,1)} %get-tuple-element.194.m_ref, bf16[2,592,512]{2,1,0:T(8,128)(2,1)} %convolution_convert_fusion.up_ref, f32[2,592,128]{2,1,0:T(8,128)} %get-tuple-element.195.exact_ref, ...), custom_call_target="tpu_custom_call" | custom-call | flops 10000000 | bytes 1024 | tf_op jit(solution)/shard_map/mix_back/pallas_call | solution.py:742
  224.1 3.6 bitcast_convert_fusion.4
  227.7 7.6 %mix_back.5 = (bf16[2,592,1536]{2,1,0:T(8,128)(2,1)}, f32[2,1,384]{2,1,0:T(1,128)}) custom-call(s32[3]{0:T(128)S(1)} %pad_add_fusion.at_ref, bf16[2,592,384]{2,1,0:T(8,128)(2,1)} %get-tuple-element.199.m_ref, bf16[2,592,512]{2,1,0:T(8,128)(2,1)} %convolution_convert_fusion.up_ref, ...), custom_call_target="tpu_custom_call", output_to_operand_aliasing={{0}: (5, {})} | custom-call | flops 10000000 | bytes 1024 | tf_op jit(solution)/shard_map/mix_back/pallas_call | solution.py:742
  235.4 3.6 bitcast_convert_fusion.3
  239.0 1.9 collective-permute-start.16
  242.3 6.9 %all-to-all-done.in_ref = bf16[4,512,1024]{2,1,0:T(8,128)(2,1)} async-done(((bf16[4,512,1024]{2,1,0:T(8,128)(2,1)}), bf16[4,512,1024]{2,1,0:T(8,128)(2,1)}, u32[]{:S(2)}, u32[]{:S(2)}) %all-to-all-start) | async-done | bytes 4194336 | tf_op jit(solution)/shard_map/all_to_all | solution.py:66
  249.3 4.2 %add.144 = bf16[512,1024]{1,0:T(8,128)(2,1)} custom-call(bf16[4,512,1024]{2,1,0:T(8,128)(2,1)} %all-to-all-done.in_ref), custom_call_target="tpu_custom_call" | custom-call | flops 10000000 | bytes 1024 | tf_op jit(solution)/shard_map/add/pallas_call | solution.py:502
  253.5 7.6 %mix_back.6 = (bf16[2,592,1536]{2,1,0:T(8,128)(2,1)}, f32[2,1,384]{2,1,0:T(1,128)}) custom-call(s32[3]{0:T(128)S(1)} %pad_add_fusion.at_ref, bf16[2,592,384]{2,1,0:T(8,128)(2,1)} %get-tuple-element.207.m_ref, bf16[2,592,512]{2,1,0:T(8,128)(2,1)} %convolution_convert_fusion.up_ref, ...), custom_call_target="tpu_custom_call", output_to_operand_aliasing={{0}: (5, {})} | custom-call | flops 10000000 | bytes 1024 | tf_op jit(solution)/shard_map/mix_back/pallas_call | solution.py:742
  261.1 3.6 bitcast_convert_fusion.2
  265.7 7.8 %mix_back.7 = (bf16[2,592,1536]{2,1,0:T(8,128)(2,1)}, f32[2,1,384]{2,1,0:T(1,128)}) custom-call(s32[3]{0:T(128)S(1)} %pad_add_fusion.at_ref, bf16[2,592,384]{2,1,0:T(8,128)(2,1)} %get-tuple-element.156.m_ref, bf16[2,592,512]{2,1,0:T(8,128)(2,1)} %convolution_convert_fusion.up_ref, ...), custom_call_target="tpu_custom_call", output_to_operand_aliasing={{0}: (5, {})} | custom-call | flops 10000000 | bytes 1024 | tf_op jit(solution)/shard_map/mix_back/pallas_call | solution.py:742
  273.5 3.7 bitcast_convert_fusion.1
  277.2 5.3 %reduce-scatter.6.cloned.1.call-done = bf16[512,256]{1,0:T(8,128)(2,1)} async-done(((bf16[512,1024]{1,0:T(8,128)(2,1)}), bf16[512,256]{1,0:T(8,128)(2,1)}) %reduce-scatter.6.cloned.1.call-update) | async-done | bytes 262160 | tf_op jit(solution)/shard_map/reduce_scatter | solution.py:75
  283.7 2.1 pad_maximum_fusion
  285.8 3.7 all-to-all-start.1
  289.4 8.5 %fusion.6.a_ref = bf16[2,592,1024]{2,1,0:T(8,128)(2,1)} fusion(bf16[2,592,1536]{2,1,0:T(8,128)(2,1)} %get-tuple-element.216, bf16[1024,1536]{1,0:T(8,128)(2,1)} %get-tuple-element.217), kind=kOutput, calls=%fused_computation.7 | convolution fusion | flops 3725754368 | bytes 9207808 | tf_op jit(solution)/shard_map/itf,df->itd/dot_general | solution.py:1011
  298.0 1.8 add_convert_fusion
  302.4 2.0 collective-permute-start.20
  305.6 9.9 %reduce-scatter.8.cloned.1.call-done = bf16[512,256]{1,0:T(8,128)(2,1)} async-done(((bf16[512,1024]{1,0:T(8,128)(2,1)}), bf16[512,256]{1,0:T(8,128)(2,1)}) %reduce-scatter.8.cloned.1.call-update) | async-done | bytes 262160 | tf_op jit(solution)/shard_map/reduce_scatter | solution.py:75
  318.1 4.7 %all-to-all-start.2 = ((bf16[4,1152,256]{2,1,0:T(8,128)(2,1)}), bf16[4,1152,256]{2,1,0:T(8,128)(2,1)}, u32[]{:S(2)}, u32[]{:S(2)}) async-start(bf16[4,1152,256]{2,1,0:T(8,128)(2,1)} %broadcast_in_dim.42), calls=%async_computation.5 | async-start | bytes 4718592 | tf_op jit(solution)/shard_map/all_to_all | solution.py:71
  322.9 8.3 %fusion.12.in_ref.a_ref = bf16[2,592,1024]{2,1,0:T(8,128)(2,1)S(1)} fusion(bf16[2,592,2048]{2,1,0:T(8,128)(2,1)} %get-tuple-element.218.a_ref, bf16[2048,1024]{1,0:T(8,128)(2,1)} %get-tuple-element.219), kind=kOutput, calls=%fused_computation.9 | convolution fusion | flops 4967268352 | bytes 11468800 | tf_op jit(solution)/shard_map/ith,hd->itd/dot_general | solution.py:1016
  331.3 2.1 fusion.22.refs_0_
  333.4 1.7 half.1
  335.3 2.1 collective-permute-start.24
  339.0 3.7 close.1
  342.7 3.2 copy.66
  345.9 8.3 %norm_back.3 = (f32[2,577,512]{2,1,0:T(8,128)}, f32[2,2,1024]{2,1,0:T(2,128)}) custom-call(s32[3]{0:T(128)S(1)} %pad_add_fusion.at_ref, bf16[2,592,1024]{2,1,0:T(8,128)(2,1)} %get-tuple-element.191.base_ref, bf16[2,592,1024]{2,1,0:T(8,128)(2,1)} %get-tuple-element.138.x_ref.v_ref, bf16[2,592,1024]{2,1,0:T(8,128)(2,1)} %fusion.6.a_ref, ...), custom_call_target="tpu_custom_call" | custom-call | flops 10000000 | bytes 1024 | tf_op jit(solution)/shard_map/norm_back/pallas_call | solution.py:222
  354.2 4.9 %copy.67 = f32[2,577,512]{2,0,1:T(2,128)} copy(f32[2,577,512]{2,1,0:T(8,128)} %get-tuple-element.277) | data formatting | bytes 4726784
  359.3 2.0 collective-permute-start.27
  367.6 3.6 collective-permute-start.31
  372.8 1.8 copy.68
  374.6 1.9 spread.1
  (222 shorter events, 50.4 us)
Async XLA Ops:
  7.2 76.0 %all-gather.5.cloned.1.call-start = ((), (), s32[]{:S(2)}) async-start(), calls=%async_computation.9 | async-start | bytes 2621440 | tf_op jit(solution)/shard_map/all_gather | solution.py:901
  12.6 10.2 %collective-permute-start.3 = (bf16[2,592,512]{2,1,0:T(8,128)(2,1)S(1)}, bf16[2,592,512]{2,1,0:T(8,128)(2,1)S(1)}, u32[]{:S(2)}, u32[]{:S(2)}) collective-permute-start(bf16[2,592,512]{2,1,0:T(8,128)(2,1)S(1)} %pad_maximum_fusion.1.own_ref), channel_id=1, source_target_pairs={{0,1},{1,0},{2,3},{3,2},{4,5},{5,4},{6,7},{7,6},{8,9},{9,8},{10,11... | collective-permute-start | bytes 3637256 | tf_op jit(solution)/shard_map/ppermute | solution.py:21
  13.2 13.3 %collective-permute-start = (bf16[784,128]{1,0:T(8,128)(2,1)}, bf16[784,128]{1,0:T(8,128)(2,1)}, u32[]{:S(2)}, u32[]{:S(2)}) collective-permute-start(bf16[784,128]{1,0:T(8,128)(2,1)} %pad_maximum_fusion.5), channel_id=1, source_target_pairs={{0,2},{2,0},{4,6},{6,4},{1,3},{3,1},{5,7},{7,5},{8,10},{10,8},{12,... | collective-permute-start | bytes 602120 | tf_op jit(solution)/shard_map/ppermute | solution.py:21
  15.8 17.7 %collective-permute-start.1 = (bf16[784,128]{1,0:T(8,128)(2,1)}, bf16[784,128]{1,0:T(8,128)(2,1)}, u32[]{:S(2)}, u32[]{:S(2)}) collective-permute-start(bf16[784,128]{1,0:T(8,128)(2,1)} %pad_maximum_fusion.5), channel_id=1, source_target_pairs={{0,4},{2,6},{4,0},{6,2},{1,5},{3,7},{5,1},{7,3},{8,12},{10,14},{12... | collective-permute-start | bytes 602120 | tf_op jit(solution)/shard_map/ppermute | solution.py:21
  18.4 15.1 %collective-permute-start.2 = (bf16[784,128]{1,0:T(8,128)(2,1)}, bf16[784,128]{1,0:T(8,128)(2,1)}, u32[]{:S(2)}, u32[]{:S(2)}) collective-permute-start(bf16[784,128]{1,0:T(8,128)(2,1)} %pad_maximum_fusion.5), channel_id=1, source_target_pairs={{0,6},{2,4},{4,2},{6,0},{1,7},{3,5},{5,3},{7,1},{8,14},{10,12},{12... | collective-permute-start | bytes 602120 | tf_op jit(solution)/shard_map/ppermute | solution.py:21
  22.8 10.7 %copy-start.27 = (bf16[512,256]{1,0:T(8,128)(2,1)S(1)}, bf16[512,256]{1,0:T(8,128)(2,1)}, u32[]{:S(2)}) copy-start(bf16[512,256]{1,0:T(8,128)(2,1)} %param.18) | copy-start | bytes 786436
  22.9 16.6 %copy-start.32 = (bf16[2,512]{1,0:T(2,128)(2,1)S(1)}, bf16[2,512]{1,0:T(2,128)(2,1)}, u32[]{:S(2)}) copy-start(bf16[2,512]{1,0:T(2,128)(2,1)} %param.17) | copy-start | bytes 6148
  26.5 13.2 %copy-start.2 = (bf16[2,592,1024]{2,1,0:T(8,128)(2,1)S(1)}, bf16[2,592,1024]{2,1,0:T(8,128)(2,1)}, u32[]{:S(2)}) copy-start(bf16[2,592,1024]{2,1,0:T(8,128)(2,1)} %get-tuple-element.139.n_ref) | copy-start | bytes 7274500
  34.4 84.1 %all-gather.7.cloned.1.call-start = ((), (), s32[]{:S(2)}) async-start(), calls=%async_computation.10 | async-start | bytes 1310720 | tf_op jit(solution)/shard_map/all_gather | solution.py:905
  34.6 17.7 %copy-start.8 = (bf16[256,3,512]{2,0,1:T(8,128)(2,1)S(1)}, bf16[256,3,512]{2,0,1:T(8,128)(2,1)}, u32[]{:S(2)}) copy-start(bf16[256,3,512]{2,0,1:T(8,128)(2,1)} %param.16) | copy-start | bytes 2359300
  35.9 22.7 %copy-start.10 = (bf16[2320,128]{1,0:T(8,128)(2,1)}, bf16[2320,128]{1,0:T(8,128)(2,1)S(1)}, u32[]{:S(2)}) copy-start(bf16[2320,128]{1,0:T(8,128)(2,1)S(1)} %stack.63.rest_ref) | copy-start | bytes 1781764
  35.9 16.4 %collective-permute-start.6 = (bf16[2320,128]{1,0:T(8,128)(2,1)S(1)}, bf16[2320,128]{1,0:T(8,128)(2,1)S(1)}, u32[]{:S(2)}, u32[]{:S(2)}) collective-permute-start(bf16[2320,128]{1,0:T(8,128)(2,1)S(1)} %stack.63.rest_ref), channel_id=1, source_target_pairs={{0,8},{8,0},{16,24},{24,16},{1,9},{9,1},{17,25},{25,17},{2,10},{10... | collective-permute-start | bytes 1781768 | tf_op jit(solution)/shard_map/ppermute | solution.py:21
  37.4 26.5 %collective-permute-start.5 = (bf16[2320,128]{1,0:T(8,128)(2,1)S(1)}, bf16[2320,128]{1,0:T(8,128)(2,1)S(1)}, u32[]{:S(2)}, u32[]{:S(2)}) collective-permute-start(bf16[2320,128]{1,0:T(8,128)(2,1)S(1)} %stack.63.rest_ref), channel_id=1, source_target_pairs={{0,16},{8,24},{16,0},{24,8},{1,17},{9,25},{17,1},{25,9},{2,18},{10... | collective-permute-start | bytes 1781768 | tf_op jit(solution)/shard_map/ppermute | solution.py:21
  39.0 31.2 %collective-permute-start.4 = (bf16[2320,128]{1,0:T(8,128)(2,1)S(1)}, bf16[2320,128]{1,0:T(8,128)(2,1)S(1)}, u32[]{:S(2)}, u32[]{:S(2)}) collective-permute-start(bf16[2320,128]{1,0:T(8,128)(2,1)S(1)} %stack.63.rest_ref), channel_id=1, source_target_pairs={{0,24},{8,16},{16,8},{24,0},{1,25},{9,17},{17,9},{25,1},{2,26},{10... | collective-permute-start | bytes 1781768 | tf_op jit(solution)/shard_map/ppermute | solution.py:21
  52.3 6.3 %copy-start.12 = (bf16[2320,128]{1,0:T(8,128)(2,1)}, bf16[2320,128]{1,0:T(8,128)(2,1)S(1)}, u32[]{:S(2)}) copy-start(bf16[2320,128]{1,0:T(8,128)(2,1)S(1)} %collective-permute-done.6.rest_ref) | copy-start | bytes 1781764
  63.9 6.2 %copy-start.13 = (bf16[2320,128]{1,0:T(8,128)(2,1)}, bf16[2320,128]{1,0:T(8,128)(2,1)S(1)}, u32[]{:S(2)}) copy-start(bf16[2320,128]{1,0:T(8,128)(2,1)S(1)} %collective-permute-done.5.rest_ref) | copy-start | bytes 1781764
  77.3 9.6 %copy-start.4 = (bf16[2,592,512]{2,1,0:T(8,128)(2,1)S(1)}, bf16[2,592,512]{2,1,0:T(8,128)(2,1)}, u32[]{:S(2)}) copy-start(bf16[2,592,512]{2,1,0:T(8,128)(2,1)} %get-tuple-element.153.a_ref) | copy-start | bytes 3637252
  86.9 6.9 %copy-start.36 = (bf16[2048]{0:T(1024)(128)(2,1)S(1)}, bf16[2048]{0:T(1024)(128)(2,1)}, u32[]{:S(2)}) copy-start(bf16[2048]{0:T(1024)(128)(2,1)} %param.21) | copy-start | bytes 12292
  91.5 5.0 %collective-permute-start.7 = (bf16[2,592,1024]{2,1,0:T(8,128)(2,1)}, bf16[2,592,1024]{2,1,0:T(8,128)(2,1)}, u32[]{:S(2)}, u32[]{:S(2)}) collective-permute-start(bf16[2,592,1024]{2,1,0:T(8,128)(2,1)} %get-tuple-element.154.a_ref), channel_id=1, source_target_pairs={{0,1},{1,0},{2,3},{3,2},{4,5},{5,4},{6,7},{7,6},{8,9},{9,8},{10,11... | collective-permute-start | bytes 7274504 | tf_op jit(solution)/shard_map/ppermute | solution.py:21
  91.5 162.0 %reduce-scatter.4.cloned.1.call-start = ((), (), s32[]{:S(2)}) async-start(), calls=%async_computation.6 | async-start | bytes 5242880 | tf_op jit(solution)/shard_map/reduce_scatter | solution.py:75
  91.8 31.6 %collective-permute-start.8 = (bf16[2,592,512]{2,1,0:T(8,128)(2,1)}, bf16[2,592,512]{2,1,0:T(8,128)(2,1)}, u32[]{:S(2)}, u32[]{:S(2)}) collective-permute-start(bf16[2,592,512]{2,1,0:T(8,128)(2,1)} %pad.9.own_ref), channel_id=1, source_target_pairs={{0,1},{1,0},{2,3},{3,2},{4,5},{5,4},{6,7},{7,6},{8,9},{9,8},{10,11... | collective-permute-start | bytes 3637256 | tf_op jit(solution)/shard_map/ppermute | solution.py:21
  92.3 37.6 %collective-permute-start.10 = (bf16[3,256,512]{2,1,0:T(8,128)(2,1)}, bf16[3,256,512]{2,1,0:T(8,128)(2,1)}, u32[]{:S(2)}, u32[]{:S(2)}) collective-permute-start(bf16[3,256,512]{2,1,0:T(8,128)(2,1)} %unpack.1.rest_ref), channel_id=1, source_target_pairs={{0,16},{8,24},{16,0},{24,8},{1,17},{9,25},{17,1},{25,9},{2,18},{10... | collective-permute-start | bytes 2359304 | tf_op jit(solution)/shard_map/ppermute | solution.py:21
  93.8 43.8 %collective-permute-start.11 = (bf16[3,256,512]{2,1,0:T(8,128)(2,1)}, bf16[3,256,512]{2,1,0:T(8,128)(2,1)}, u32[]{:S(2)}, u32[]{:S(2)}) collective-permute-start(bf16[3,256,512]{2,1,0:T(8,128)(2,1)} %unpack.1.rest_ref), channel_id=1, source_target_pairs={{0,24},{8,16},{16,8},{24,0},{1,25},{9,17},{17,9},{25,1},{2,26},{10... | collective-permute-start | bytes 2359304 | tf_op jit(solution)/shard_map/ppermute | solution.py:21
  95.3 42.4 %collective-permute-start.9 = (bf16[3,256,512]{2,1,0:T(8,128)(2,1)}, bf16[3,256,512]{2,1,0:T(8,128)(2,1)}, u32[]{:S(2)}, u32[]{:S(2)}) collective-permute-start(bf16[3,256,512]{2,1,0:T(8,128)(2,1)} %unpack.1.rest_ref), channel_id=1, source_target_pairs={{0,8},{8,0},{16,24},{24,16},{1,9},{9,1},{17,25},{25,17},{2,10},{10... | collective-permute-start | bytes 2359304 | tf_op jit(solution)/shard_map/ppermute | solution.py:21
  103.8 28.5 %copy-start.43 = (s32[2]{0:T(128)S(1)}, s32[2]{0:T(128)}, u32[]{:S(2)}) copy-start(s32[2]{0:T(128)} %param.15) | copy-start | bytes 28
  109.3 28.4 %copy-start.1 = (bf16[2,592,1024]{2,1,0:T(8,128)(2,1)S(1)}, bf16[2,592,1024]{2,1,0:T(8,128)(2,1)}, u32[]{:S(2)}) copy-start(bf16[2,592,1024]{2,1,0:T(8,128)(2,1)} %get-tuple-element.159.n_ref.b_ref) | copy-start | bytes 7274500
  121.9 42.8 %collective-permute-start.12 = (bf16[3,512,256]{2,1,0:T(8,128)(2,1)}, bf16[3,512,256]{2,1,0:T(8,128)(2,1)}, u32[]{:S(2)}, u32[]{:S(2)}) collective-permute-start(bf16[3,512,256]{2,1,0:T(8,128)(2,1)} %others.1.refs_0_), channel_id=1, source_target_pairs={{0,8},{8,0},{16,24},{24,16},{1,9},{9,1},{17,25},{25,17},{2,10},{10... | collective-permute-start | bytes 2359304 | tf_op jit(solution)/shard_map/ppermute | solution.py:21
  123.3 41.3 %collective-permute-start.13 = (bf16[3,512,256]{2,1,0:T(8,128)(2,1)}, bf16[3,512,256]{2,1,0:T(8,128)(2,1)}, u32[]{:S(2)}, u32[]{:S(2)}) collective-permute-start(bf16[3,512,256]{2,1,0:T(8,128)(2,1)} %others.1.refs_0_), channel_id=1, source_target_pairs={{0,16},{8,24},{16,0},{24,8},{1,17},{9,25},{17,1},{25,9},{2,18},{10... | collective-permute-start | bytes 2359304 | tf_op jit(solution)/shard_map/ppermute | solution.py:21
  129.9 35.0 %collective-permute-start.14 = (bf16[3,512,256]{2,1,0:T(8,128)(2,1)}, bf16[3,512,256]{2,1,0:T(8,128)(2,1)}, u32[]{:S(2)}, u32[]{:S(2)}) collective-permute-start(bf16[3,512,256]{2,1,0:T(8,128)(2,1)} %others.1.refs_0_), channel_id=1, source_target_pairs={{0,24},{8,16},{16,8},{24,0},{1,25},{9,17},{17,9},{25,1},{2,26},{10... | collective-permute-start | bytes 2359304 | tf_op jit(solution)/shard_map/ppermute | solution.py:21
  154.2 10.7 %copy-start.11 = (bf16[2048,256]{1,0:T(8,128)(2,1)S(1)}, bf16[2048,256]{1,0:T(8,128)(2,1)}, u32[]{:S(2)}) copy-start(bf16[2048,256]{1,0:T(8,128)(2,1)} %own_ref.9) | copy-start | bytes 3145732
  177.2 11.1 %copy-start.19 = (bf16[1024,2048]{1,0:T(8,128)(2,1)S(1)}, bf16[1024,2048]{1,0:T(8,128)(2,1)}, u32[]{:S(2)}) copy-start(bf16[1024,2048]{1,0:T(8,128)(2,1)} %get-tuple-element.190) | copy-start | bytes 12582916
  177.2 11.1 %copy-start.20 = (bf16[2,592,2048]{2,1,0:T(8,128)(2,1)S(1)}, bf16[2,592,2048]{2,1,0:T(8,128)(2,1)}, u32[]{:S(2)}) copy-start(bf16[2,592,2048]{2,1,0:T(8,128)(2,1)} %get-tuple-element.189.a_ref) | copy-start | bytes 14548996
  194.2 6.3 %collective-permute-start.15 = (bf16[2,592,1024]{2,1,0:T(8,128)(2,1)S(1)}, bf16[2,592,1024]{2,1,0:T(8,128)(2,1)}, u32[]{:S(2)}, u32[]{:S(2)}) collective-permute-start(bf16[2,592,1024]{2,1,0:T(8,128)(2,1)S(1)} %fusion.9.a_ref), channel_id=1, source_target_pairs={{0,1},{1,0},{2,3},{3,2},{4,5},{5,4},{6,7},{7,6},{8,9},{9,8},{10,11... | collective-permute-start | bytes 7274504 | tf_op jit(solution)/shard_map/ppermute | solution.py:21
  195.6 53.7 %all-to-all-start = ((bf16[4,512,1024]{2,1,0:T(8,128)(2,1)}), bf16[4,512,1024]{2,1,0:T(8,128)(2,1)}, u32[]{:S(2)}, u32[]{:S(2)}) async-start(bf16[4,512,1024]{2,1,0:T(8,128)(2,1)} %bitcast.114), calls=%async_computation | async-start | bytes 8388608 | tf_op jit(solution)/shard_map/all_to_all | solution.py:66
  200.4 82.0 %reduce-scatter.6.cloned.1.call-start = ((), (), s32[]{:S(2)}) async-start(), calls=%async_computation.7 | async-start | bytes 1310720 | tf_op jit(solution)/shard_map/reduce_scatter | solution.py:75
  200.5 8.8 %copy-start.42 = (bf16[512,1024]{1,0:T(8,128)(2,1)S(1)}, bf16[512,1024]{1,0:T(8,128)(2,1)}, u32[]{:S(2)}) copy-start(bf16[512,1024]{1,0:T(8,128)(2,1)} %get-tuple-element.192) | copy-start | bytes 3145732
  216.2 7.9 %copy-start.3 = (bf16[2,592,1024]{2,1,0:T(8,128)(2,1)S(1)}, bf16[2,592,1024]{2,1,0:T(8,128)(2,1)}, u32[]{:S(2)}) copy-start(bf16[2,592,1024]{2,1,0:T(8,128)(2,1)} %get-tuple-element.139.n_ref) | copy-start | bytes 7274500
  216.2 99.2 %reduce-scatter.8.cloned.1.call-start = ((), (), s32[]{:S(2)}) async-start(), calls=%async_computation.8 | async-start | bytes 1310720 | tf_op jit(solution)/shard_map/reduce_scatter | solution.py:75
  239.0 14.5 %copy-start.16 = (f32[2,8,592]{2,1,0:T(8,128)S(1)}, f32[2,8,592]{2,1,0:T(8,128)}, u32[]{:S(2)}) copy-start(f32[2,8,592]{2,1,0:T(8,128)} %get-tuple-element.209.stats_ref) | copy-start | bytes 113668
  239.0 26.7 %collective-permute-start.16 = (bf16[1024,384]{1,0:T(8,128)(2,1)}, bf16[1024,384]{1,0:T(8,128)(2,1)S(1)}, u32[]{:S(2)}, u32[]{:S(2)}) collective-permute-start(bf16[1024,384]{1,0:T(8,128)(2,1)} %bitcast_convert_fusion.4), channel_id=1, source_target_pairs={{0,8},{8,0},{16,24},{24,16},{1,9},{9,1},{17,25},{25,17},{2,10},{10... | collective-permute-start | bytes 2359304 | tf_op jit(solution)/shard_map/ppermute | solution.py:21
  240.9 36.4 %collective-permute-start.17 = (bf16[1024,384]{1,0:T(8,128)(2,1)}, bf16[1024,384]{1,0:T(8,128)(2,1)}, u32[]{:S(2)}, u32[]{:S(2)}) collective-permute-start(bf16[1024,384]{1,0:T(8,128)(2,1)} %bitcast_convert_fusion.3), channel_id=1, source_target_pairs={{0,16},{8,24},{16,0},{24,8},{1,17},{9,25},{17,1},{25,9},{2,18},{10... | collective-permute-start | bytes 2359304 | tf_op jit(solution)/shard_map/ppermute | solution.py:21
  264.7 19.0 %collective-permute-start.18 = (bf16[1024,384]{1,0:T(8,128)(2,1)}, bf16[1024,384]{1,0:T(8,128)(2,1)}, u32[]{:S(2)}, u32[]{:S(2)}) collective-permute-start(bf16[1024,384]{1,0:T(8,128)(2,1)} %bitcast_convert_fusion.2), channel_id=1, source_target_pairs={{0,24},{8,16},{16,8},{24,0},{1,25},{9,17},{17,9},{25,1},{2,26},{10... | collective-permute-start | bytes 2359304 | tf_op jit(solution)/shard_map/ppermute | solution.py:21
  265.6 7.9 %copy-start.24 = (bf16[1024,384]{1,0:T(8,128)(2,1)}, bf16[1024,384]{1,0:T(8,128)(2,1)S(1)}, u32[]{:S(2)}) copy-start(bf16[1024,384]{1,0:T(8,128)(2,1)S(1)} %collective-permute-done.16) | copy-start | bytes 2359300
  273.5 10.2 %copy-start.23 = (bf16[2048,256]{1,0:T(8,128)(2,1)S(1)}, bf16[2048,256]{1,0:T(8,128)(2,1)}, u32[]{:S(2)}) copy-start(bf16[2048,256]{1,0:T(8,128)(2,1)} %reduce-scatter.4.cloned.1.call-done) | copy-start | bytes 3145732
  285.8 19.4 %all-to-all-start.1 = ((bf16[4,640,256]{2,1,0:T(8,128)(2,1)}), bf16[4,640,256]{2,1,0:T(8,128)(2,1)S(1)}, u32[]{:S(2)}, u32[]{:S(2)}) async-start(bf16[4,640,256]{2,1,0:T(8,128)(2,1)} %pad_maximum_fusion), calls=%async_computation.3 | async-start | bytes 2621440 | tf_op jit(solution)/shard_map/all_to_all | solution.py:66
  289.4 8.5 %copy-start.25 = (bf16[1024,384]{1,0:T(8,128)(2,1)S(1)}, bf16[1024,384]{1,0:T(8,128)(2,1)}, u32[]{:S(2)}) copy-start(bf16[1024,384]{1,0:T(8,128)(2,1)} %copy-done.24) | copy-start | bytes 2359300
  289.4 8.5 %copy-start.26 = (bf16[1024,384]{1,0:T(8,128)(2,1)S(1)}, bf16[1024,384]{1,0:T(8,128)(2,1)}, u32[]{:S(2)}) copy-start(bf16[1024,384]{1,0:T(8,128)(2,1)} %bitcast_convert_fusion.1) | copy-start | bytes 2359300
  297.9 47.9 %collective-permute-start.23 = (bf16[2,592,1024]{2,1,0:T(8,128)(2,1)}, bf16[2,592,1024]{2,1,0:T(8,128)(2,1)}, u32[]{:S(2)}, u32[]{:S(2)}) collective-permute-start(bf16[2,592,1024]{2,1,0:T(8,128)(2,1)} %fusion.6.a_ref), channel_id=1, source_target_pairs={{0,1},{1,0},{2,3},{3,2},{4,5},{5,4},{6,7},{7,6},{8,9},{9,8},{10,11... | collective-permute-start | bytes 7274504 | tf_op jit(solution)/shard_map/ppermute | solution.py:21
  300.8 30.5 %collective-permute-start.19 = (bf16[256,384]{1,0:T(8,128)(2,1)}, bf16[256,384]{1,0:T(8,128)(2,1)}, u32[]{:S(2)}, u32[]{:S(2)}) collective-permute-start(bf16[256,384]{1,0:T(8,128)(2,1)} %get-tuple-element.294), channel_id=1, source_target_pairs={{0,2},{2,0},{4,6},{6,4},{1,3},{3,1},{5,7},{7,5},{8,10},{10,8},{12,... | collective-permute-start | bytes 589832 | tf_op jit(solution)/shard_map/ppermute | solution.py:21
  302.4 28.9 %collective-permute-start.20 = (bf16[256,384]{1,0:T(8,128)(2,1)}, bf16[256,384]{1,0:T(8,128)(2,1)}, u32[]{:S(2)}, u32[]{:S(2)}) collective-permute-start(bf16[256,384]{1,0:T(8,128)(2,1)} %get-tuple-element.296), channel_id=1, source_target_pairs={{0,4},{2,6},{4,0},{6,2},{1,5},{3,7},{5,1},{7,3},{8,12},{10,14},{12... | collective-permute-start | bytes 589832 | tf_op jit(solution)/shard_map/ppermute | solution.py:21
  304.4 26.9 %collective-permute-start.21 = (bf16[256,384]{1,0:T(8,128)(2,1)}, bf16[256,384]{1,0:T(8,128)(2,1)}, u32[]{:S(2)}, u32[]{:S(2)}) collective-permute-start(bf16[256,384]{1,0:T(8,128)(2,1)} %get-tuple-element.295), channel_id=1, source_target_pairs={{0,6},{2,4},{4,2},{6,0},{1,7},{3,5},{5,3},{7,1},{8,14},{10,12},{12... | collective-permute-start | bytes 589832 | tf_op jit(solution)/shard_map/ppermute | solution.py:21
  318.1 41.0 %all-to-all-start.2 = ((bf16[4,1152,256]{2,1,0:T(8,128)(2,1)}), bf16[4,1152,256]{2,1,0:T(8,128)(2,1)}, u32[]{:S(2)}, u32[]{:S(2)}) async-start(bf16[4,1152,256]{2,1,0:T(8,128)(2,1)} %broadcast_in_dim.42), calls=%async_computation.5 | async-start | bytes 4718592 | tf_op jit(solution)/shard_map/all_to_all | solution.py:71
  331.2 7.8 %copy-start.9 = (bf16[2,592,1024]{2,1,0:T(8,128)(2,1)}, bf16[2,592,1024]{2,1,0:T(8,128)(2,1)S(1)}, u32[]{:S(2)}) copy-start(bf16[2,592,1024]{2,1,0:T(8,128)(2,1)S(1)} %fusion.12.in_ref.a_ref) | copy-start | bytes 7274500
  335.1 3.9 collective-permute-start.22
  335.2 7.5 %copy-start.28 = (f32[3,1024]{1,0:T(4,128)}, f32[3,1024]{1,0:T(4,128)S(1)}, u32[]{:S(2)}) copy-start(f32[3,1024]{1,0:T(4,128)S(1)} %reduce_sum.57) | copy-start | bytes 36868
  335.3 23.8 %collective-permute-start.24 = (bf16[256,384]{1,0:T(8,128)(2,1)S(1)}, bf16[256,384]{1,0:T(8,128)(2,1)S(1)}, u32[]{:S(2)}, u32[]{:S(2)}) collective-permute-start(bf16[256,384]{1,0:T(8,128)(2,1)S(1)} %fusion.22.refs_0_), channel_id=1, source_target_pairs={{0,8},{8,0},{16,24},{24,16},{1,9},{9,1},{17,25},{25,17},{2,10},{10... | collective-permute-start | bytes 589832 | tf_op jit(solution)/shard_map/ppermute | solution.py:21
  337.4 21.7 %collective-permute-start.25 = (bf16[256,384]{1,0:T(8,128)(2,1)S(1)}, bf16[256,384]{1,0:T(8,128)(2,1)S(1)}, u32[]{:S(2)}, u32[]{:S(2)}) collective-permute-start(bf16[256,384]{1,0:T(8,128)(2,1)S(1)} %fusion.22.refs_0_), channel_id=1, source_target_pairs={{0,16},{8,24},{16,0},{24,8},{1,17},{9,25},{17,1},{25,9},{2,18},{10... | collective-permute-start | bytes 589832 | tf_op jit(solution)/shard_map/ppermute | solution.py:21
  338.9 20.2 %collective-permute-start.26 = (bf16[256,384]{1,0:T(8,128)(2,1)S(1)}, bf16[256,384]{1,0:T(8,128)(2,1)S(1)}, u32[]{:S(2)}, u32[]{:S(2)}) collective-permute-start(bf16[256,384]{1,0:T(8,128)(2,1)S(1)} %fusion.22.refs_0_), channel_id=1, source_target_pairs={{0,24},{8,16},{16,8},{24,0},{1,25},{9,17},{17,9},{25,1},{2,26},{10... | collective-permute-start | bytes 589832 | tf_op jit(solution)/shard_map/ppermute | solution.py:21
  359.3 8.0 %collective-permute-start.27 = (f32[6144]{0:T(1024)S(1)}, f32[6144]{0:T(1024)S(1)}, u32[]{:S(2)}, u32[]{:S(2)}) collective-permute-start(f32[6144]{0:T(1024)S(1)} %pad_maximum_fusion.6), channel_id=1, source_target_pairs={{0,8},{8,0},{16,24},{24,16},{1,9},{9,1},{17,25},{25,17},{2,10},{10... | collective-permute-start | bytes 73736 | tf_op jit(solution)/shard_map/ppermute | solution.py:21
  361.3 6.0 %collective-permute-start.28 = (f32[6144]{0:T(1024)S(1)}, f32[6144]{0:T(1024)S(1)}, u32[]{:S(2)}, u32[]{:S(2)}) collective-permute-start(f32[6144]{0:T(1024)S(1)} %pad_maximum_fusion.6), channel_id=1, source_target_pairs={{0,16},{8,24},{16,0},{24,8},{1,17},{9,25},{17,1},{25,9},{2,18},{10... | collective-permute-start | bytes 73736 | tf_op jit(solution)/shard_map/ppermute | solution.py:21
  362.8 4.7 %collective-permute-start.29 = (f32[6144]{0:T(1024)S(1)}, f32[6144]{0:T(1024)S(1)}, u32[]{:S(2)}, u32[]{:S(2)}) collective-permute-start(f32[6144]{0:T(1024)S(1)} %pad_maximum_fusion.6), channel_id=1, source_target_pairs={{0,24},{8,16},{16,8},{24,0},{1,25},{9,17},{17,9},{25,1},{2,26},{10... | collective-permute-start | bytes 73736 | tf_op jit(solution)/shard_map/ppermute | solution.py:21
  367.5 9.0 %collective-permute-start.30 = (f32[6144]{0:T(1024)S(1)}, f32[6144]{0:T(1024)S(1)}, u32[]{:S(2)}, u32[]{:S(2)}) collective-permute-start(f32[6144]{0:T(1024)S(1)} %add_add_fusion.1), channel_id=1, source_target_pairs={{0,2},{2,0},{4,6},{6,4},{1,3},{3,1},{5,7},{7,5},{8,10},{10,8},{12,... | collective-permute-start | bytes 73736 | tf_op jit(solution)/shard_map/ppermute | solution.py:21
  367.6 8.9 %collective-permute-start.31 = (f32[6144]{0:T(1024)S(1)}, f32[6144]{0:T(1024)S(1)}, u32[]{:S(2)}, u32[]{:S(2)}) collective-permute-start(f32[6144]{0:T(1024)S(1)} %add_add_fusion.1), channel_id=1, source_target_pairs={{0,4},{2,6},{4,0},{6,2},{1,5},{3,7},{5,1},{7,3},{8,12},{10,14},{12... | collective-permute-start | bytes 73736 | tf_op jit(solution)/shard_map/ppermute | solution.py:21
  371.2 5.6 %collective-permute-start.32 = (f32[6144]{0:T(1024)S(1)}, f32[6144]{0:T(1024)S(1)}, u32[]{:S(2)}, u32[]{:S(2)}) collective-permute-start(f32[6144]{0:T(1024)S(1)} %add_add_fusion.1), channel_id=1, source_target_pairs={{0,6},{2,4},{4,2},{6,0},{1,7},{3,5},{5,3},{7,1},{8,14},{10,12},{12... | collective-permute-start | bytes 73736 | tf_op jit(solution)/shard_map/ppermute | solution.py:21
  (22 other events, 82.5 us)
Sparse Core Ops, SparseCore 0:
  34.5 48.6 all-gather.4
  91.6 26.7 all-gather.6
  177.4 74.5 reduce-scatter.3
  254.8 27.6 reduce-scatter.5
  285.2 30.2 reduce-scatter.7
